TPU v7x, 32 devices: a whole 2x2x4 slice. The times are simulated.
32 devices in a mesh: leaf: 8 (over z, y), sub: 4 (over x, core).
Axes of the slice: x: 2, y: 2, z: 4, core: 2. Of those that a mesh axis runs over, the one named last changes fastest.
Arguments:
- points: bfloat16 [512, 64, 256], P(('leaf', 'sub')), may hold values from -6 to 6
- probe_bits: int32 [512, 16, 256], P(('leaf', 'sub')), may hold values from 0 to 1
- leaf_skel: int32 [512, 128], P(('leaf', 'sub')), may hold values from 0 to 255, as said below
- leaf_basis: bfloat16 [512, 128, 256], P(('leaf', 'sub')), may hold values from -0.4375 to 0.4375
- device_skel: int32 [32, 128], P(('leaf', 'sub')), may hold values from 0 to 2047, as said below
- device_basis: bfloat16 [32, 128, 2048], P(('leaf', 'sub')), may hold values from -0.25 to 0.25
- subtree_skel: int32 [8, 128], P('leaf'), may hold values from 0 to 511, as said below
- subtree_basis: bfloat16 [8, 128, 512], P('leaf'), may hold values from -0.375 to 0.375
- upper_skel: int32 [8, 2, 128], P('leaf'), may hold values from 0 to 255, as said below
- upper_basis: bfloat16 [8, 2, 128, 256], P('leaf'), as said below
- near_pairs: int32 [32, 80, 2], P(('leaf', 'sub')), may hold values from 0 to 63, as said below
- near_count: int32 [32], P(('leaf', 'sub')), may hold values from 1 to 80, 1024 in all
- far_pairs: int32 [32, 96, 2], P(('leaf', 'sub')), may hold values from 0 to 63, as said below
Outputs:
- product: float32 [512, 16, 256], P(('leaf', 'sub'))
Inputs may be any that keep to these rules, and one draw needn't show every extreme that they name: `leaf_skel`: each row names 128 different points of its leaf. `device_skel`: each row names 128 different columns. `subtree_skel`: each row names 128 different columns. `upper_skel`: each row names 128 different columns; entries [g, t-1] are equal for all subtrees g under one node of level t. `upper_basis`: entries [g, t-1] are equal for all subtrees g under one node of level t. `near_pairs`: entry 0 of a row is a leaf of the device (0 to 15), entry 1 a leaf of its subtree numbered 0 to 63 in the subtree, never the first leaf itself; the rows of one device are different pairs. `near_count`: some device has exactly 80 pairs. `far_pairs`: as for near_pairs; every row is used.
All inputs are finite; a program needn't handle non-finite values.
Results may differ from a plain program's by a relative error of at most 0.013.
Values may be sent and summed in bfloat16 or wider, within the bound.
No kernel may reach another device: no remote copies, remote signals or barrier semaphores. Data moves between devices by JAX's collectives and lax.ppermute only.
A program may use at most 128 MiB of HBM per device.

v0:
```python
import jax
import jax.numpy as jnp
from jax import lax
from jax.sharding import PartitionSpec as P


def swapped(block, axis, apart):
    count = lax.axis_size(axis)
    route = []
    for low in range(count):
        high = low | 1 << apart
        if high != low and high < count:
            route += [(low, high), (high, low)]
    return lax.ppermute(block, axis, route)


def kernel_tile(first_set, second_set):
    cross_terms = jnp.einsum(
        "...da,...db->...ab", first_set, second_set, preferred_element_type=jnp.float32
    )
    first_wide = first_set.astype(jnp.float32)
    second_wide = second_set.astype(jnp.float32)
    first_norm = jnp.sum(first_wide * first_wide, axis=-2)
    second_norm = jnp.sum(second_wide * second_wide, axis=-2)
    distance = first_norm[..., :, None] + second_norm[..., None, :] - 2.0 * cross_terms
    return jnp.exp(-distance / first_set.shape[-2]).astype(jnp.bfloat16)


def on_device(
    points,
    probe_bits,
    leaf_skel,
    leaf_basis,
    device_skel,
    device_basis,
    subtree_skel,
    subtree_basis,
    upper_skel,
    upper_basis,
    near_pairs,
    near_count,
    far_pairs,
):
    leaves = points.shape[0]
    features = points.shape[1]
    leaf_size = points.shape[2]
    probes = probe_bits.shape[1]
    skeleton = leaf_skel.shape[1]
    groups = lax.axis_size("sub")
    position = lax.axis_index("sub")
    subtree = lax.axis_index("leaf")
    levels = lax.axis_size("leaf").bit_length() - 1
    sign_values = (2 * probe_bits - 1).astype(jnp.bfloat16)
    leaf_coords = jnp.take_along_axis(points, leaf_skel[:, None, :], axis=2)
    leaf_weights = jnp.einsum(
        "lpm,lrm->lpr", sign_values, leaf_basis, preferred_element_type=jnp.float32
    ).astype(jnp.bfloat16)
    joined_weights = jnp.transpose(leaf_weights, (1, 0, 2)).reshape(probes, leaves * skeleton)
    joined_coords = jnp.transpose(leaf_coords, (1, 0, 2)).reshape(features, leaves * skeleton)
    device_weights = jnp.einsum(
        "pc,rc->pr", joined_weights, device_basis[0], preferred_element_type=jnp.float32
    ).astype(jnp.bfloat16)
    device_coords = jnp.take(joined_coords, device_skel[0], axis=1)
    all_points, all_signs, all_coords, all_weights, node_coords, node_weights, all_bases = (
        lax.all_gather(points, "sub", axis=0, tiled=True),
        lax.all_gather(sign_values, "sub", axis=0, tiled=True),
        lax.all_gather(leaf_coords, "sub", axis=0, tiled=True),
        lax.all_gather(leaf_weights, "sub", axis=0, tiled=True),
        lax.all_gather(device_coords[None], "sub", axis=0, tiled=True),
        lax.all_gather(device_weights[None], "sub", axis=0, tiled=True),
        lax.all_gather(leaf_basis, "sub", axis=0, tiled=True),
    )
    self_block = kernel_tile(points, points)
    self_part = jnp.einsum(
        "lpm,lmn->lpn", sign_values, self_block, preferred_element_type=jnp.float32
    )
    group_weights = jnp.transpose(node_weights, (1, 0, 2)).reshape(probes, groups * skeleton)
    group_coords = jnp.transpose(node_coords, (1, 0, 2)).reshape(features, groups * skeleton)
    state_weights = jnp.einsum(
        "pc,rc->pr", group_weights, subtree_basis[0], preferred_element_type=jnp.float32
    ).astype(jnp.bfloat16)
    state_coords = jnp.take(group_coords, subtree_skel[0], axis=1)
    far_own = []
    side_marks = []
    for height in range(1, levels + 1):
        other_coords, other_weights = swapped((state_coords, state_weights), "leaf", height - 1)
        on_right = subtree >> height - 1 & 1 == 1
        left_coords = jnp.where(on_right, other_coords, state_coords)
        right_coords = jnp.where(on_right, state_coords, other_coords)
        left_weights = jnp.where(on_right, other_weights, state_weights)
        right_weights = jnp.where(on_right, state_weights, other_weights)
        kernel_block = kernel_tile(right_coords, left_coords)
        to_left = jnp.dot(right_weights, kernel_block, preferred_element_type=jnp.float32)
        to_right = jnp.einsum(
            "pl,rl->pr", left_weights, kernel_block, preferred_element_type=jnp.float32
        )
        far_own.append(jnp.where(on_right, to_right, to_left))
        side_marks.append(on_right)
        if height < levels:
            both_weights = jnp.concatenate([left_weights, right_weights], axis=1)
            both_coords = jnp.concatenate([left_coords, right_coords], axis=1)
            state_weights = jnp.einsum(
                "pc,rc->pr",
                both_weights,
                upper_basis[0, height - 1],
                preferred_element_type=jnp.float32,
            ).astype(jnp.bfloat16)
            state_coords = jnp.take(both_coords, upper_skel[0, height - 1], axis=1)
    potential = far_own[levels - 1]
    for height in range(levels - 1, 0, -1):
        spread = jnp.dot(
            potential.astype(jnp.bfloat16),
            upper_basis[0, height - 1],
            preferred_element_type=jnp.float32,
        )
        potential = far_own[height - 1] + jnp.where(
            side_marks[height - 1], spread[:, skeleton:], spread[:, :skeleton]
        )
    sub_spread = jnp.dot(
        potential.astype(jnp.bfloat16), subtree_basis[0], preferred_element_type=jnp.float32
    )
    device_potential = lax.dynamic_slice_in_dim(sub_spread, position * skeleton, skeleton, 1)
    dev_spread = jnp.dot(
        device_potential.astype(jnp.bfloat16), device_basis[0], preferred_element_type=jnp.float32
    )
    leaf_potential = jnp.transpose(dev_spread.reshape(probes, leaves, skeleton), (1, 0, 2))
    tree_part = jnp.einsum(
        "lpr,lrm->lpm",
        leaf_potential.astype(jnp.bfloat16),
        leaf_basis,
        preferred_element_type=jnp.float32,
    )
    sub_leaves = all_points.shape[0]
    own_first = position * leaves
    capacity = near_pairs.shape[1]
    first_all = own_first + near_pairs[0, :, 0]
    second_all = near_pairs[0, :, 1]
    first_pair = jnp.int32(0)
    stop_pair = near_count[0]

    def locate(logical):
        return jnp.clip(logical, 0, capacity - 1)

    per_block = min(16, capacity)
    rounds = (jnp.maximum(stop_pair, 0) + per_block - 1) // per_block

    def near_step(counter, partial_value):
        logical = counter * per_block + jnp.arange(per_block, dtype=jnp.int32)
        live_mask = (logical < stop_pair).astype(jnp.float32)[:, None, None]
        slot_ids = locate(logical)
        first_leaf = jnp.take(first_all, slot_ids)
        second_leaf = jnp.take(second_all, slot_ids)
        kernel_block = kernel_tile(
            jnp.take(all_points, second_leaf, axis=0), jnp.take(all_points, first_leaf, axis=0)
        )
        to_first = jnp.einsum(
            "fpm,fmn->fpn",
            jnp.take(all_signs, second_leaf, axis=0),
            kernel_block,
            preferred_element_type=jnp.float32,
        )
        to_second = jnp.einsum(
            "fpn,fmn->fpm",
            jnp.take(all_signs, first_leaf, axis=0),
            kernel_block,
            preferred_element_type=jnp.float32,
        )
        return (
            partial_value.at[first_leaf]
            .add(to_first * live_mask)
            .at[second_leaf]
            .add(to_second * live_mask)
        )

    partial_value = lax.fori_loop(
        0, rounds, near_step, jnp.zeros((sub_leaves, probes, leaf_size), jnp.float32)
    )
    far_first = far_pairs[0, :, 0]
    far_second = far_pairs[0, :, 1]
    far_block = kernel_tile(
        jnp.take(all_coords, far_second, axis=0), jnp.take(leaf_coords, far_first, axis=0)
    )
    to_first_far = jnp.einsum(
        "fpb,fba->fpa",
        jnp.take(all_weights, far_second, axis=0),
        far_block,
        preferred_element_type=jnp.float32,
    ).astype(jnp.bfloat16)
    to_second_far = jnp.einsum(
        "fpa,fba->fpb",
        jnp.take(leaf_weights, far_first, axis=0),
        far_block,
        preferred_element_type=jnp.float32,
    ).astype(jnp.bfloat16)
    first_points = jnp.einsum(
        "fpr,frm->fpm",
        to_first_far,
        jnp.take(leaf_basis, far_first, axis=0),
        preferred_element_type=jnp.float32,
    )
    second_points = jnp.einsum(
        "fpr,frm->fpm",
        to_second_far,
        jnp.take(all_bases, far_second, axis=0),
        preferred_element_type=jnp.float32,
    )
    partial_value = (
        partial_value.at[own_first + far_first].add(first_points).at[far_second].add(second_points)
    )
    mine = lax.psum_scatter(
        partial_value.astype(jnp.bfloat16), "sub", scatter_dimension=0, tiled=True
    ).astype(jnp.float32)
    return mine + self_part + tree_part


def solution(mesh):
    return jax.shard_map(
        on_device,
        mesh=mesh,
        in_specs=(
            P(("leaf", "sub"), None, None),
            P(("leaf", "sub"), None, None),
            P(("leaf", "sub"), None),
            P(("leaf", "sub"), None, None),
            P(("leaf", "sub"), None),
            P(("leaf", "sub"), None, None),
            P("leaf", None),
            P("leaf", None, None),
            P("leaf", None, None),
            P("leaf", None, None, None),
            P(("leaf", "sub"), None, None),
            P(("leaf", "sub")),
            P(("leaf", "sub"), None, None),
        ),
        out_specs=P(("leaf", "sub"), None, None),
        check_vma=False,
    )
```

profile of v0, /device:TPU:6, one launch (start us, length us, event | category | flops | bytes accessed | tf_op | source)
XLA Modules:
  0.0 294.5 jit_solution(16588914274924938745)
XLA Ops:
  6.5 0.7 fusion.80
  8.0 1.5 copy.26
  9.5 11.1 %gather_fusion.14 = bf16[2048,64]{1,0:T(8,128)(2,1)S(1)} fusion(bf16[16,64,256]{1,2,0:T(8,128)(2,1)S(1)} %copy.26, s32[2048]{0:T(1024)S(1)} %fusion.80), kind=kCustom, calls=%fused_computation.16 | custom fusion | bytes 540672 | tf_op jit(solution)/shard_map/jit(take_along_axis)/gather | solution.py:54
  20.9 0.7 fusion.52
  24.0 5.3 %all-gather = bf16[64,128]{1,0:T(8,128)(2,1)S(1)} all-gather(bf16[16,128]{1,0:T(8,128)(2,1)S(1)} %convolution_convert_fusion.7), channel_id=2, replica_groups=mesh['leaf'=8,'sub'=4] {'sub'}, dimensions={0}, use_global_device_ids=true | all-gather | bytes 20480 | tf_op jit(solution)/shard_map/all_gather | solution.py:70
  31.2 5.7 %all_gather.27 = bf16[4,64,128]{2,1,0:T(8,128)(2,1)S(1)} all-gather(bf16[1,64,128]{2,1,0:T(8,128)(2,1)S(1)} %copy.32), channel_id=1, replica_groups=mesh['leaf'=8,'sub'=4] {'sub'}, dimensions={0}, use_global_device_ids=true | all-gather | bytes 81920 | tf_op jit(solution)/shard_map/all_gather | solution.py:69
  37.9 1.6 collective-permute-start.1
  40.2 7.4 %all_gather.21 = bf16[64,16,256]{2,1,0:T(8,128)(2,1)} all-gather(bf16[16,16,256]{2,1,0:T(8,128)(2,1)S(1)} %add_convert_fusion), channel_id=1, replica_groups=mesh['leaf'=8,'sub'=4] {'sub'}, dimensions={0}, use_global_device_ids=true | all-gather | bytes 655360 | tf_op jit(solution)/shard_map/all_gather | solution.py:66
  48.8 0.8 gather_fusion.8
  50.9 0.7 convolution_convert_fusion.5
  51.6 1.6 collective-permute-start.2
  53.2 7.8 %all_gather.23 = bf16[64,16,128]{2,1,0:T(8,128)(2,1)S(1)} all-gather(bf16[16,16,128]{2,1,0:T(8,128)(2,1)S(1)} %convolution_convert_fusion.2), channel_id=1, replica_groups=mesh['leaf'=8,'sub'=4] {'sub'}, dimensions={0}, use_global_device_ids=true | all-gather | bytes 327680 | tf_op jit(solution)/shard_map/all_gather | solution.py:68
  61.7 6.0 %gather_fusion.9 = bf16[96,128,256]{2,1,0:T(8,128)(2,1)} fusion(bf16[16,128,256]{2,1,0:T(8,128)(2,1)S(1)} %copy-done.1, s32[1024]{0:T(1024)S(1)} %get-tuple-element.108), kind=kCustom, calls=%fused_computation.11 | custom fusion | bytes 12583296 | tf_op jit(solution)/shard_map/jit(_take)/gather | solution.py:198
  67.6 1.4 gather_fusion.10
  69.0 2.0 copy.36
  72.4 1.6 convolution_convert_fusion.4
  74.0 2.6 collective-permute-start.4
  76.6 0.9 multiply_reduce_fusion.9
  80.4 2.6 collective-permute-done.3
  83.0 0.8 multiply_reduce_fusion.7
  85.9 3.8 %collective-permute-done.5 = bf16[64,128]{0,1:T(8,128)(2,1)S(1)} collective-permute-done((bf16[64,128]{0,1:T(8,128)(2,1)S(1)}, bf16[64,128]{0,1:T(8,128)(2,1)S(1)}, u32[]{:S(2)}, u32[]{:S(2)}) %collective-permute-start.5) | collective-permute-done | bytes 16416 | tf_op jit(solution)/shard_map/ppermute | solution.py:14
  89.7 0.8 multiply_reduce_fusion.6
  90.5 3.2 %gather_fusion.7 = bf16[96,64,128]{2,1,0:T(8,128)(2,1)} fusion(bf16[64,64,128]{2,1,0:T(8,128)(2,1)} %all-gather.7.cloned.1.call-done, s32[1024]{0:T(1024)S(1)} %get-tuple-element.109), kind=kCustom, calls=%fused_computation.9 | custom fusion | bytes 3146112 | tf_op jit(solution)/shard_map/jit(_take)/gather | solution.py:181
  93.6 2.0 multiply_reduce_fusion.3
  95.6 6.1 %exponential_convert_fusion.1 = bf16[96,128,128]{2,1,0:T(8,128)(2,1)} fusion(f32[96,128]{1,0:T(8,128)S(1)} %multiply_reduce_fusion.2, f32[96,128]{1,0:T(8,128)S(1)} %multiply_reduce_fusion.3, bf16[96,64,128]{2,1,0:T(8,128)(2,1)} %gather_fusion.7, pred[96]{0:T(512)(128)(4,1)} %get-tuple-element.101, bf16[96,64,128]{2,1,0:T(8,128)(2,1)S(1)} %gather_fusion.8, ...), kind=kOutput, calls=%fused_computation.52 | convolution fusion | flops 212336640 | bytes 6389952 | tf_op jit(solution)/shard_map/...da,...db->...ab/dot_general | solution.py:18
  101.8 6.7 %fusion.11 = f32[96,16,256]{2,1,0:T(8,128)} fusion(bf16[96,128,256]{2,1,0:T(8,128)(2,1)} %gather_fusion.9, pred[96]{0:T(512)(128)(4,1)S(1)} %copy-done.43, bf16[96,128,128]{2,1,0:T(8,128)(2,1)} %exponential_convert_fusion.1, bf16[96,16,128]{2,1,0:T(8,128)(2,1)S(1)} %gather_fusion.6, pred[96]{0:T(512)(128)(4,1)S(1)} %copy-done.40), kind=kOutput, calls=%fused_computation.50 | convolution fusion | flops 154533888 | bytes 11403456 | tf_op jit(solution)/shard_map/fpr,frm->fpm/dot_general | solution.py:195
  108.5 1.1 broadcast_in_dim.141
  109.6 23.6 %while.10 = (s32[]{:T(128)}, f32[64,16,256]{2,1,0:T(8,128)}, s32[]{:T(128)}, s32[80]{0:T(128)S(1)}, s32[80]{0:T(128)S(1)}, /*index=5*/bf16[64,16,256]{2,1,0:T(8,...) while((s32[]{:T(128)}, f32[64,16,256]{2,1,0:T(8,128)}, s32[]{:T(128)}, ...), condition=%wide.region_5.9_spmd, body=%wide.region_0.8_spmd.sunk | while | flops 210628064 | bytes 17644208 | solution.py:175
  111.0 2.2 gather_fusion.2
  113.5 2.2 gather_fusion.3
  115.7 0.8 copy-done.4
  116.7 2.7 exponential_convert_fusion.4
  119.4 2.3 gather_fusion.4
  122.8 1.3 convolution_multiply_fusion.7
  124.2 2.6 scatter_fusion
  126.8 2.3 gather_fusion.5
  129.0 1.6 convolution_multiply_fusion.8
  130.6 2.6 scatter_fusion.1
  133.2 13.3 %scatter_fusion.2 = f32[64,16,256]{2,1,0:T(8,128)} fusion(f32[64,16,256]{2,1,0:T(8,128)} %get-tuple-element.52, s32[96]{0:T(128)} %get-tuple-element.105, f32[96,16,256]{2,1,0:T(8,128)} %fusion.11), kind=kCustom, calls=%fused_computation.19 | custom fusion | flops 393216 | bytes 4718976 | tf_op jit(solution)/shard_map/scatter-add | solution.py:208
  146.5 8.3 %gather_fusion.11 = bf16[96,128,256]{2,1,0:T(8,128)(2,1)} fusion(bf16[64,128,256]{2,1,0:T(8,128)(2,1)} %all-gather.9.cloned.1.call-done, s32[1024]{0:T(1024)} %copy-done.35), kind=kCustom, calls=%fused_computation.13 | custom fusion | bytes 12583296 | tf_op jit(solution)/shard_map/jit(_take)/gather | solution.py:204
  154.9 7.6 %fusion.9 = f32[96,16,256]{2,1,0:T(8,128)} fusion(bf16[96,128,256]{2,1,0:T(8,128)(2,1)} %gather_fusion.11, pred[96]{0:T(512)(128)(4,1)S(1)} %copy-done.41, bf16[96,128,128]{2,1,0:T(8,128)(2,1)} %exponential_convert_fusion.1, bf16[96,16,128]{2,1,0:T(8,128)(2,1)S(1)} %copy-done.12, pred[96]{0:T(512)(128)(4,1)S(1)} %copy-done.44), kind=kOutput, calls=%fused_computation.48 | convolution fusion | flops 154533888 | bytes 11403456 | tf_op jit(solution)/shard_map/fpr,frm->fpm/dot_general | solution.py:201
  162.6 8.9 %scatter_fusion.3 = f32[64,16,256]{2,1,0:T(8,128)S(1)} fusion(f32[64,16,256]{2,1,0:T(8,128)S(1)} %copy-done.2, s32[96]{0:T(128)S(1)} %copy-done.37, f32[96,16,256]{2,1,0:T(8,128)} %fusion.9), kind=kCustom, calls=%fused_computation.20 | custom fusion | flops 393216 | bytes 4718976 | tf_op jit(solution)/shard_map/scatter-add | solution.py:208
  171.5 0.9 convert_element_type.118
  172.6 0.8 fusion.84
  173.4 0.9 fusion.40
  175.0 109.4 %reduce-scatter.2.cloned.1.call-done = bf16[16,16,256]{2,1,0:T(8,128)(2,1)} async-done(((bf16[64,16,256]{2,1,0:T(8,128)(2,1)}), bf16[16,16,256]{2,1,0:T(8,128)(2,1)}) %reduce-scatter.2.cloned.1.call-update) | async-done | bytes 131088 | tf_op jit(solution)/shard_map/reduce_scatter | solution.py:210
  284.4 2.4 fusion.18
  286.8 1.1 convolution_add_fusion
  (174 shorter events, 19.1 us)
Async XLA Ops:
  6.5 22.8 %copy-start = (bf16[1,128,512]{2,1,0:T(8,128)(2,1)S(1)}, bf16[1,128,512]{2,1,0:T(8,128)(2,1)}, u32[]{:S(2)}) copy-start(bf16[1,128,512]{2,1,0:T(8,128)(2,1)} %param.30) | copy-start | bytes 393220
  6.5 83.9 %all-gather.7.cloned.1.call-start = ((), (), s32[]{:S(2)}) async-start(), calls=%async_computation.2 | async-start | bytes 1310720 | tf_op jit(solution)/shard_map/all_gather | solution.py:67
  9.5 13.8 %copy-start.13 = (s32[16,16,256]{2,1,0:T(8,128)S(1)}, s32[16,16,256]{2,1,0:T(8,128)}, u32[]{:S(2)}) copy-start(s32[16,16,256]{2,1,0:T(8,128)} %param.24) | copy-start | bytes 786436
  9.5 13.8 %copy-start.1 = (bf16[16,128,256]{2,1,0:T(8,128)(2,1)S(1)}, bf16[16,128,256]{2,1,0:T(8,128)(2,1)}, u32[]{:S(2)}) copy-start(bf16[16,128,256]{2,1,0:T(8,128)(2,1)} %param.26) | copy-start | bytes 3145732
  20.7 9.3 %copy-start.49 = (s32[1,128]{1,0:T(1,128)S(1)}, s32[1,128]{1,0:T(1,128)}, u32[]{:S(2)}) copy-start(s32[1,128]{1,0:T(1,128)} %param.27) | copy-start | bytes 1540
  20.7 9.3 %copy-start.50 = (s32[1,128]{1,0:T(1,128)S(1)}, s32[1,128]{1,0:T(1,128)}, u32[]{:S(2)}) copy-start(s32[1,128]{1,0:T(1,128)} %param.29) | copy-start | bytes 1540
  20.9 18.6 %copy-start.6 = (bf16[16,64,256]{2,1,0:T(8,128)(2,1)S(1)}, bf16[16,64,256]{2,1,0:T(8,128)(2,1)}, u32[]{:S(2)}) copy-start(bf16[16,64,256]{2,1,0:T(8,128)(2,1)} %param.23) | copy-start | bytes 1572868
  21.7 86.8 %all-gather.5.cloned.1.call-start = ((), (), s32[]{:S(2)}) async-start(), calls=%async_computation.1 | async-start | bytes 2621440 | tf_op jit(solution)/shard_map/all_gather | solution.py:65
  22.5 25.2 %copy-start.38 = (s32[1,96,2]{1,2,0:T(2,128)S(1)}, s32[1,96,2]{1,2,0:T(2,128)}, u32[]{:S(2)}) copy-start(s32[1,96,2]{1,2,0:T(2,128)} %param.35) | copy-start | bytes 2308
  22.5 26.3 %copy-start.46 = (s32[1,80,2]{1,2,0:T(2,128)S(1)}, s32[1,80,2]{1,2,0:T(2,128)}, u32[]{:S(2)}) copy-start(s32[1,80,2]{1,2,0:T(2,128)} %param.33) | copy-start | bytes 1924
  22.5 26.3 %copy-start.5 = (bf16[16,64,128]{2,1,0:T(8,128)(2,1)S(1)}, bf16[16,64,128]{2,1,0:T(8,128)(2,1)}, u32[]{:S(2)}) copy-start(bf16[16,64,128]{2,1,0:T(8,128)(2,1)} %get-tuple-element.90) | copy-start | bytes 786436
  22.5 124.0 %all-gather.9.cloned.1.call-start = ((), (), s32[]{:S(2)}) async-start(), calls=%async_computation.3 | async-start | bytes 5242880 | tf_op jit(solution)/shard_map/all_gather | solution.py:71
  23.2 261.2 %reduce-scatter.2.cloned.1.call-start = ((), (), s32[]{:S(2)}) async-start(), calls=%async_computation.4 | async-start | bytes 655360 | tf_op jit(solution)/shard_map/reduce_scatter | solution.py:210
  23.3 25.5 %copy-start.10 = (bf16[16,16,256]{2,1,0:T(8,128)(2,1)}, bf16[16,16,256]{2,1,0:T(8,128)(2,1)S(1)}, u32[]{:S(2)}) copy-start(bf16[16,16,256]{2,1,0:T(8,128)(2,1)S(1)} %add_convert_fusion) | copy-start | bytes 393220
  24.0 25.7 %copy-start.45 = (s32[1,2,128]{2,1,0:T(2,128)S(1)}, s32[1,2,128]{2,1,0:T(2,128)}, u32[]{:S(2)}) copy-start(s32[1,2,128]{2,1,0:T(2,128)} %param.31) | copy-start | bytes 3076
  29.5 21.4 %collective-permute-start = (bf16[16,128]{1,0:T(8,128)(2,1)S(1)}, bf16[16,128]{1,0:T(8,128)(2,1)S(1)}, u32[]{:S(2)}, u32[]{:S(2)}) collective-permute-start(bf16[16,128]{1,0:T(8,128)(2,1)S(1)} %convolution_convert_fusion.6), channel_id=1, source_target_pairs={{0,4},{4,0},{8,12},{12,8},{16,20},{20,16},{24,28},{28,24},{1,5},{5... | collective-permute-start | bytes 12296 | tf_op jit(solution)/shard_map/ppermute | solution.py:14
  30.0 20.2 %copy-start.39 = (pred[128]{0:T(512)(128)(4,1)}, pred[128]{0:T(512)(128)(4,1)S(1)}, u32[]{:S(2)}) copy-start(pred[128]{0:T(512)(128)(4,1)S(1)} %compare_and_fusion.7) | copy-start | bytes 388
  37.1 13.8 %copy-start.16 = (bf16[1,2,128,256]{3,2,1,0:T(8,128)(2,1)S(1)}, bf16[1,2,128,256]{3,2,1,0:T(8,128)(2,1)}, u32[]{:S(2)}) copy-start(bf16[1,2,128,256]{3,2,1,0:T(8,128)(2,1)} %param.32) | copy-start | bytes 393220
  37.9 38.7 %collective-permute-start.1 = (bf16[64,128]{0,1:T(8,128)(2,1)S(1)}, bf16[64,128]{0,1:T(8,128)(2,1)}, u32[]{:S(2)}, u32[]{:S(2)}) collective-permute-start(bf16[64,128]{0,1:T(8,128)(2,1)S(1)} %select_bitcast_fusion.2), channel_id=1, source_target_pairs={{0,4},{4,0},{8,12},{12,8},{16,20},{20,16},{24,28},{28,24},{1,5},{5... | collective-permute-start | bytes 49160 | tf_op jit(solution)/shard_map/ppermute | solution.py:14
  48.8 41.6 %copy-start.35 = (s32[1024]{0:T(1024)}, s32[1024]{0:T(1024)S(1)}, u32[]{:S(2)}) copy-start(s32[1024]{0:T(1024)S(1)} %get-tuple-element.109) | copy-start | bytes 12292
  50.9 16.7 %copy-start.31 = (bf16[16,128]{1,0:T(8,128)(2,1)}, bf16[16,128]{1,0:T(8,128)(2,1)S(1)}, u32[]{:S(2)}) copy-start(bf16[16,128]{1,0:T(8,128)(2,1)S(1)} %get-tuple-element.97) | copy-start | bytes 12292
  51.6 20.1 %collective-permute-start.2 = (bf16[16,128]{1,0:T(8,128)(2,1)}, bf16[16,128]{1,0:T(8,128)(2,1)}, u32[]{:S(2)}, u32[]{:S(2)}) collective-permute-start(bf16[16,128]{1,0:T(8,128)(2,1)} %convolution_convert_fusion.5), channel_id=1, source_target_pairs={{0,8},{8,0},{4,12},{12,4},{16,24},{24,16},{20,28},{28,20},{1,9},{9... | collective-permute-start | bytes 12296 | tf_op jit(solution)/shard_map/ppermute | solution.py:14
  74.0 98.6 %collective-permute-start.4 = (bf16[16,128]{1,0:T(8,128)(2,1)}, bf16[16,128]{1,0:T(8,128)(2,1)}, u32[]{:S(2)}, u32[]{:S(2)}) collective-permute-start(bf16[16,128]{1,0:T(8,128)(2,1)} %convolution_convert_fusion.4), channel_id=1, source_target_pairs={{0,16},{16,0},{4,20},{20,4},{8,24},{24,8},{12,28},{28,12},{1,17},{... | collective-permute-start | bytes 12296 | tf_op jit(solution)/shard_map/ppermute | solution.py:14
  79.0 4.0 %collective-permute-start.3 = (bf16[64,128]{0,1:T(8,128)(2,1)S(1)}, bf16[64,128]{0,1:T(8,128)(2,1)S(1)}, u32[]{:S(2)}, u32[]{:S(2)}) collective-permute-start(bf16[64,128]{0,1:T(8,128)(2,1)S(1)} %select_bitcast_fusion.1), channel_id=1, source_target_pairs={{0,8},{8,0},{4,12},{12,4},{16,24},{24,16},{20,28},{28,20},{1,9},{9... | collective-permute-start | bytes 49160 | tf_op jit(solution)/shard_map/ppermute | solution.py:14
  79.7 22.1 %copy-start.14 = (bf16[128,128]{1,0:T(8,128)(2,1)}, bf16[128,128]{1,0:T(8,128)(2,1)S(1)}, u32[]{:S(2)}) copy-start(bf16[128,128]{1,0:T(8,128)(2,1)S(1)} %fusion.32) | copy-start | bytes 98308
  84.6 17.1 %copy-start.24 = (bf16[64,128]{0,1:T(8,128)(2,1)}, bf16[64,128]{0,1:T(8,128)(2,1)S(1)}, u32[]{:S(2)}) copy-start(bf16[64,128]{0,1:T(8,128)(2,1)S(1)} %select_bitcast_fusion) | copy-start | bytes 49156
  84.6 5.1 %collective-permute-start.5 = (bf16[64,128]{0,1:T(8,128)(2,1)S(1)}, bf16[64,128]{0,1:T(8,128)(2,1)S(1)}, u32[]{:S(2)}, u32[]{:S(2)}) collective-permute-start(bf16[64,128]{0,1:T(8,128)(2,1)S(1)} %select_bitcast_fusion), channel_id=1, source_target_pairs={{0,16},{16,0},{4,20},{20,4},{8,24},{24,8},{12,28},{28,12},{1,17},{... | collective-permute-start | bytes 49160 | tf_op jit(solution)/shard_map/ppermute | solution.py:14
  85.2 16.5 %copy-start.18 = (bf16[128,128]{1,0:T(8,128)(2,1)}, bf16[128,128]{1,0:T(8,128)(2,1)S(1)}, u32[]{:S(2)}) copy-start(bf16[128,128]{1,0:T(8,128)(2,1)S(1)} %fusion.33) | copy-start | bytes 98308
  89.7 12.0 %copy-start.26 = (bf16[64,128]{0,1:T(8,128)(2,1)}, bf16[64,128]{0,1:T(8,128)(2,1)S(1)}, u32[]{:S(2)}) copy-start(bf16[64,128]{0,1:T(8,128)(2,1)S(1)} %collective-permute-done.5) | copy-start | bytes 49156
  111.0 8.4 %copy-start.20 = (pred[16]{0:T(512)(128)(4,1)}, pred[16]{0:T(512)(128)(4,1)S(1)}, u32[]{:S(2)}) copy-start(pred[16]{0:T(512)(128)(4,1)S(1)} %get-tuple-element.167) | copy-start | bytes 52 | tf_op jit(solution)/shard_map/while
  111.0 8.4 %copy-start.21 = (s32[16]{0:T(128)}, s32[16]{0:T(128)S(1)}, u32[]{:S(2)}) copy-start(s32[16]{0:T(128)S(1)} %get-tuple-element.166) | copy-start | bytes 196 | tf_op jit(solution)/shard_map/while
  111.0 8.4 %copy-start.22 = (s32[16]{0:T(128)}, s32[16]{0:T(128)S(1)}, u32[]{:S(2)}) copy-start(s32[16]{0:T(128)S(1)} %get-tuple-element.164) | copy-start | bytes 196 | tf_op jit(solution)/shard_map/while
  146.5 8.4 %copy-start.44 = (pred[96]{0:T(512)(128)(4,1)S(1)}, pred[96]{0:T(512)(128)(4,1)}, u32[]{:S(2)}) copy-start(pred[96]{0:T(512)(128)(4,1)} %copy-done.42) | copy-start | bytes 292
  162.5 9.9 %copy-start.25 = (bf16[64,128]{0,1:T(8,128)(2,1)S(1)}, bf16[64,128]{0,1:T(8,128)(2,1)}, u32[]{:S(2)}) copy-start(bf16[64,128]{0,1:T(8,128)(2,1)} %copy-done.24) | copy-start | bytes 49156
  162.5 9.9 %copy-start.27 = (bf16[64,128]{0,1:T(8,128)(2,1)S(1)}, bf16[64,128]{0,1:T(8,128)(2,1)}, u32[]{:S(2)}) copy-start(bf16[64,128]{0,1:T(8,128)(2,1)} %copy-done.26) | copy-start | bytes 49156
  162.5 9.9 %copy-start.47 = (f32[128]{0:T(128)S(1)}, f32[128]{0:T(128)}, u32[]{:S(2)}) copy-start(f32[128]{0:T(128)} %get-tuple-element.53) | copy-start | bytes 1540
  162.5 9.9 %copy-start.48 = (f32[128]{0:T(128)S(1)}, f32[128]{0:T(128)}, u32[]{:S(2)}) copy-start(f32[128]{0:T(128)} %get-tuple-element.54) | copy-start | bytes 1540
  162.5 10.9 %copy-start.17 = (bf16[1,2,128,256]{3,2,1,0:T(8,128)(2,1)S(1)}, bf16[1,2,128,256]{3,2,1,0:T(8,128)(2,1)}, u32[]{:S(2)}) copy-start(bf16[1,2,128,256]{3,2,1,0:T(8,128)(2,1)} %param.32) | copy-start | bytes 393220
  162.5 11.9 %copy-start.19 = (bf16[128,128]{1,0:T(8,128)(2,1)S(1)}, bf16[128,128]{1,0:T(8,128)(2,1)}, u32[]{:S(2)}) copy-start(bf16[128,128]{1,0:T(8,128)(2,1)} %copy-done.18) | copy-start | bytes 98308
  162.5 11.9 %copy-start.29 = (f32[16,128]{1,0:T(8,128)S(1)}, f32[16,128]{1,0:T(8,128)}, u32[]{:S(2)}) copy-start(f32[16,128]{1,0:T(8,128)} %fusion.110) | copy-start | bytes 24580
  162.5 11.9 %copy-start.34 = (bf16[16,128]{1,0:T(8,128)(2,1)S(1)}, bf16[16,128]{1,0:T(8,128)(2,1)}, u32[]{:S(2)}) copy-start(bf16[16,128]{1,0:T(8,128)(2,1)} %copy-done.33) | copy-start | bytes 12292
  162.5 12.1 %copy-start.15 = (bf16[128,128]{1,0:T(8,128)(2,1)S(1)}, bf16[128,128]{1,0:T(8,128)(2,1)}, u32[]{:S(2)}) copy-start(bf16[128,128]{1,0:T(8,128)(2,1)} %copy-done.14) | copy-start | bytes 98308
  162.6 12.1 %copy-start.28 = (f32[16,128]{1,0:T(8,128)S(1)}, f32[16,128]{1,0:T(8,128)}, u32[]{:S(2)}) copy-start(f32[16,128]{1,0:T(8,128)} %fusion.109) | copy-start | bytes 24580
  162.6 12.1 %copy-start.32 = (bf16[16,128]{1,0:T(8,128)(2,1)S(1)}, bf16[16,128]{1,0:T(8,128)(2,1)}, u32[]{:S(2)}) copy-start(bf16[16,128]{1,0:T(8,128)(2,1)} %copy-done.31) | copy-start | bytes 12292
  162.6 121.8 %copy-start.7 = (bf16[16,64,256]{2,1,0:T(8,128)(2,1)S(1)}, bf16[16,64,256]{2,1,0:T(8,128)(2,1)}, u32[]{:S(2)}) copy-start(bf16[16,64,256]{2,1,0:T(8,128)(2,1)} %param.23) | copy-start | bytes 1572868
  162.6 121.8 %copy-start.11 = (bf16[16,16,256]{2,1,0:T(8,128)(2,1)S(1)}, bf16[16,16,256]{2,1,0:T(8,128)(2,1)}, u32[]{:S(2)}) copy-start(bf16[16,16,256]{2,1,0:T(8,128)(2,1)} %copy-done.10) | copy-start | bytes 393220
  162.6 121.8 %copy-start.30 = (f32[16,256]{1,0:T(8,128)S(1)}, f32[16,256]{1,0:T(8,128)}, u32[]{:S(2)}) copy-start(f32[16,256]{1,0:T(8,128)} %multiply_reduce_fusion.4) | copy-start | bytes 49156
  175.0 111.9 %copy-start.8 = (bf16[2048,128]{1,0:T(8,128)(2,1)S(1)}, bf16[2048,128]{1,0:T(8,128)(2,1)}, u32[]{:S(2)}) copy-start(bf16[2048,128]{1,0:T(8,128)(2,1)} %copy.36) | copy-start | bytes 1572868
  (13 other events, 60.9 us)
Sparse Core Ops, SparseCore 0:
  21.8 17.3 all-gather.6
  40.7 23.9 all-gather.4
  66.3 34.4 all-gather.8
  172.5 111.8 reduce-scatter.1
where the time goes:
time: 300 us; the launch traced here: 294 us
  waiting for transfers between devices  117 us (39%)
  local copies, waits for them, and re-layouts  51.5 us (17%)
  other arithmetic  40.8 us (14%)
  matrix products  36.8 us (12%)
  blocking collectives  26.3 us (9%)
  between operations  14.5 us (5%)
  starting transfers between devices  7.25 us (2%)
    reduce_scatter x1, waiting for transfers between devices, on_device(): lax.psum_scatter(partial_value.astype(jnp.bfloat16), 'sub', scatter_dimen...  109 us
    scatter-add x2, other arithmetic, on_device(): partial_value.at[own_first + far_first].add(first_points).at[far_second]  22.2 us
    gather x2, local copies, waits for them, and re-layouts, on_device(): leaf_coords = jnp.take_along_axis(points, leaf_skel[:, None, :], axis=2)  11.4 us
    dot_general x5, matrix products, kernel_tile(): jnp.einsum('...da,...db->...ab', first_set, second_set, preferred_element...  9.26 us
    gather x1, local copies, waits for them, and re-layouts, on_device(): jnp.take(all_bases, far_second, axis=0)  8.34 us
    all_gather x1, blocking collectives, on_device(): lax.all_gather(leaf_weights, 'sub', axis=0, tiled=True)  7.79 us
    dot_general x1, matrix products, on_device(): jnp.einsum('fpr,frm->fpm', to_second_far, jnp.take(all_bases, far_second,...  7.57 us
    all_gather x1, blocking collectives, on_device(): lax.all_gather(sign_values, 'sub', axis=0, tiled=True)  7.43 us
  transfers between devices with their start and end apart: 10, of which 3 were waited for; matrix products, arithmetic and copies ran while one was open for 37% of the time, Pallas kernels for 0%

commit v1 on v0

v1 whole, which is shorter than its diff:
```python
import functools

import jax
import jax.numpy as jnp
from jax import lax
from jax.experimental import pallas as pl
from jax.experimental.pallas import tpu as pltpu
from jax.sharding import PartitionSpec as P

BF16 = jnp.bfloat16
F32 = jnp.float32
AUG = 16
NEAR_STEP = 16
FAR_STEP = 32
LIST_ROWS = 16
VMEM = pl.BlockSpec(memory_space=pltpu.VMEM)
SMEM = pl.BlockSpec(memory_space=pltpu.SMEM)
ANY = pl.BlockSpec(memory_space=pl.ANY)
VMEM_LIMIT = 56 << 20


def flipped(block, axis, bits):
    count = lax.axis_size(axis)
    return lax.ppermute(block, axis, [(low, low ^ bits) for low in range(count)])


def dot(left, right, left_dim, right_dim):
    return lax.dot_general(
        left, right, (((left_dim,), (right_dim,)), ((), ())), preferred_element_type=F32
    )


def one_hot(columns, rows, start=0):
    spots = lax.broadcasted_iota(jnp.int32, (rows, columns.shape[1]), 0) + start
    return jnp.where(spots == columns, 1.0, 0.0).astype(BF16)


def norm_parts(coords):
    wide = coords.astype(F32)
    norm = jnp.sum(wide * wide, axis=0, keepdims=True) * (-1.0 / coords.shape[0])
    high = norm.astype(BF16).astype(F32)
    rest = norm - high
    middle = rest.astype(BF16).astype(F32)
    return high, middle, rest - middle


def aug_rows(parts, width, norm_first):
    row = lax.broadcasted_iota(jnp.int32, (AUG, width), 0)
    start, ones = (0, 3) if norm_first else (3, 0)
    block = jnp.where((row >= ones) & (row < ones + 3), 1.0, 0.0)
    for index, part in enumerate(parts):
        block = jnp.where(row == start + index, part, block)
    return block.astype(BF16)


def with_norms(coords, norm_first):
    rows = aug_rows(norm_parts(coords), coords.shape[1], norm_first)
    scaled = (coords.astype(F32) * (2.0 / coords.shape[0])).astype(BF16) if norm_first else coords
    return jnp.concatenate([scaled, rows], axis=0)


def tile(left, right, left_dim, right_dim):
    return jnp.exp(dot(left, right, left_dim, right_dim)).astype(BF16)


def list_row(pairs, row, width):
    count = pairs.shape[0]
    pick = lax.broadcasted_iota(jnp.int32, (8, 2), 0) == lax.broadcasted_iota(
        jnp.int32, (8, 2), 1
    ) + row
    rows = dot(jnp.where(pick, 1.0, 0.0).astype(BF16), pairs.astype(F32).astype(BF16), 1, 1)
    if count == width:
        return rows
    return jnp.concatenate([rows, jnp.zeros((8, width - count), F32)], axis=1)


def prep_kernel(
    points, bits, leaf_skel, leaf_basis, dev_skel, dev_basis, near, near_count, far, q1, q2
):
    leaves, features, size = points.shape
    probes = bits.shape[1]
    skeleton = leaf_skel.shape[1]
    node_weights = jnp.zeros((probes, skeleton), F32)
    node_coords = jnp.zeros((features, skeleton), F32)
    for leaf in range(leaves):
        span = slice(leaf * skeleton, (leaf + 1) * skeleton)
        signs = (2 * bits[leaf] - 1).astype(F32).astype(BF16)
        q2[leaf, :, :size] = signs
        weights = dot(signs, leaf_basis[leaf], 1, 1).astype(BF16)
        q2[leaf, :, size:] = weights
        node_weights += dot(weights, dev_basis[0, :, span], 1, 1)
        coords = dot(points[leaf], one_hot(leaf_skel[leaf : leaf + 1, :], size), 1, 0).astype(BF16)
        node_coords += dot(coords, one_hot(dev_skel[...], skeleton, leaf * skeleton), 1, 0)
    q1[:features] = node_coords.astype(BF16)
    q1[features : features + probes] = node_weights.astype(BF16)
    lists = list_row(near[0], 0, skeleton) + list_row(far[0], 2, skeleton)
    row = lax.broadcasted_iota(jnp.int32, lists.shape, 0)
    lists = jnp.where(row == 4, near_count[0].astype(F32), lists)
    base = features + probes
    q1[base : base + LIST_ROWS] = jnp.concatenate([lists, jnp.zeros_like(lists)], 0).astype(BF16)
    q1[base + LIST_ROWS :] = leaf_skel[...].astype(F32).astype(BF16)


def own_kernel(points, leaf_skel, q2, lhs_t, rhs, lhs_c, rhs_c, near):
    leaves, features, size = points.shape
    for leaf in range(leaves):
        left = with_norms(points[leaf], True)
        right = with_norms(points[leaf], False)
        both = dot(
            jnp.concatenate([left, right], 0), one_hot(leaf_skel[leaf : leaf + 1, :], size), 1, 0
        )
        rhs[leaf] = right
        lhs_t[leaf] = left.T
        lhs_c[leaf] = both[: features + AUG].T.astype(BF16)
        rhs_c[leaf] = both[features + AUG :].astype(BF16)
    for leaf in range(leaves):
        block = tile(lhs_t[leaf], rhs[leaf], 1, 0)
        near[leaf] = dot(q2[leaf, :, :size], block, 1, 1)


def node_kernel(features, probes, cap, far_cap, mine, one, two, three, basis, skel, node, lists, q1):
    skeleton = mine.shape[1]
    leaves = mine.shape[0] - features - probes - LIST_ROWS
    shift = leaves.bit_length() - 1
    groups = 4
    me = lax.axis_index("sub")
    for rel, ref in enumerate((mine, one, two, three)):
        q1[rel] = ref[...]
    weights = jnp.zeros((probes, skeleton), F32)
    coords = jnp.zeros((features, skeleton), F32)
    for spot in range(groups):
        block = q1[jnp.bitwise_xor(me, spot)]
        span = slice(spot * skeleton, (spot + 1) * skeleton)
        weights += dot(block[features : features + probes], basis[0, :, span], 1, 1)
        coords += dot(block[:features], one_hot(skel[...], skeleton, spot * skeleton), 1, 0)
    node[:features] = coords.astype(BF16)
    node[features:] = weights.astype(BF16)

    base = features + probes
    lane = lax.broadcasted_iota(jnp.int32, (1, skeleton), 1)
    rows = [q1[rel, base : base + LIST_ROWS].astype(F32) for rel in range(groups)]
    whole = [block.astype(jnp.int32) for block in rows]
    segments = []
    for kind, limit in ((0, cap), (2, far_cap)):
        for rel in (None, 0, 1, 2, 3):
            block = whole[0 if rel is None else rel]
            first = block[kind : kind + 1]
            second = block[kind + 1 : kind + 2]
            used = lane < (block[4:5] if kind == 0 else limit)
            owner = second >> shift
            inner = second & (leaves - 1)
            if rel is None:
                apart = jnp.bitwise_xor(owner, me)
                own, slot = first, (apart & 1) * leaves + inner
                crosses = apart >= 2
                segments.append((kind, 0, own, slot, used & jnp.logical_not(crosses)))
                segments.append((kind, 1, own, slot, used & crosses))
            else:
                own, slot = inner, (rel & 1) * leaves + first
                segments.append((kind, rel >> 1, own, slot, used & (owner == me)))
    masks = jnp.concatenate([jnp.where(part[4], 1.0, 0.0) for part in segments], 0)
    count = len(segments)
    padded = -count % 16
    masks = jnp.concatenate([masks, jnp.zeros((padded, skeleton), F32)], 0)
    before = lax.broadcasted_iota(jnp.int32, (skeleton, skeleton), 0) < lax.broadcasted_iota(
        jnp.int32, (skeleton, skeleton), 1
    )
    prefix = dot(masks.astype(BF16), jnp.where(before, 1.0, 0.0).astype(BF16), 1, 0)
    totals = jnp.sum(masks, axis=1, keepdims=True)
    width = lists.shape[1]
    for kind in (0, 2):
        for cross in (0, 1):
            offset = jnp.zeros((1, 1), F32)
            result = jnp.zeros((8, width), F32)
            for index, part in enumerate(segments):
                if part[0] != kind or part[1] != cross:
                    continue
                place = jnp.where(part[4], prefix[index : index + 1] + offset, -1.0)
                offset += totals[index : index + 1]
                spots = lax.broadcasted_iota(jnp.int32, (width, skeleton), 0)
                hot = jnp.where(spots == place.astype(jnp.int32), 1.0, 0.0).astype(BF16)
                values = jnp.concatenate(
                    [part[2].astype(F32), part[3].astype(F32), jnp.zeros((6, skeleton), F32)], 0
                ).astype(BF16)
                result += dot(values, hot, 1, 1)
            line = kind + cross
            lists[2 * line : 2 * line + 2] = result[:2].astype(jnp.int32)
            lists[8 + line : 9 + line] = jnp.broadcast_to(offset, (1, width)).astype(jnp.int32)
    lists[12:] = jnp.zeros((4, width), jnp.int32)


def level_kernel(features, height, mine, other, basis, skel, node, pair):
    skeleton = mine.shape[1]
    on_right = (lax.axis_index("leaf") >> (height - 1)) & 1
    pair[0] = mine[...]
    pair[1] = other[...]
    left = pair[on_right]
    right = pair[1 - on_right]
    line = skel[0, height - 1 : height, :]
    weights = dot(left[features:], basis[0, height - 1, :, :skeleton], 1, 1)
    weights += dot(right[features:], basis[0, height - 1, :, skeleton:], 1, 1)
    coords = dot(left[:features], one_hot(line, skeleton), 1, 0)
    coords += dot(right[:features], one_hot(line, skeleton, skeleton), 1, 0)
    node[:features] = coords.astype(BF16)
    node[features:] = weights.astype(BF16)


def down_kernel(features, levels, *refs):
    nodes, refs = refs[: 2 * levels], refs[2 * levels :]
    upper_basis, subtree_basis, dev_basis, potentials = refs
    skeleton = nodes[0].shape[1]
    me = lax.axis_index("sub")
    subtree = lax.axis_index("leaf")
    far = []
    for level in range(levels):
        mine, other = nodes[2 * level], nodes[2 * level + 1]
        block = tile(
            with_norms(mine[:features], True), with_norms(other[:features], False), 0, 0
        )
        far.append(dot(other[features:], block, 1, 1))
    potential = far[levels - 1]
    for height in range(levels - 1, 0, -1):
        side = pl.multiple_of(((subtree >> (height - 1)) & 1) * skeleton, skeleton)
        part = upper_basis[0, height - 1, :, pl.ds(side, skeleton)]
        potential = far[height - 1] + dot(potential.astype(BF16), part, 1, 0)
    spot = pl.multiple_of(me * skeleton, skeleton)
    device = dot(potential.astype(BF16), subtree_basis[0, :, pl.ds(spot, skeleton)], 1, 0)
    spread = dot(device.astype(BF16), dev_basis[0], 1, 0).astype(BF16)
    for leaf in range(potentials.shape[0]):
        potentials[leaf] = spread[:, leaf * skeleton : (leaf + 1) * skeleton]


def build_sources(rhs, rhs_c, q1, base, features, probes, leaves):
    size = rhs.shape[2]
    skels = q1[features + probes + LIST_ROWS :].astype(F32).astype(jnp.int32)
    for leaf in range(leaves):
        right = with_norms(rhs[base + leaf, :features], False)
        rhs[base + leaf, features:] = right[features:]
        rhs_c[base + leaf] = dot(right, one_hot(skels[leaf : leaf + 1], size), 1, 0).astype(BF16)


def pair_sums(cross, lists, lhs_t, lhs_c, rhs, rhs_c, sw, near, far):
    size = rhs.shape[2]
    skeleton = rhs_c.shape[2]
    line = cross
    count = lists[8 + line, 0]

    def near_step(step, carry):
        results = []
        for index in range(NEAR_STEP):
            spot = step * NEAR_STEP + index
            own, slot = lists[2 * line, spot], lists[2 * line + 1, spot]
            block = tile(lhs_t[own], rhs[slot], 1, 0)
            part = dot(sw[slot, :, :size], block, 1, 1)
            results.append((own, jnp.where(spot < count, part, 0.0)))
        for own, part in results:
            near[own] += part
        return carry

    lax.fori_loop(0, (count + NEAR_STEP - 1) // NEAR_STEP, near_step, 0)
    far_line = 2 + cross
    far_count = lists[8 + far_line, 0]

    def far_step(step, carry):
        results = []
        for index in range(0, FAR_STEP, 2):
            spots = [step * FAR_STEP + index + half for half in range(2)]
            owns = [lists[2 * far_line, spot] for spot in spots]
            slots = [lists[2 * far_line + 1, spot] for spot in spots]
            blocks = [tile(lhs_c[own], rhs_c[slot], 1, 0) for own, slot in zip(owns, slots)]
            weights = jnp.concatenate([sw[slot, :, size:] for slot in slots], 0)
            part = dot(weights, jnp.concatenate(blocks, 0), 1, 1)
            probes = part.shape[0] // 2
            for half in range(2):
                mine = part[half * probes : (half + 1) * probes, half * skeleton : (half + 1) * skeleton]
                mine = mine.astype(BF16).astype(F32)
                results.append((owns[half], jnp.where(spots[half] < far_count, mine, 0.0)))
        for own, part in results:
            far[own] += part
        return carry

    lax.fori_loop(0, (far_count + FAR_STEP - 1) // FAR_STEP, far_step, 0)


def chip_kernel(
    features, lists, q1, lhs_t, lhs_c, own_rhs, own_rhs_c, own_q2, points, q2, near_in,
    near, far, rhs, rhs_c, sw, sems,
):
    leaves = own_rhs.shape[0]
    probes = q2.shape[1]
    copies = [
        pltpu.make_async_copy(points, rhs.at[pl.ds(leaves, leaves), pl.ds(0, features)], sems.at[0]),
        pltpu.make_async_copy(own_rhs, rhs.at[pl.ds(0, leaves)], sems.at[1]),
        pltpu.make_async_copy(own_rhs_c, rhs_c.at[pl.ds(0, leaves)], sems.at[2]),
        pltpu.make_async_copy(own_q2, sw.at[pl.ds(0, leaves)], sems.at[3]),
        pltpu.make_async_copy(q2, sw.at[pl.ds(leaves, leaves)], sems.at[4]),
    ]
    for copy in copies:
        copy.start()
    near[...] = near_in[...]
    far[...] = jnp.zeros_like(far)
    copies[0].wait()
    build_sources(rhs, rhs_c, q1, leaves, features, probes, leaves)
    for copy in copies[1:]:
        copy.wait()
    pair_sums(0, lists, lhs_t, lhs_c, rhs, rhs_c, sw, near, far)


def cross_kernel(
    features, lists, q1_two, q1_three, lhs_t, lhs_c, points_two, points_three, q2_two, q2_three,
    near_in, far_in, potentials, leaf_basis,
    out, near, far, rhs, rhs_c, sw, basis, sems,
):
    leaves = points_two.shape[0]
    probes = q2_two.shape[1]
    copies = []
    for index, (source, signs) in enumerate(((points_two, q2_two), (points_three, q2_three))):
        span = pl.ds(index * leaves, leaves)
        copies.append(
            pltpu.make_async_copy(source, rhs.at[span, pl.ds(0, features)], sems.at[2 * index])
        )
        copies.append(pltpu.make_async_copy(signs, sw.at[span], sems.at[2 * index + 1]))
    copies.append(pltpu.make_async_copy(leaf_basis, basis, sems.at[4]))
    for copy in copies:
        copy.start()
    near[...] = near_in[...]
    far[...] = far_in[...]
    copies[0].wait()
    build_sources(rhs, rhs_c, q1_two, 0, features, probes, leaves)
    copies[2].wait()
    build_sources(rhs, rhs_c, q1_three, leaves, features, probes, leaves)
    copies[1].wait()
    copies[3].wait()
    pair_sums(1, lists, lhs_t, lhs_c, rhs, rhs_c, sw, near, far)
    copies[4].wait()
    for leaf in range(leaves):
        total = potentials[leaf].astype(F32) + far[leaf]
        high = total.astype(BF16)
        low = (total - high.astype(F32)).astype(BF16)
        part = dot(jnp.concatenate([high, low], 0), basis[leaf], 1, 0)
        out[leaf] = near[leaf] + part[:probes] + part[probes:]


def call(kernel, name, out_shape, in_specs, scratch, micros, *args):
    return pl.pallas_call(
        kernel,
        name=name,
        out_shape=out_shape,
        in_specs=in_specs,
        out_specs=jax.tree.map(lambda _: VMEM, out_shape),
        scratch_shapes=scratch,
        compiler_params=pltpu.CompilerParams(vmem_limit_bytes=VMEM_LIMIT),
        cost_estimate=pl.CostEstimate(
            flops=int(micros * 1e9), bytes_accessed=int(micros * 1e6), transcendentals=0
        ),
    )(*args)


def on_device(
    points,
    probe_bits,
    leaf_skel,
    leaf_basis,
    device_skel,
    device_basis,
    subtree_skel,
    subtree_basis,
    upper_skel,
    upper_basis,
    near_pairs,
    near_count,
    far_pairs,
):
    leaves, features, size = points.shape
    probes = probe_bits.shape[1]
    skeleton = leaf_skel.shape[1]
    levels = lax.axis_size("leaf").bit_length() - 1
    cap = near_pairs.shape[1]
    far_cap = far_pairs.shape[1]
    depth = features + AUG
    width = max(-(-3 * cap // 128), -(-3 * far_cap // 128)) * 128
    q1_rows = features + probes + LIST_ROWS + leaves
    shape = jax.ShapeDtypeStruct

    points_two = flipped(points, "sub", 2)
    points_one = flipped(points, "sub", 1)

    q1, q2 = call(
        prep_kernel,
        "prep",
        (shape((q1_rows, skeleton), BF16), shape((leaves, probes, size + skeleton), BF16)),
        [VMEM] * 7 + [SMEM, VMEM],
        [],
        4,
        points,
        probe_bits,
        leaf_skel,
        leaf_basis,
        device_skel,
        device_basis,
        near_pairs,
        near_count,
        far_pairs,
    )
    q1_one, q1_two, q1_three = (flipped(q1, "sub", bits) for bits in (1, 2, 3))
    q2_two = flipped(q2, "sub", 2)
    q2_one = flipped(q2, "sub", 1)

    lhs_t, rhs, lhs_c, rhs_c, near = call(
        own_kernel,
        "own",
        (
            shape((leaves, size, depth), BF16),
            shape((leaves, depth, size), BF16),
            shape((leaves, skeleton, depth), BF16),
            shape((leaves, depth, skeleton), BF16),
            shape((leaves, probes, size), F32),
        ),
        [VMEM] * 3,
        [],
        5,
        points,
        leaf_skel,
        q2,
    )

    node, lists = call(
        functools.partial(node_kernel, features, probes, cap, far_cap),
        "node",
        (shape((features + probes, skeleton), BF16), shape((16, width), jnp.int32)),
        [VMEM] * 6,
        [pltpu.VMEM((4, q1_rows, skeleton), BF16)],
        2,
        q1,
        q1_one,
        q1_two,
        q1_three,
        subtree_basis,
        subtree_skel,
    )
    nodes = []
    for height in range(1, levels + 1):
        other = flipped(node, "leaf", 1 << (height - 1))
        nodes += [node, other]
        if height < levels:
            node = call(
                functools.partial(level_kernel, features, height),
                f"level{height}",
                shape((features + probes, skeleton), BF16),
                [VMEM] * 4,
                [pltpu.VMEM((2, features + probes, skeleton), BF16)],
                1,
                node,
                other,
                upper_basis,
                upper_skel,
            )

    near, far = call(
        functools.partial(chip_kernel, features),
        "chip",
        (shape((leaves, probes, size), F32), shape((leaves, probes, skeleton), F32)),
        [SMEM, VMEM, VMEM, VMEM] + [ANY] * 5 + [VMEM],
        [
            pltpu.VMEM((2 * leaves, depth, size), BF16),
            pltpu.VMEM((2 * leaves, depth, skeleton), BF16),
            pltpu.VMEM((2 * leaves, probes, size + skeleton), BF16),
            pltpu.SemaphoreType.DMA((5,)),
        ],
        10,
        lists,
        q1_one,
        lhs_t,
        lhs_c,
        rhs,
        rhs_c,
        q2,
        points_one,
        q2_one,
        near,
    )

    potentials = call(
        functools.partial(down_kernel, features, levels),
        "down",
        shape((leaves, probes, skeleton), BF16),
        [VMEM] * (2 * levels + 3),
        [],
        2,
        *nodes,
        upper_basis,
        subtree_basis,
        device_basis,
    )

    points_three = flipped(points_two, "sub", 1)
    q2_three = flipped(q2_two, "sub", 1)
    return call(
        functools.partial(cross_kernel, features),
        "cross",
        shape((leaves, probes, size), F32),
        [SMEM] + [VMEM] * 4 + [ANY] * 4 + [VMEM] * 3 + [ANY],
        [
            pltpu.VMEM((leaves, probes, size), F32),
            pltpu.VMEM((leaves, probes, skeleton), F32),
            pltpu.VMEM((2 * leaves, depth, size), BF16),
            pltpu.VMEM((2 * leaves, depth, skeleton), BF16),
            pltpu.VMEM((2 * leaves, probes, size + skeleton), BF16),
            pltpu.VMEM((leaves, skeleton, size), BF16),
            pltpu.SemaphoreType.DMA((5,)),
        ],
        10,
        lists,
        q1_two,
        q1_three,
        lhs_t,
        lhs_c,
        points_two,
        points_three,
        q2_two,
        q2_three,
        near,
        far,
        potentials,
        leaf_basis,
    )


def solution(mesh):
    return jax.shard_map(
        on_device,
        mesh=mesh,
        in_specs=(
            P(("leaf", "sub"), None, None),
            P(("leaf", "sub"), None, None),
            P(("leaf", "sub"), None),
            P(("leaf", "sub"), None, None),
            P(("leaf", "sub"), None),
            P(("leaf", "sub"), None, None),
            P("leaf", None),
            P("leaf", None, None),
            P("leaf", None, None),
            P("leaf", None, None, None),
            P(("leaf", "sub"), None, None),
            P(("leaf", "sub")),
            P(("leaf", "sub"), None, None),
        ),
        out_specs=P(("leaf", "sub"), None, None),
        check_vma=False,
    )
```

time: 300 us -> 71.4 us (0.24); the launches traced: 294 us -> 71.1 us
  waiting for transfers between devices: 117 us -> 7.74 us
  Pallas kernels: 0 us -> 46.7 us
  local copies, waits for them, and re-layouts: 51.5 us -> 6.92 us
  other arithmetic: 40.8 us -> 0 us
  matrix products: 36.8 us -> 0 us
  blocking collectives: 26.3 us -> 0 us
  between operations: 14.5 us -> 0.77 us
    reduce_scatter x1 -> x0, waiting for transfers between devices: 109 us -> none  [on_device(): lax.psum_scatter(partial_value.astype(jnp.bfloat16), 'sub', scatter_dimen...]
    pallas_call x0 -> x8, Pallas kernels: none -> 46.7 us  [call(): pl.pallas_call(kernel, name=name, out_shape=out_shape, in_specs=in_specs,...]
    gather x18 -> x0, local copies, waits for them, and re-layouts: 44.7 us -> none  [the longest x2 11.4 us: on_device(): leaf_coords = jnp.take_along_axis(points, leaf_skel[:, None, :], axis=2)]
    dot_general x22 -> x0, matrix products: 36.8 us -> none  [the longest x5 9.26 us: kernel_tile(): jnp.einsum('...da,...db->...ab', first_set, second_set, preferred_element...]
    scatter-add x4 -> x0, other arithmetic: 27.4 us -> none  [the longest x2 22.2 us: on_device(): partial_value.at[own_first + far_first].add(first_points).at[far_second]]
    all_gather x4 -> x0, blocking collectives: 26.3 us -> none  [the longest x1 7.79 us: on_device(): lax.all_gather(leaf_weights, 'sub', axis=0, tiled=True)]
    reduce_sum x8 -> x0, other arithmetic: 6.25 us -> none  [the longest x4 3.7 us: kernel_tile(): first_norm = jnp.sum(first_wide * first_wide, axis=-2)]
    unnamed x91 -> x32, local copies, waits for them, and re-layouts: 1.75 us -> 6.92 us
  transfers between devices with their start and end apart: 10 -> 12, of which waited for: 3 -> 3; matrix products, arithmetic and copies ran while one was open for 37% -> 0% of each run, Pallas kernels for 0% -> 34%
where the time goes in v1:
time: 71.4 us; the launch traced here: 71.1 us
  Pallas kernels  46.7 us (65%)
  starting transfers between devices  9.02 us (13%)
  waiting for transfers between devices  7.74 us (11%)
  local copies, waits for them, and re-layouts  6.92 us (10%)
  between operations  0.77 us (1%)
    pallas_call x8, Pallas kernels, call(): pl.pallas_call(kernel, name=name, out_shape=out_shape, in_specs=in_specs,...  46.7 us
    ppermute x12, starting transfers between devices, flipped(): lax.ppermute(block, axis, [(low, low ^ bits) for low in range(count)])  9.02 us
    ppermute x12, waiting for transfers between devices, flipped(): lax.ppermute(block, axis, [(low, low ^ bits) for low in range(count)])  7.74 us
    unnamed x32, local copies, waits for them, and re-layouts  6.92 us
  transfers between devices with their start and end apart: 12, of which 3 were waited for; matrix products, arithmetic and copies ran while one was open for 0% of the time, Pallas kernels for 34%

profile of v1, /device:TPU:6, one launch (start us, length us, event | category | flops | bytes accessed | tf_op | source)
XLA Modules:
  0.0 71.1 jit_solution(1519947682630208256)
XLA Ops:
  0.0 1.4 %copy.15.far = s32[1,96,2]{2,1,0:T(8,128)} copy(s32[1,96,2]{1,2,0:T(2,128)} %param.25) | data formatting | bytes 1536 | tf_op args[12]
  1.4 0.0 copy-done
  1.4 0.7 copy.14.near
  2.8 4.7 %prep.1 = (bf16[112,128]{1,0:T(8,128)(2,1)}, bf16[16,16,384]{2,1,0:T(8,128)(2,1)}) custom-call(bf16[16,64,256]{2,1,0:T(8,128)(2,1)} %points.3, s32[16,16,256]{2,1,0:T(8,128)} %bits.1, s32[16,128]{1,0:T(8,128)} %leaf_skel.3, bf16[16,128,256]{2,1,0:T(8,128)(2,1)} %leaf_basis.3, s32[1,128]{1,0:T(1,128)} %dev_skel.1, bf16[1,128,2048]{2,1,0:T(8,128)(2,1)} %refs_8_.1, ...), custom_call_target="tpu_custom_call" | custom-call | flops 4000000000 | bytes 4000000 | tf_op jit(solution)/shard_map/prep/pallas_call | solution.py:345
  7.5 0.0 collective-permute-start
  7.5 0.5 collective-permute-start.1
  8.1 1.3 %collective-permute-start.2 = (bf16[112,128]{1,0:T(8,128)(2,1)}, bf16[112,128]{1,0:T(8,128)(2,1)S(1)}, u32[]{:S(2)}, u32[]{:S(2)}) collective-permute-start(bf16[112,128]{1,0:T(8,128)(2,1)} %get-tuple-element.16.mine), channel_id=1, source_target_pairs={{0,3},{1,2},{2,1},{3,0},{4,7},{5,6},{6,5},{7,4},{8,11},{9,10},{10,... | collective-permute-start | bytes 86024 | tf_op jit(solution)/shard_map/ppermute | solution.py:24
  9.4 0.0 collective-permute-done.one.q1
  9.4 2.5 %collective-permute-done.1.two.q1_two = bf16[112,128]{1,0:T(8,128)(2,1)S(1)} collective-permute-done((bf16[112,128]{1,0:T(8,128)(2,1)}, bf16[112,128]{1,0:T(8,128)(2,1)S(1)}, u32[]{:S(2)}, u32[]{:S(2)}) %collective-permute-start.1) | collective-permute-done | bytes 28704 | tf_op jit(solution)/shard_map/ppermute | solution.py:24
  11.9 0.0 collective-permute-done.2.three.q1_three
  11.9 0.0 copy-done.11
  11.9 0.6 copy-done.9
  12.5 0.6 copy-done.10
  13.1 2.4 %node.1 = (bf16[80,128]{1,0:T(8,128)(2,1)}, s32[16,384]{1,0:T(8,128)}) custom-call(bf16[112,128]{1,0:T(8,128)(2,1)} %get-tuple-element.16.mine, bf16[112,128]{1,0:T(8,128)(2,1)} %copy-done.11, bf16[112,128]{1,0:T(8,128)(2,1)} %copy-done.9, bf16[112,128]{1,0:T(8,128)(2,1)} %copy-done.10, bf16[1,128,512]{2,1,0:T(8,128)(2,1)} %refs_7_.1, s32[1,128]{1,0:T(1,128)} %skel.3), custom_call_target="tpu_custom_call" | custom-call | flops 2000000000 | bytes 2000000 | tf_op jit(solution)/shard_map/node/pallas_call | solution.py:345
  15.4 0.4 collective-permute-start.9
  15.8 3.6 %collective-permute-done.9.other.refs_1_ = bf16[80,128]{1,0:T(8,128)(2,1)S(1)} collective-permute-done((bf16[80,128]{1,0:T(8,128)(2,1)}, bf16[80,128]{1,0:T(8,128)(2,1)S(1)}, u32[]{:S(2)}, u32[]{:S(2)}) %collective-permute-start.9) | collective-permute-done | bytes 20512 | tf_op jit(solution)/shard_map/ppermute | solution.py:24
  19.4 0.6 copy-done.12
  20.0 1.7 %level1.1.mine.refs_2_ = bf16[80,128]{1,0:T(8,128)(2,1)} custom-call(bf16[80,128]{1,0:T(8,128)(2,1)} %get-tuple-element.26.mine.refs_0_, bf16[80,128]{1,0:T(8,128)(2,1)} %copy-done.12, bf16[1,2,128,256]{3,2,1,0:T(8,128)(2,1)} %refs_6_.1, s32[1,2,128]{2,1,0:T(2,128)} %skel.5), custom_call_target="tpu_custom_call" | custom-call | flops 1000000000 | bytes 1000000 | tf_op jit(solution)/shard_map/level1/pallas_call | solution.py:345
  21.8 1.6 %collective-permute-start.10 = (bf16[80,128]{1,0:T(8,128)(2,1)}, bf16[80,128]{1,0:T(8,128)(2,1)S(1)}, u32[]{:S(2)}, u32[]{:S(2)}) collective-permute-start(bf16[80,128]{1,0:T(8,128)(2,1)} %level1.1.mine.refs_2_), channel_id=1, source_target_pairs={{0,8},{4,12},{8,0},{12,4},{16,24},{20,28},{24,16},{28,20},{1,9},{5... | collective-permute-start | bytes 61448 | tf_op jit(solution)/shard_map/ppermute | solution.py:24
  23.4 0.0 copy-done.1
  23.4 0.0 collective-permute-start.7
  23.4 0.5 collective-permute-start.8
  23.9 0.6 collective-permute-start.5
  24.4 1.4 %collective-permute-start.3 = (bf16[16,64,256]{2,1,0:T(8,128)(2,1)S(1)}, bf16[16,64,256]{2,1,0:T(8,128)(2,1)S(1)}, u32[]{:S(2)}, u32[]{:S(2)}) collective-permute-start(bf16[16,64,256]{2,1,0:T(8,128)(2,1)S(1)} %copy-done.1), channel_id=1, source_target_pairs={{0,2},{1,3},{2,0},{3,1},{4,6},{5,7},{6,4},{7,5},{8,10},{9,11},{10,... | collective-permute-start | bytes 1572872 | tf_op jit(solution)/shard_map/ppermute | solution.py:24
  25.9 0.0 collective-permute-done.10.other.refs_3_
  25.9 0.6 copy-done.13
  26.5 1.7 %level2.1.refs_4_ = bf16[80,128]{1,0:T(8,128)(2,1)} custom-call(bf16[80,128]{1,0:T(8,128)(2,1)} %level1.1.mine.refs_2_, bf16[80,128]{1,0:T(8,128)(2,1)} %copy-done.13, bf16[1,2,128,256]{3,2,1,0:T(8,128)(2,1)} %refs_6_.1, s32[1,2,128]{2,1,0:T(2,128)} %skel.5), custom_call_target="tpu_custom_call" | custom-call | flops 1000000000 | bytes 1000000 | tf_op jit(solution)/shard_map/level2/pallas_call | solution.py:345
  28.2 2.6 %collective-permute-start.11 = (bf16[80,128]{1,0:T(8,128)(2,1)}, bf16[80,128]{1,0:T(8,128)(2,1)S(1)}, u32[]{:S(2)}, u32[]{:S(2)}) collective-permute-start(bf16[80,128]{1,0:T(8,128)(2,1)} %level2.1.refs_4_), channel_id=1, source_target_pairs={{0,16},{4,20},{8,24},{12,28},{16,0},{20,4},{24,8},{28,12},{1,17},{... | collective-permute-start | bytes 61448 | tf_op jit(solution)/shard_map/ppermute | solution.py:24
  30.8 6.0 %own.1 = (bf16[16,256,80]{2,1,0:T(8,128)(2,1)}, bf16[16,80,256]{2,1,0:T(8,128)(2,1)}, bf16[16,128,80]{2,1,0:T(8,128)(2,1)}, bf16[16,80,128]{2,1,0:T(8,128)(2,1)}, f32[16,16,256]{2,1,0:T(8,128)}) custom-call(bf16[16,64,256]{2,1,0:T(8,128)(2,1)} %points.3, s32[16,128]{1,0:T(8,128)} %leaf_skel.3, bf16[16,16,384]{2,1,0:T(8,128)(2,1)} %get-tuple-element.18.q2.own_q2), custom_call_target="tpu_custom_call" | custom-call | flops 5000000000 | bytes 5000000 | tf_op jit(solution)/shard_map/own/pallas_call | solution.py:345
  36.8 0.0 collective-permute-done.11.refs_5_
  36.8 0.6 copy-done.14
  37.4 2.8 %down.1.potentials = bf16[16,16,128]{2,1,0:T(8,128)(2,1)} custom-call(bf16[80,128]{1,0:T(8,128)(2,1)} %get-tuple-element.26.mine.refs_0_, bf16[80,128]{1,0:T(8,128)(2,1)} %copy-done.12, bf16[80,128]{1,0:T(8,128)(2,1)} %level1.1.mine.refs_2_, bf16[80,128]{1,0:T(8,128)(2,1)} %copy-done.13, bf16[80,128]{1,0:T(8,128)(2,1)} %level2.1.refs_4_, ...), custom_call_target="tpu_custom_call" | custom-call | flops 2000000000 | bytes 2000000 | tf_op jit(solution)/shard_map/down/pallas_call | solution.py:345
  40.3 0.0 collective-permute-done.5.q2_two
  40.3 0.1 collective-permute-start.6
  40.4 1.6 %collective-permute-done.3.points_two = bf16[16,64,256]{2,1,0:T(8,128)(2,1)S(1)} collective-permute-done((bf16[16,64,256]{2,1,0:T(8,128)(2,1)S(1)}, bf16[16,64,256]{2,1,0:T(8,128)(2,1)S(1)}, u32[]{:S(2)}, u32[]{:S(2)}) %collective-permute-start.3) | collective-permute-done | bytes 524320 | tf_op jit(solution)/shard_map/ppermute | solution.py:24
  42.0 0.0 collective-permute-start.4
  42.0 0.0 collective-permute-done.8.q2
  42.0 0.0 collective-permute-done.7.points
  42.0 0.0 copy-start.3
  42.0 0.7 copy-done.7
  42.7 0.2 copy-done.3
  42.9 13.9 %chip.1 = (f32[16,16,256]{2,1,0:T(8,128)}, f32[16,16,128]{2,1,0:T(8,128)}) custom-call(s32[16,384]{1,0:T(8,128)} %get-tuple-element.17.lists, bf16[112,128]{1,0:T(8,128)(2,1)} %copy-done.11, bf16[16,256,80]{2,1,0:T(8,128)(2,1)} %get-tuple-element.19.lhs_t, bf16[16,128,80]{2,1,0:T(8,128)(2,1)} %get-tuple-element.20.lhs_c, ...), custom_call_target="tpu_custom_call" | custom-call | flops 10000000000 | bytes 10000000 | tf_op jit(solution)/shard_map/chip/pallas_call | solution.py:345
  56.8 0.0 collective-permute-done.6.q2_three
  56.8 0.0 collective-permute-done.4.points_three
  56.9 0.0 copy-start.4
  56.9 0.6 copy-done.8
  57.5 0.2 copy-done.4
  57.7 13.4 %cross.1 = f32[16,16,256]{2,1,0:T(8,128)} custom-call(s32[16,384]{1,0:T(8,128)} %get-tuple-element.17.lists, bf16[112,128]{1,0:T(8,128)(2,1)} %copy-done.9, bf16[112,128]{1,0:T(8,128)(2,1)} %copy-done.10, bf16[16,256,80]{2,1,0:T(8,128)(2,1)} %get-tuple-element.19.lhs_t, bf16[16,128,80]{2,1,0:T(8,128)(2,1)} %get-tuple-element.20.lhs_c, ...), custom_call_target="tpu_custom_call" | custom-call | flops 10000000000 | bytes 10000000 | tf_op jit(solution)/shard_map/cross/pallas_call | solution.py:345
  (16 shorter events, 0.0 us)
Async XLA Ops:
  0.0 1.4 %copy-start = (s32[1,80,2]{1,2,0:T(2,128)S(1)}, s32[1,80,2]{1,2,0:T(2,128)}, u32[]{:S(2)}) copy-start(s32[1,80,2]{1,2,0:T(2,128)} %param.23) | copy-start | bytes 1924
  7.5 1.9 %collective-permute-start = (bf16[112,128]{1,0:T(8,128)(2,1)}, bf16[112,128]{1,0:T(8,128)(2,1)S(1)}, u32[]{:S(2)}, u32[]{:S(2)}) collective-permute-start(bf16[112,128]{1,0:T(8,128)(2,1)} %get-tuple-element.16.mine), channel_id=1, source_target_pairs={{0,1},{1,0},{2,3},{3,2},{4,5},{5,4},{6,7},{7,6},{8,9},{9,8},{10,11... | collective-permute-start | bytes 86024 | tf_op jit(solution)/shard_map/ppermute | solution.py:24
  7.5 4.3 %collective-permute-start.1 = (bf16[112,128]{1,0:T(8,128)(2,1)}, bf16[112,128]{1,0:T(8,128)(2,1)S(1)}, u32[]{:S(2)}, u32[]{:S(2)}) collective-permute-start(bf16[112,128]{1,0:T(8,128)(2,1)} %get-tuple-element.16.mine), channel_id=1, source_target_pairs={{0,2},{1,3},{2,0},{3,1},{4,6},{5,7},{6,4},{7,5},{8,10},{9,11},{10,... | collective-permute-start | bytes 86024 | tf_op jit(solution)/shard_map/ppermute | solution.py:24
  8.1 3.8 %collective-permute-start.2 = (bf16[112,128]{1,0:T(8,128)(2,1)}, bf16[112,128]{1,0:T(8,128)(2,1)S(1)}, u32[]{:S(2)}, u32[]{:S(2)}) collective-permute-start(bf16[112,128]{1,0:T(8,128)(2,1)} %get-tuple-element.16.mine), channel_id=1, source_target_pairs={{0,3},{1,2},{2,1},{3,0},{4,7},{5,6},{6,5},{7,4},{8,11},{9,10},{10,... | collective-permute-start | bytes 86024 | tf_op jit(solution)/shard_map/ppermute | solution.py:24
  9.4 2.5 %copy-start.11 = (bf16[112,128]{1,0:T(8,128)(2,1)}, bf16[112,128]{1,0:T(8,128)(2,1)S(1)}, u32[]{:S(2)}) copy-start(bf16[112,128]{1,0:T(8,128)(2,1)S(1)} %collective-permute-done.one.q1) | copy-start | bytes 86020
  11.9 0.6 copy-start.9
  12.5 0.6 copy-start.10
  15.4 7.9 %copy-start.1 = (bf16[16,64,256]{2,1,0:T(8,128)(2,1)S(1)}, bf16[16,64,256]{2,1,0:T(8,128)(2,1)}, u32[]{:S(2)}) copy-start(bf16[16,64,256]{2,1,0:T(8,128)(2,1)} %points.3) | copy-start | bytes 1572868
  15.4 7.9 %copy-start.5 = (bf16[16,16,384]{2,1,0:T(8,128)(2,1)S(1)}, bf16[16,16,384]{2,1,0:T(8,128)(2,1)}, u32[]{:S(2)}) copy-start(bf16[16,16,384]{2,1,0:T(8,128)(2,1)} %get-tuple-element.18.q2.own_q2) | copy-start | bytes 589828
  15.4 4.0 %collective-permute-start.9 = (bf16[80,128]{1,0:T(8,128)(2,1)}, bf16[80,128]{1,0:T(8,128)(2,1)S(1)}, u32[]{:S(2)}, u32[]{:S(2)}) collective-permute-start(bf16[80,128]{1,0:T(8,128)(2,1)} %get-tuple-element.26.mine.refs_0_), channel_id=1, source_target_pairs={{0,4},{4,0},{8,12},{12,8},{16,20},{20,16},{24,28},{28,24},{1,5},{5... | collective-permute-start | bytes 61448 | tf_op jit(solution)/shard_map/ppermute | solution.py:24
  19.4 0.6 copy-start.12
  21.8 4.1 %collective-permute-start.10 = (bf16[80,128]{1,0:T(8,128)(2,1)}, bf16[80,128]{1,0:T(8,128)(2,1)S(1)}, u32[]{:S(2)}, u32[]{:S(2)}) collective-permute-start(bf16[80,128]{1,0:T(8,128)(2,1)} %level1.1.mine.refs_2_), channel_id=1, source_target_pairs={{0,8},{4,12},{8,0},{12,4},{16,24},{20,28},{24,16},{28,20},{1,9},{5... | collective-permute-start | bytes 61448 | tf_op jit(solution)/shard_map/ppermute | solution.py:24
  23.4 18.7 %collective-permute-start.7 = (bf16[16,64,256]{2,1,0:T(8,128)(2,1)S(1)}, bf16[16,64,256]{2,1,0:T(8,128)(2,1)S(1)}, u32[]{:S(2)}, u32[]{:S(2)}) collective-permute-start(bf16[16,64,256]{2,1,0:T(8,128)(2,1)S(1)} %copy-done.1), channel_id=1, source_target_pairs={{0,1},{1,0},{2,3},{3,2},{4,5},{5,4},{6,7},{7,6},{8,9},{9,8},{10,11... | collective-permute-start | bytes 1572872 | tf_op jit(solution)/shard_map/ppermute | solution.py:24
  23.4 18.6 %collective-permute-start.8 = (bf16[16,16,384]{2,1,0:T(8,128)(2,1)S(1)}, bf16[16,16,384]{2,1,0:T(8,128)(2,1)S(1)}, u32[]{:S(2)}, u32[]{:S(2)}) collective-permute-start(bf16[16,16,384]{2,1,0:T(8,128)(2,1)S(1)} %copy-done.5), channel_id=1, source_target_pairs={{0,1},{1,0},{2,3},{3,2},{4,5},{5,4},{6,7},{7,6},{8,9},{9,8},{10,11... | collective-permute-start | bytes 589832 | tf_op jit(solution)/shard_map/ppermute | solution.py:24
  23.9 16.4 %collective-permute-start.5 = (bf16[16,16,384]{2,1,0:T(8,128)(2,1)S(1)}, bf16[16,16,384]{2,1,0:T(8,128)(2,1)S(1)}, u32[]{:S(2)}, u32[]{:S(2)}) collective-permute-start(bf16[16,16,384]{2,1,0:T(8,128)(2,1)S(1)} %copy-done.5), channel_id=1, source_target_pairs={{0,2},{1,3},{2,0},{3,1},{4,6},{5,7},{6,4},{7,5},{8,10},{9,11},{10,... | collective-permute-start | bytes 589832 | tf_op jit(solution)/shard_map/ppermute | solution.py:24
  24.4 17.5 %collective-permute-start.3 = (bf16[16,64,256]{2,1,0:T(8,128)(2,1)S(1)}, bf16[16,64,256]{2,1,0:T(8,128)(2,1)S(1)}, u32[]{:S(2)}, u32[]{:S(2)}) collective-permute-start(bf16[16,64,256]{2,1,0:T(8,128)(2,1)S(1)} %copy-done.1), channel_id=1, source_target_pairs={{0,2},{1,3},{2,0},{3,1},{4,6},{5,7},{6,4},{7,5},{8,10},{9,11},{10,... | collective-permute-start | bytes 1572872 | tf_op jit(solution)/shard_map/ppermute | solution.py:24
  25.9 0.6 copy-start.13
  28.2 8.6 %collective-permute-start.11 = (bf16[80,128]{1,0:T(8,128)(2,1)}, bf16[80,128]{1,0:T(8,128)(2,1)S(1)}, u32[]{:S(2)}, u32[]{:S(2)}) collective-permute-start(bf16[80,128]{1,0:T(8,128)(2,1)} %level2.1.refs_4_), channel_id=1, source_target_pairs={{0,16},{4,20},{8,24},{12,28},{16,0},{20,4},{24,8},{28,12},{1,17},{... | collective-permute-start | bytes 61448 | tf_op jit(solution)/shard_map/ppermute | solution.py:24
  36.8 0.6 copy-start.14
  40.3 16.5 %copy-start.6 = (bf16[16,16,384]{2,1,0:T(8,128)(2,1)}, bf16[16,16,384]{2,1,0:T(8,128)(2,1)S(1)}, u32[]{:S(2)}) copy-start(bf16[16,16,384]{2,1,0:T(8,128)(2,1)S(1)} %collective-permute-done.5.q2_two) | copy-start | bytes 589828
  40.3 16.5 %collective-permute-start.6 = (bf16[16,16,384]{2,1,0:T(8,128)(2,1)S(1)}, bf16[16,16,384]{2,1,0:T(8,128)(2,1)S(1)}, u32[]{:S(2)}, u32[]{:S(2)}) collective-permute-start(bf16[16,16,384]{2,1,0:T(8,128)(2,1)S(1)} %collective-permute-done.5.q2_two), channel_id=1, source_target_pairs={{0,1},{1,0},{2,3},{3,2},{4,5},{5,4},{6,7},{7,6},{8,9},{9,8},{10,11... | collective-permute-start | bytes 589832 | tf_op jit(solution)/shard_map/ppermute | solution.py:24
  42.0 14.8 %copy-start.2 = (bf16[16,64,256]{2,1,0:T(8,128)(2,1)}, bf16[16,64,256]{2,1,0:T(8,128)(2,1)S(1)}, u32[]{:S(2)}) copy-start(bf16[16,64,256]{2,1,0:T(8,128)(2,1)S(1)} %collective-permute-done.3.points_two) | copy-start | bytes 1572868
  42.0 14.9 %collective-permute-start.4 = (bf16[16,64,256]{2,1,0:T(8,128)(2,1)S(1)}, bf16[16,64,256]{2,1,0:T(8,128)(2,1)S(1)}, u32[]{:S(2)}, u32[]{:S(2)}) collective-permute-start(bf16[16,64,256]{2,1,0:T(8,128)(2,1)S(1)} %collective-permute-done.3.points_two), channel_id=1, source_target_pairs={{0,1},{1,0},{2,3},{3,2},{4,5},{5,4},{6,7},{7,6},{8,9},{9,8},{10,11... | collective-permute-start | bytes 1572872 | tf_op jit(solution)/shard_map/ppermute | solution.py:24
  42.0 0.7 copy-start.7
  42.0 0.9 %copy-start.3 = (bf16[16,64,256]{2,1,0:T(8,128)(2,1)}, bf16[16,64,256]{2,1,0:T(8,128)(2,1)S(1)}, u32[]{:S(2)}) copy-start(bf16[16,64,256]{2,1,0:T(8,128)(2,1)S(1)} %collective-permute-done.7.points) | copy-start | bytes 1572868
  56.8 0.7 copy-start.8
  56.9 0.9 %copy-start.4 = (bf16[16,64,256]{2,1,0:T(8,128)(2,1)}, bf16[16,64,256]{2,1,0:T(8,128)(2,1)S(1)}, u32[]{:S(2)}) copy-start(bf16[16,64,256]{2,1,0:T(8,128)(2,1)S(1)} %collective-permute-done.4.points_three) | copy-start | bytes 1572868

commit v2 on v1

v2 whole, which is shorter than its diff:
```python
import functools

import jax
import jax.numpy as jnp
from jax import lax
from jax.experimental import pallas as pl
from jax.experimental.pallas import tpu as pltpu
from jax.sharding import PartitionSpec as P


BF16 = jnp.bfloat16
F32 = jnp.float32
AUG = 16
NEAR_STEP = 16
FAR_STEP = 32
LIST_ROWS = 16
VMEM = pl.BlockSpec(memory_space=pltpu.VMEM)
SMEM = pl.BlockSpec(memory_space=pltpu.SMEM)
ANY = pl.BlockSpec(memory_space=pl.ANY)
VMEM_LIMIT = 24 << 20
TOKEN = (8, 128)


def flipped(block, axis, bits):
    count = lax.axis_size(axis)
    return lax.ppermute(block, axis, [(low, low ^ bits) for low in range(count)])


def dot(left, right, left_dim, right_dim):
    return lax.dot_general(
        left, right, (((left_dim,), (right_dim,)), ((), ())), preferred_element_type=F32
    )


def one_hot(columns, rows, start=0):
    spots = lax.broadcasted_iota(jnp.int32, (rows, columns.shape[1]), 0) + start
    return jnp.where(spots == columns, 1.0, 0.0).astype(BF16)


def norm_parts(coords):
    wide = coords.astype(F32)
    norm = jnp.sum(wide * wide, axis=0, keepdims=True) * (-1.0 / coords.shape[0])
    high = norm.astype(BF16).astype(F32)
    rest = norm - high
    middle = rest.astype(BF16).astype(F32)
    return high, middle, rest - middle


def aug_rows(parts, width, norm_first):
    row = lax.broadcasted_iota(jnp.int32, (AUG, width), 0)
    start, ones = (0, 3) if norm_first else (3, 0)
    block = jnp.where((row >= ones) & (row < ones + 3), 1.0, 0.0)
    for index, part in enumerate(parts):
        block = jnp.where(row == start + index, part, block)
    return block.astype(BF16)


def with_norms(coords, norm_first):
    rows = aug_rows(norm_parts(coords), coords.shape[1], norm_first)
    scaled = (coords.astype(F32) * (2.0 / coords.shape[0])).astype(BF16) if norm_first else coords
    return jnp.concatenate([scaled, rows], axis=0)


def tile(left, right, left_dim, right_dim):
    return jnp.exp(dot(left, right, left_dim, right_dim)).astype(BF16)


def list_rows(pairs, row, width):
    pick = lax.broadcasted_iota(jnp.int32, (8, 2), 0) == lax.broadcasted_iota(
        jnp.int32, (8, 2), 1
    ) + row
    spread = jnp.where(pick, 1.0, 0.0).astype(BF16)
    rows = dot(spread, pairs.astype(F32).astype(BF16), 1, 0)
    short = width - pairs.shape[1]
    return jnp.concatenate([rows, jnp.zeros((8, short), F32)], axis=1) if short else rows


def prep_kernel(
    points, bits, leaf_skel, leaf_basis, dev_skel, dev_basis, near, near_count, far, q1, q2
):
    leaves, features, size = points.shape
    probes = bits.shape[1]
    skeleton = leaf_skel.shape[1]
    node_weights = jnp.zeros((probes, skeleton), F32)
    node_coords = jnp.zeros((features, skeleton), F32)
    for leaf in range(leaves):
        span = slice(leaf * skeleton, (leaf + 1) * skeleton)
        signs = (2 * bits[leaf] - 1).astype(F32).astype(BF16)
        q2[leaf, :, :size] = signs
        weights = dot(signs, leaf_basis[leaf], 1, 1).astype(BF16)
        q2[leaf, :, size:] = weights
        node_weights += dot(weights, dev_basis[0, :, span], 1, 1)
        coords = dot(points[leaf], one_hot(leaf_skel[leaf : leaf + 1, :], size), 1, 0).astype(BF16)
        node_coords += dot(coords, one_hot(dev_skel[...], skeleton, leaf * skeleton), 1, 0)
    q1[:features] = node_coords.astype(BF16)
    q1[features : features + probes] = node_weights.astype(BF16)
    lists = list_rows(near[0], 0, skeleton) + list_rows(far[0], 2, skeleton)
    row = lax.broadcasted_iota(jnp.int32, lists.shape, 0)
    lists = jnp.where(row == 4, near_count[0].astype(F32), lists)
    base = features + probes
    q1[base : base + LIST_ROWS] = jnp.concatenate([lists, jnp.zeros_like(lists)], 0).astype(BF16)
    q1[base + LIST_ROWS :] = leaf_skel[...].astype(F32).astype(BF16)


def own_kernel(points, leaf_skel, q2, lhs_t, lhs_c, rhs, rhs_c, sw, near, token):
    leaves, features, size = points.shape
    for leaf in range(leaves):
        left = with_norms(points[leaf], True)
        right = with_norms(points[leaf], False)
        both = dot(
            jnp.concatenate([left, right], 0), one_hot(leaf_skel[leaf : leaf + 1, :], size), 1, 0
        )
        rhs[leaf] = right
        lhs_t[leaf] = left.T
        lhs_c[leaf] = both[: features + AUG].T.astype(BF16)
        rhs_c[leaf] = both[features + AUG :].astype(BF16)
        sw[leaf] = q2[leaf]
    for leaf in range(leaves):
        block = tile(lhs_t[leaf], rhs[leaf], 1, 0)
        near[leaf] = dot(q2[leaf, :, :size], block, 1, 1)
    token[...] = jnp.zeros_like(token)


def node_kernel(
    features, probes, cap, far_cap, mine, one, two, three, basis, skel, token, node, lists, q1
):
    skeleton = mine.shape[1]
    leaves = mine.shape[0] - features - probes - LIST_ROWS
    shift = leaves.bit_length() - 1
    groups = 4
    me = lax.axis_index("sub")
    for rel, ref in enumerate((mine, one, two, three)):
        q1[rel] = ref[...]
    weights = jnp.zeros((probes, skeleton), F32)
    coords = jnp.zeros((features, skeleton), F32)
    for spot in range(groups):
        block = q1[jnp.bitwise_xor(me, spot)]
        span = slice(spot * skeleton, (spot + 1) * skeleton)
        weights += dot(block[features : features + probes], basis[0, :, span], 1, 1)
        coords += dot(block[:features], one_hot(skel[...], skeleton, spot * skeleton), 1, 0)
    node[:features] = coords.astype(BF16)
    node[features:] = weights.astype(BF16)

    base = features + probes
    lane = lax.broadcasted_iota(jnp.int32, (1, skeleton), 1)
    rows = [q1[rel, base : base + LIST_ROWS].astype(F32) for rel in range(groups)]
    whole = [block.astype(jnp.int32) for block in rows]
    segments = []
    for kind, limit in ((0, cap), (2, far_cap)):
        for rel in (None, 0, 1, 2, 3):
            block = whole[0 if rel is None else rel]
            first = block[kind : kind + 1]
            second = block[kind + 1 : kind + 2]
            used = lane < (block[4:5] if kind == 0 else limit)
            owner = second >> shift
            inner = second & (leaves - 1)
            if rel is not None:
                line = 0 if kind == 0 else 1 + (rel >> 1)
                segments.append((line, inner, rel * leaves + first, used & (owner == me)))
                continue
            apart = jnp.bitwise_xor(owner, me)
            slot = apart * leaves + inner
            if kind == 0:
                segments.append((0, first, slot, used))
            else:
                segments.append((1, first, slot, used & (apart < 2)))
                segments.append((2, first, slot, used & (apart >= 2)))
    masks = jnp.concatenate([jnp.where(part[3], 1.0, 0.0) for part in segments], 0)
    masks = jnp.concatenate([masks, jnp.zeros((-len(segments) % 16, skeleton), F32)], 0)
    before = lax.broadcasted_iota(jnp.int32, (skeleton, skeleton), 0) < lax.broadcasted_iota(
        jnp.int32, (skeleton, skeleton), 1
    )
    prefix = dot(masks.astype(BF16), jnp.where(before, 1.0, 0.0).astype(BF16), 1, 0)
    totals = jnp.sum(masks, axis=1, keepdims=True)
    width = lists.shape[1]
    for line in range(3):
        offset = jnp.zeros((1, 1), F32)
        result = jnp.zeros((8, width), F32)
        for index, part in enumerate(segments):
            if part[0] != line:
                continue
            place = jnp.where(part[3], prefix[index : index + 1] + offset, -1.0)
            offset += totals[index : index + 1]
            spots = lax.broadcasted_iota(jnp.int32, (width, skeleton), 0)
            hot = jnp.where(spots == place.astype(jnp.int32), 1.0, 0.0).astype(BF16)
            values = jnp.concatenate(
                [part[1].astype(F32), part[2].astype(F32), jnp.zeros((6, skeleton), F32)], 0
            ).astype(BF16)
            result += dot(values, hot, 1, 1)
        lists[2 * line : 2 * line + 2] = result[:2].astype(jnp.int32)
        lists[8 + line : 9 + line] = jnp.broadcast_to(offset, (1, width)).astype(jnp.int32)
    lists[6:8] = jnp.zeros((2, width), jnp.int32)
    lists[11:] = jnp.zeros((5, width), jnp.int32)


def build(rel, points, q1, q2, rhs, rhs_c, sw):
    leaves, _, size = points.shape
    base = rel * leaves
    skels = q1[q1.shape[0] - leaves :].astype(F32).astype(jnp.int32)
    for leaf in range(leaves):
        right = with_norms(points[leaf], False)
        rhs[base + leaf] = right
        rhs_c[base + leaf] = dot(right, one_hot(skels[leaf : leaf + 1], size), 1, 0).astype(BF16)
        sw[base + leaf] = q2[leaf]


def level_kernel(features, height, mine, other, basis, skel, after, node, pair):
    skeleton = mine.shape[1]
    on_right = (lax.axis_index("leaf") >> (height - 1)) & 1
    pair[0] = mine[...]
    pair[1] = other[...]
    left = pair[on_right]
    right = pair[1 - on_right]
    line = skel[0, height - 1 : height, :]
    weights = dot(left[features:], basis[0, height - 1, :, :skeleton], 1, 1)
    weights += dot(right[features:], basis[0, height - 1, :, skeleton:], 1, 1)
    coords = dot(left[:features], one_hot(line, skeleton), 1, 0)
    coords += dot(right[:features], one_hot(line, skeleton, skeleton), 1, 0)
    node[:features] = coords.astype(BF16)
    node[features:] = weights.astype(BF16)


def far_sums(line, size, lists, lhs_c, rhs_c, sw, far):
    skeleton = rhs_c.shape[2]
    count = lists[8 + line, 0]

    def step_of(step, carry):
        results = []
        for index in range(0, FAR_STEP, 2):
            spots = [step * FAR_STEP + index + half for half in range(2)]
            owns = [lists[2 * line, spot] for spot in spots]
            slots = [lists[2 * line + 1, spot] for spot in spots]
            blocks = [tile(lhs_c[own], rhs_c[slot], 1, 0) for own, slot in zip(owns, slots)]
            weights = jnp.concatenate([sw[slot, :, size:] for slot in slots], 0)
            part = dot(weights, jnp.concatenate(blocks, 0), 1, 1)
            probes = part.shape[0] // 2
            for half in range(2):
                rows = slice(half * probes, (half + 1) * probes)
                mine = part[rows, half * skeleton : (half + 1) * skeleton]
                mine = mine.astype(BF16).astype(F32)
                results.append((owns[half], jnp.where(spots[half] < count, mine, 0.0)))
        for own, part in results:
            far[own] += part
        return carry

    lax.fori_loop(0, (count + FAR_STEP - 1) // FAR_STEP, step_of, 0)


def near_sums(size, lists, lhs_t, rhs, sw, near):
    count = lists[8, 0]

    def step_of(step, carry):
        results = []
        for index in range(NEAR_STEP):
            spot = step * NEAR_STEP + index
            own, slot = lists[0, spot], lists[1, spot]
            block = tile(lhs_t[own], rhs[slot], 1, 0)
            part = dot(sw[slot, :, :size], block, 1, 1)
            results.append((own, jnp.where(spot < count, part, 0.0)))
        for own, part in results:
            near[own] += part
        return carry

    lax.fori_loop(0, (count + NEAR_STEP - 1) // NEAR_STEP, step_of, 0)


def first_kernel(points, q1, q2, lists, lhs_c, _, __, ___, rhs, rhs_c, sw, far):
    build(1, points, q1, q2, rhs, rhs_c, sw)
    far[...] = jnp.zeros_like(far)
    far_sums(1, points.shape[2], lists, lhs_c, rhs_c, sw, far)


def second_kernel(points, q1, q2, after, _, __, ___, rhs, rhs_c, sw, token):
    build(2, points, q1, q2, rhs, rhs_c, sw)
    token[...] = jnp.zeros_like(token)


def third_kernel(points, q1, q2, lists, lhs_c, after, _, __, ___, ____, rhs, rhs_c, sw, far):
    build(3, points, q1, q2, rhs, rhs_c, sw)
    far_sums(2, points.shape[2], lists, lhs_c, rhs_c, sw, far)


def last_kernel(features, levels, *refs):
    nodes, refs = refs[: 2 * levels], refs[2 * levels :]
    upper_basis, subtree_basis, dev_basis, leaf_basis, lists, lhs_t, rhs, sw, far, near, out = refs
    leaves, probes, size = out.shape
    skeleton = nodes[0].shape[1]
    me = lax.axis_index("sub")
    subtree = lax.axis_index("leaf")
    tree = []
    for level in range(levels):
        mine, other = nodes[2 * level], nodes[2 * level + 1]
        block = tile(
            with_norms(mine[:features], True), with_norms(other[:features], False), 0, 0
        )
        tree.append(dot(other[features:], block, 1, 1))
    potential = tree[levels - 1]
    for height in range(levels - 1, 0, -1):
        side = pl.multiple_of(((subtree >> (height - 1)) & 1) * skeleton, skeleton)
        part = upper_basis[0, height - 1, :, pl.ds(side, skeleton)]
        potential = tree[height - 1] + dot(potential.astype(BF16), part, 1, 0)
    spot = pl.multiple_of(me * skeleton, skeleton)
    device = dot(potential.astype(BF16), subtree_basis[0, :, pl.ds(spot, skeleton)], 1, 0)
    spread = dot(device.astype(BF16), dev_basis[0], 1, 0).astype(BF16)
    for leaf in range(leaves):
        total = spread[:, leaf * skeleton : (leaf + 1) * skeleton].astype(F32) + far[leaf]
        high = total.astype(BF16)
        low = (total - high.astype(F32)).astype(BF16)
        part = dot(jnp.concatenate([high, low], 0), leaf_basis[leaf], 1, 0)
        out[leaf] = near[leaf] + part[:probes] + part[probes:]
    near_sums(size, lists, lhs_t, rhs, sw, out)


def call(kernel, out_shape, in_specs, micros, *args, scratch=(), aliases=()):
    return pl.pallas_call(
        kernel,
        out_shape=out_shape,
        in_specs=in_specs,
        out_specs=jax.tree.map(lambda _: VMEM, out_shape),
        scratch_shapes=scratch,
        input_output_aliases=dict(aliases),
        compiler_params=pltpu.CompilerParams(vmem_limit_bytes=VMEM_LIMIT),
        cost_estimate=pl.CostEstimate(
            flops=int(micros * 1e9), bytes_accessed=int(micros * 1e6), transcendentals=0
        ),
    )(*args)


def on_device(
    points,
    probe_bits,
    leaf_skel,
    leaf_basis,
    device_skel,
    device_basis,
    subtree_skel,
    subtree_basis,
    upper_skel,
    upper_basis,
    near_pairs,
    near_count,
    far_pairs,
):
    leaves, features, size = points.shape
    probes = probe_bits.shape[1]
    skeleton = leaf_skel.shape[1]
    levels = lax.axis_size("leaf").bit_length() - 1
    cap = near_pairs.shape[1]
    far_cap = far_pairs.shape[1]
    depth = features + AUG
    width = max(-(-5 * cap // 128), -(-3 * far_cap // 128)) * 128
    q1_rows = features + probes + LIST_ROWS + leaves
    slots = 4 * leaves
    shape = jax.ShapeDtypeStruct
    rhs_shape = shape((slots, depth, size), BF16)
    rhs_c_shape = shape((slots, depth, skeleton), BF16)
    sw_shape = shape((slots, probes, size + skeleton), BF16)
    near_shape = shape((leaves, probes, size), F32)
    far_shape = shape((leaves, probes, skeleton), F32)
    node_shape = shape((features + probes, skeleton), BF16)
    token_shape = shape(TOKEN, F32)

    q1, q2 = call(
        prep_kernel,
        (shape((q1_rows, skeleton), BF16), shape((leaves, probes, size + skeleton), BF16)),
        [VMEM] * 7 + [SMEM, VMEM],
        4,
        points,
        probe_bits,
        leaf_skel,
        leaf_basis,
        device_skel,
        device_basis,
        jnp.swapaxes(near_pairs, 1, 2),
        near_count,
        jnp.swapaxes(far_pairs, 1, 2),
    )
    q1_one, q1_two, q1_three = (
        flipped(q1, "sub", bits) for bits in (1, 2, 3)
    )
    q2_two = flipped(q2, "sub", 2)
    points_two = flipped(points, "sub", 2)
    q2_one = flipped(q2, "sub", 1)
    points_one = flipped(points, "sub", 1)

    lhs_t, lhs_c, rhs, rhs_c, sw, near, token = call(
        own_kernel,
        (
            shape((leaves, size, depth), BF16),
            shape((leaves, skeleton, depth), BF16),
            rhs_shape,
            rhs_c_shape,
            sw_shape,
            near_shape,
            token_shape,
        ),
        [VMEM] * 3,
        5,
        points,
        leaf_skel,
        q2,
    )
    node, lists = call(
        functools.partial(node_kernel, features, probes, cap, far_cap),
        (node_shape, shape((16, width), jnp.int32)),
        [VMEM] * 6 + [ANY],
        2,
        q1,
        q1_one,
        q1_two,
        q1_three,
        subtree_basis,
        subtree_skel,
        token,
        scratch=[pltpu.VMEM((4, q1_rows, skeleton), BF16)],
    )
    nodes = []
    far = after = None
    for height in range(1, levels + 1):
        other = flipped(node, "leaf", 1 << (height - 1))
        nodes += [node, other]
        if height == 1:
            rhs, rhs_c, sw, far = call(
                first_kernel,
                (rhs_shape, rhs_c_shape, sw_shape, far_shape),
                [VMEM] * 3 + [SMEM, VMEM] + [ANY] * 3,
                5,
                points_one,
                q1_one,
                q2_one,
                lists,
                lhs_c,
                rhs,
                rhs_c,
                sw,
                aliases=((5, 0), (6, 1), (7, 2)),
            )
            after = far
        if height == 2:
            points_three = flipped(points_two, "sub", 1)
            q2_three = flipped(q2_two, "sub", 1)
            rhs, rhs_c, sw, after = call(
                second_kernel,
                (rhs_shape, rhs_c_shape, sw_shape, token_shape),
                [VMEM] * 3 + [ANY] * 4,
                2,
                points_two,
                q1_two,
                q2_two,
                node,
                rhs,
                rhs_c,
                sw,
                aliases=((4, 0), (5, 1), (6, 2)),
            )
        if height == 3:
            rhs, rhs_c, sw, far = call(
                third_kernel,
                (rhs_shape, rhs_c_shape, sw_shape, far_shape),
                [VMEM] * 3 + [SMEM, VMEM] + [ANY] * 4 + [VMEM],
                5,
                points_three,
                q1_three,
                q2_three,
                lists,
                lhs_c,
                node,
                rhs,
                rhs_c,
                sw,
                far,
                aliases=((6, 0), (7, 1), (8, 2), (9, 3)),
            )
            after = far
        if height < levels:
            node = call(
                functools.partial(level_kernel, features, height),
                node_shape,
                [VMEM] * 4 + [ANY],
                1,
                node,
                other,
                upper_basis,
                upper_skel,
                after,
                scratch=[pltpu.VMEM((2, features + probes, skeleton), BF16)],
            )

    return call(
        functools.partial(last_kernel, features, levels),
        near_shape,
        [VMEM] * (2 * levels + 4) + [SMEM] + [VMEM] * 5,
        10,
        *nodes,
        upper_basis,
        subtree_basis,
        device_basis,
        leaf_basis,
        lists,
        lhs_t,
        rhs,
        sw,
        far,
        near,
    )


def solution(mesh):
    return jax.shard_map(
        on_device,
        mesh=mesh,
        in_specs=(
            P(("leaf", "sub"), None, None),
            P(("leaf", "sub"), None, None),
            P(("leaf", "sub"), None),
            P(("leaf", "sub"), None, None),
            P(("leaf", "sub"), None),
            P(("leaf", "sub"), None, None),
            P("leaf", None),
            P("leaf", None, None),
            P("leaf", None, None),
            P("leaf", None, None, None),
            P(("leaf", "sub"), None, None),
            P(("leaf", "sub")),
            P(("leaf", "sub"), None, None),
        ),
        out_specs=P(("leaf", "sub"), None, None),
        check_vma=False,
    )
```

time: 71.4 us -> 59.7 us (0.84)
  Pallas kernels: 46.7 us -> 32.4 us
  waiting for transfers between devices: 7.74 us -> 13 us
  starting transfers between devices: 9.02 us -> 7.18 us
  local copies, waits for them, and re-layouts: 6.92 us -> 5.95 us
    pallas_call x8 -> x9, Pallas kernels: 46.7 us -> 32.4 us  [call(): pl.pallas_call(kernel, out_shape=out_shape, in_specs=in_specs, out_specs=...]
    ppermute x12, waiting for transfers between devices: 7.74 us -> 13 us  [flipped(): lax.ppermute(block, axis, [(low, low ^ bits) for low in range(count)])]
    ppermute x12, starting transfers between devices: 9.02 us -> 7.18 us  [flipped(): lax.ppermute(block, axis, [(low, low ^ bits) for low in range(count)])]
    unnamed x32 -> x28, local copies, waits for them, and re-layouts: 6.92 us -> 5.95 us
  transfers between devices with their start and end apart: 12 -> 12, of which waited for: 3 -> 3; matrix products, arithmetic and copies ran while one was open for 0% -> 0% of each run, Pallas kernels for 34% -> 28%
where the time goes in v2:
time: 59.7 us; the launch traced here: 59.4 us
  Pallas kernels  32.4 us (54%)
  waiting for transfers between devices  13 us (22%)
  starting transfers between devices  7.18 us (12%)
  local copies, waits for them, and re-layouts  5.95 us (10%)
  between operations  0.8 us (1%)
    pallas_call x9, Pallas kernels, call(): pl.pallas_call(kernel, out_shape=out_shape, in_specs=in_specs, out_specs=...  32.4 us
    ppermute x12, waiting for transfers between devices, flipped(): lax.ppermute(block, axis, [(low, low ^ bits) for low in range(count)])  13 us
    ppermute x12, starting transfers between devices, flipped(): lax.ppermute(block, axis, [(low, low ^ bits) for low in range(count)])  7.18 us
    unnamed x28, local copies, waits for them, and re-layouts  5.95 us
  transfers between devices with their start and end apart: 12, of which 3 were waited for; matrix products, arithmetic and copies ran while one was open for 0% of the time, Pallas kernels for 28%

profile of v2, /device:TPU:6, one launch (start us, length us, event | category | flops | bytes accessed | tf_op | source)
XLA Modules:
  0.0 59.4 jit_solution(2074177378249352386)
XLA Ops:
  0.7 0.0 copy-start
  0.7 1.2 %copy-done = bf16[16,128,256]{2,1,0:T(8,128)(2,1)S(1)} copy-done((bf16[16,128,256]{2,1,0:T(8,128)(2,1)S(1)}, bf16[16,128,256]{2,1,0:T(8,128)(2,1)}, u32[]{:S(2)}) %copy-start) | copy-done | bytes 1048600
  1.9 1.0 %copy-done.2 = bf16[1,128,2048]{2,1,0:T(8,128)(2,1)S(1)} copy-done((bf16[1,128,2048]{2,1,0:T(8,128)(2,1)S(1)}, bf16[1,128,2048]{2,1,0:T(8,128)(2,1)}, u32[]{:S(2)}) %copy-start.2) | copy-done | bytes 524312
  2.9 0.9 %copy-done.4 = s32[16,16,256]{2,1,0:T(8,128)S(1)} copy-done((s32[16,16,256]{2,1,0:T(8,128)S(1)}, s32[16,16,256]{2,1,0:T(8,128)}, u32[]{:S(2)}) %copy-start.4) | copy-done | bytes 262168
  3.9 0.7 %copy-done.7 = s32[16,128]{1,0:T(8,128)S(1)} copy-done((s32[16,128]{1,0:T(8,128)S(1)}, s32[16,128]{1,0:T(8,128)}, u32[]{:S(2)}) %copy-start.7) | copy-done | bytes 8216
  4.6 0.7 %copy-done.9 = s32[1,80,2]{1,2,0:T(2,128)S(1)} copy-done((s32[1,80,2]{1,2,0:T(2,128)S(1)}, s32[1,80,2]{1,2,0:T(2,128)}, u32[]{:S(2)}) %copy-start.9) | copy-done | bytes 664
  5.3 0.7 %copy-done.10 = s32[1,96,2]{1,2,0:T(2,128)S(1)} copy-done((s32[1,96,2]{1,2,0:T(2,128)S(1)}, s32[1,96,2]{1,2,0:T(2,128)}, u32[]{:S(2)}) %copy-start.10) | copy-done | bytes 792
  5.9 0.7 %copy-done.12 = s32[1,128]{1,0:T(1,128)S(1)} copy-done((s32[1,128]{1,0:T(1,128)S(1)}, s32[1,128]{1,0:T(1,128)}, u32[]{:S(2)}) %copy-start.12) | copy-done | bytes 536
  6.6 3.5 %shard_map.127 = (bf16[112,128]{1,0:T(8,128)(2,1)S(1)}, bf16[16,16,384]{2,1,0:T(8,128)(2,1)S(1)}) custom-call(bf16[16,64,256]{2,1,0:T(8,128)(2,1)} %points.3, s32[16,16,256]{2,1,0:T(8,128)S(1)} %copy-done.4, s32[16,128]{1,0:T(8,128)S(1)} %copy-done.7, bf16[16,128,256]{2,1,0:T(8,128)(2,1)S(1)} %copy-done, s32[1,128]{1,0:T(1,128)S(1)} %copy-done.12, ...), custom_call_target="tpu_custom_call" | custom-call | flops 4000000000 | bytes 4000000 | tf_op jit(solution)/shard_map/pallas_call | solution.py:315
  10.1 0.1 collective-permute-start
  10.2 0.6 %collective-permute-start.1 = (bf16[112,128]{1,0:T(8,128)(2,1)S(1)}, bf16[112,128]{1,0:T(8,128)(2,1)S(1)}, u32[]{:S(2)}, u32[]{:S(2)}) collective-permute-start(bf16[112,128]{1,0:T(8,128)(2,1)S(1)} %get-tuple-element.27.mine), channel_id=1, source_target_pairs={{0,2},{1,3},{2,0},{3,1},{4,6},{5,7},{6,4},{7,5},{8,10},{9,11},{10,... | collective-permute-start | bytes 86024 | tf_op jit(solution)/shard_map/ppermute | solution.py:26
  10.8 1.2 %collective-permute-start.2 = (bf16[112,128]{1,0:T(8,128)(2,1)S(1)}, bf16[112,128]{1,0:T(8,128)(2,1)S(1)}, u32[]{:S(2)}, u32[]{:S(2)}) collective-permute-start(bf16[112,128]{1,0:T(8,128)(2,1)S(1)} %get-tuple-element.27.mine), channel_id=1, source_target_pairs={{0,3},{1,2},{2,1},{3,0},{4,7},{5,6},{6,5},{7,4},{8,11},{9,10},{10,... | collective-permute-start | bytes 86024 | tf_op jit(solution)/shard_map/ppermute | solution.py:26
  12.1 0.4 collective-permute-start.4
  12.4 0.2 collective-permute-start.5
  12.6 0.0 collective-permute-done.one.q1
  12.6 0.5 collective-permute-start.8
  13.1 1.3 %collective-permute-done.1.two.q1 = bf16[112,128]{1,0:T(8,128)(2,1)S(1)} collective-permute-done((bf16[112,128]{1,0:T(8,128)(2,1)S(1)}, bf16[112,128]{1,0:T(8,128)(2,1)S(1)}, u32[]{:S(2)}, u32[]{:S(2)}) %collective-permute-start.1) | collective-permute-done | bytes 28704 | tf_op jit(solution)/shard_map/ppermute | solution.py:26
  14.4 0.3 collective-permute-start.7
  14.7 0.0 copy-done.8
  14.7 5.0 %shard_map.128 = (bf16[16,256,80]{2,1,0:T(8,128)(2,1)S(1)}, bf16[16,128,80]{2,1,0:T(8,128)(2,1)S(1)}, bf16[64,80,256]{2,1,0:T(8,128)(2,1)S(1)}, bf16[64,80,128]{...) custom-call(bf16[16,64,256]{2,1,0:T(8,128)(2,1)} %points.3, ...), custom_call_target="tpu_custom_call" | custom-call | flops 5000000000 | bytes 5000000 | tf_op jit(solution)/shard_map/pallas_call | solution.py:315
  19.7 0.0 collective-permute-done.2.three.q1
  19.7 0.0 copy-done.5
  19.8 0.8 %shard_map.129 = (bf16[80,128]{1,0:T(8,128)(2,1)S(1)}, s32[16,512]{1,0:T(8,128)S(1)}) custom-call(bf16[112,128]{1,0:T(8,128)(2,1)S(1)} %get-tuple-element.27.mine, bf16[112,128]{1,0:T(8,128)(2,1)S(1)} %collective-permute-done.one.q1, bf16[112,128]{1,0:T(8,128)(2,1)S(1)} %collective-permute-done.1.two.q1, ...), custom_call_target="tpu_custom_call" | custom-call | flops 2000000000 | bytes 2000000 | tf_op jit(solution)/shard_map/pallas_call | solution.py:315
  20.5 0.5 collective-permute-start.3
  21.0 0.0 collective-permute-done.8.q2
  21.0 0.0 collective-permute-start.11
  21.0 10.0 %collective-permute-done.7.points = bf16[16,64,256]{2,1,0:T(8,128)(2,1)S(1)} collective-permute-done((bf16[16,64,256]{2,1,0:T(8,128)(2,1)}, bf16[16,64,256]{2,1,0:T(8,128)(2,1)S(1)}, u32[]{:S(2)}, u32[]{:S(2)}) %collective-permute-start.7) | collective-permute-done | bytes 524320 | tf_op jit(solution)/shard_map/ppermute | solution.py:26
  31.0 0.0 collective-permute-start.10
  31.0 0.0 collective-permute-done.5.q2
  31.0 0.0 collective-permute-done.4.points
  31.0 0.0 copy-start.6
  31.0 0.0 copy-start.11
  31.0 4.9 %shard_map.130 = (bf16[64,80,256]{2,1,0:T(8,128)(2,1)S(1)}, bf16[64,80,128]{2,1,0:T(8,128)(2,1)S(1)}, bf16[64,16,384]{2,1,0:T(8,128)(2,1)S(1)}, f32[16,16,128]{2,1,0:T(8,128)S(1)}) custom-call(bf16[16,64,256]{2,1,0:T(8,128)(2,1)S(1)} %collective-permute-done.4.points, ...), custom_call_target="tpu_custom_call", output_to_operand_aliasing={{0}: (5, {}), {1}: (6, {}), {2}: (7, {})} | custom-call | flops 5000000000 | bytes 5000000 | tf_op jit(solution)/shard_map/pallas_call | solution.py:315
  36.0 0.0 collective-permute-done.3.other.refs_1_
  36.0 0.0 copy-done.6
  36.0 0.0 copy-done.11
  36.0 0.2 shard_map.131.after.mine.refs_2_
  36.2 1.6 %collective-permute-start.6 = (bf16[80,128]{1,0:T(8,128)(2,1)S(1)}, bf16[80,128]{1,0:T(8,128)(2,1)S(1)}, u32[]{:S(2)}, u32[]{:S(2)}) collective-permute-start(bf16[80,128]{1,0:T(8,128)(2,1)S(1)} %shard_map.131.after.mine.refs_2_), channel_id=1, source_target_pairs={{0,8},{4,12},{8,0},{12,4},{16,24},{20,28},{24,16},{28,20},{1,9},{5... | collective-permute-start | bytes 61448 | tf_op jit(solution)/shard_map/ppermute | solution.py:26
  37.8 0.5 shard_map.132
  38.3 1.7 %collective-permute-done.6.other.refs_3_ = bf16[80,128]{1,0:T(8,128)(2,1)S(1)} collective-permute-done((bf16[80,128]{1,0:T(8,128)(2,1)S(1)}, bf16[80,128]{1,0:T(8,128)(2,1)S(1)}, u32[]{:S(2)}, u32[]{:S(2)}) %collective-permute-start.6) | collective-permute-done | bytes 20512 | tf_op jit(solution)/shard_map/ppermute | solution.py:26
  40.0 0.2 shard_map.133.after.refs_4_
  40.2 1.8 %collective-permute-start.9 = (bf16[80,128]{1,0:T(8,128)(2,1)S(1)}, bf16[80,128]{1,0:T(8,128)(2,1)S(1)}, u32[]{:S(2)}, u32[]{:S(2)}) collective-permute-start(bf16[80,128]{1,0:T(8,128)(2,1)S(1)} %shard_map.133.after.refs_4_), channel_id=1, source_target_pairs={{0,16},{4,20},{8,24},{12,28},{16,0},{20,4},{24,8},{28,12},{1,17},{... | collective-permute-start | bytes 61448 | tf_op jit(solution)/shard_map/ppermute | solution.py:26
  42.0 0.0 collective-permute-done.11.q2
  42.0 0.0 collective-permute-done.10.points
  42.0 0.0 copy-start.3
  42.0 4.9 %shard_map.134 = (bf16[64,80,256]{2,1,0:T(8,128)(2,1)S(1)}, bf16[64,80,128]{2,1,0:T(8,128)(2,1)S(1)}, bf16[64,16,384]{2,1,0:T(8,128)(2,1)S(1)}, f32[16,16,128]{2,1,0:T(8,128)S(1)}) custom-call(bf16[16,64,256]{2,1,0:T(8,128)(2,1)S(1)} %collective-permute-done.10.points, ...), custom_call_target="tpu_custom_call", output_to_operand_aliasing={{0}: (6, {}), {1}: (7, {}), {2}: (8, {}), {3}: (9, {})} | custom-call | flops 5000000000 | bytes 5000000 | tf_op jit(solution)/shard_map/pallas_call | solution.py:315
  46.9 0.0 collective-permute-done.9.refs_5_
  47.0 12.4 %shard_map.135 = f32[16,16,256]{2,1,0:T(8,128)} custom-call(bf16[80,128]{1,0:T(8,128)(2,1)S(1)} %get-tuple-element.30.mine.refs_0_, bf16[80,128]{1,0:T(8,128)(2,1)S(1)} %collective-permute-done.3.other.refs_1_, bf16[80,128]{1,0:T(8,128)(2,1)S(1)} %shard_map.131.after.mine.refs_2_, bf16[80,128]{1,0:T(8,128)(2,1)S(1)} %collective-permute-done.6.other.refs_3_, ...), custom_call_target="tpu_custom_call" | custom-call | flops 10000000000 | bytes 10000000 | tf_op jit(solution)/shard_map/pallas_call | solution.py:315
  (13 shorter events, 0.0 us)
Async XLA Ops:
  0.7 1.2 %copy-start = (bf16[16,128,256]{2,1,0:T(8,128)(2,1)S(1)}, bf16[16,128,256]{2,1,0:T(8,128)(2,1)}, u32[]{:S(2)}) copy-start(bf16[16,128,256]{2,1,0:T(8,128)(2,1)} %refs_9_.1) | copy-start | bytes 3145732
  1.9 1.0 %copy-start.2 = (bf16[1,128,2048]{2,1,0:T(8,128)(2,1)S(1)}, bf16[1,128,2048]{2,1,0:T(8,128)(2,1)}, u32[]{:S(2)}) copy-start(bf16[1,128,2048]{2,1,0:T(8,128)(2,1)} %refs_8_.1) | copy-start | bytes 1572868
  2.9 0.9 %copy-start.4 = (s32[16,16,256]{2,1,0:T(8,128)S(1)}, s32[16,16,256]{2,1,0:T(8,128)}, u32[]{:S(2)}) copy-start(s32[16,16,256]{2,1,0:T(8,128)} %bits.1) | copy-start | bytes 786436
  3.9 0.7 %copy-start.7 = (s32[16,128]{1,0:T(8,128)S(1)}, s32[16,128]{1,0:T(8,128)}, u32[]{:S(2)}) copy-start(s32[16,128]{1,0:T(8,128)} %leaf_skel.3) | copy-start | bytes 24580
  4.6 0.7 %copy-start.9 = (s32[1,80,2]{1,2,0:T(2,128)S(1)}, s32[1,80,2]{1,2,0:T(2,128)}, u32[]{:S(2)}) copy-start(s32[1,80,2]{1,2,0:T(2,128)} %param.23) | copy-start | bytes 1924
  5.2 0.7 %copy-start.10 = (s32[1,96,2]{1,2,0:T(2,128)S(1)}, s32[1,96,2]{1,2,0:T(2,128)}, u32[]{:S(2)}) copy-start(s32[1,96,2]{1,2,0:T(2,128)} %param.25) | copy-start | bytes 2308
  5.9 0.7 %copy-start.12 = (s32[1,128]{1,0:T(1,128)S(1)}, s32[1,128]{1,0:T(1,128)}, u32[]{:S(2)}) copy-start(s32[1,128]{1,0:T(1,128)} %dev_skel.1) | copy-start | bytes 1540
  6.6 8.1 %copy-start.8 = (s32[16,128]{1,0:T(8,128)S(1)}, s32[16,128]{1,0:T(8,128)}, u32[]{:S(2)}) copy-start(s32[16,128]{1,0:T(8,128)} %leaf_skel.3) | copy-start | bytes 24580
  10.1 2.4 %collective-permute-start = (bf16[112,128]{1,0:T(8,128)(2,1)S(1)}, bf16[112,128]{1,0:T(8,128)(2,1)S(1)}, u32[]{:S(2)}, u32[]{:S(2)}) collective-permute-start(bf16[112,128]{1,0:T(8,128)(2,1)S(1)} %get-tuple-element.27.mine), channel_id=1, source_target_pairs={{0,1},{1,0},{2,3},{3,2},{4,5},{5,4},{6,7},{7,6},{8,9},{9,8},{10,11... | collective-permute-start | bytes 86024 | tf_op jit(solution)/shard_map/ppermute | solution.py:26
  10.2 4.2 %collective-permute-start.1 = (bf16[112,128]{1,0:T(8,128)(2,1)S(1)}, bf16[112,128]{1,0:T(8,128)(2,1)S(1)}, u32[]{:S(2)}, u32[]{:S(2)}) collective-permute-start(bf16[112,128]{1,0:T(8,128)(2,1)S(1)} %get-tuple-element.27.mine), channel_id=1, source_target_pairs={{0,2},{1,3},{2,0},{3,1},{4,6},{5,7},{6,4},{7,5},{8,10},{9,11},{10,... | collective-permute-start | bytes 86024 | tf_op jit(solution)/shard_map/ppermute | solution.py:26
  10.8 8.9 %collective-permute-start.2 = (bf16[112,128]{1,0:T(8,128)(2,1)S(1)}, bf16[112,128]{1,0:T(8,128)(2,1)S(1)}, u32[]{:S(2)}, u32[]{:S(2)}) collective-permute-start(bf16[112,128]{1,0:T(8,128)(2,1)S(1)} %get-tuple-element.27.mine), channel_id=1, source_target_pairs={{0,3},{1,2},{2,1},{3,0},{4,7},{5,6},{6,5},{7,4},{8,11},{9,10},{10,... | collective-permute-start | bytes 86024 | tf_op jit(solution)/shard_map/ppermute | solution.py:26
  12.1 18.9 %collective-permute-start.4 = (bf16[16,64,256]{2,1,0:T(8,128)(2,1)}, bf16[16,64,256]{2,1,0:T(8,128)(2,1)S(1)}, u32[]{:S(2)}, u32[]{:S(2)}) collective-permute-start(bf16[16,64,256]{2,1,0:T(8,128)(2,1)} %points.3), channel_id=1, source_target_pairs={{0,1},{1,0},{2,3},{3,2},{4,5},{5,4},{6,7},{7,6},{8,9},{9,8},{10,11... | collective-permute-start | bytes 1572872 | tf_op jit(solution)/shard_map/ppermute | solution.py:26
  12.4 7.3 %copy-start.5 = (bf16[1,128,512]{2,1,0:T(8,128)(2,1)S(1)}, bf16[1,128,512]{2,1,0:T(8,128)(2,1)}, u32[]{:S(2)}) copy-start(bf16[1,128,512]{2,1,0:T(8,128)(2,1)} %refs_7_.1) | copy-start | bytes 393220
  12.4 7.3 %copy-start.13 = (s32[1,128]{1,0:T(1,128)S(1)}, s32[1,128]{1,0:T(1,128)}, u32[]{:S(2)}) copy-start(s32[1,128]{1,0:T(1,128)} %skel.3) | copy-start | bytes 1540
  12.4 18.6 %collective-permute-start.5 = (bf16[16,16,384]{2,1,0:T(8,128)(2,1)S(1)}, bf16[16,16,384]{2,1,0:T(8,128)(2,1)S(1)}, u32[]{:S(2)}, u32[]{:S(2)}) collective-permute-start(bf16[16,16,384]{2,1,0:T(8,128)(2,1)S(1)} %get-tuple-element.28.q2), channel_id=1, source_target_pairs={{0,1},{1,0},{2,3},{3,2},{4,5},{5,4},{6,7},{7,6},{8,9},{9,8},{10,11... | collective-permute-start | bytes 589832 | tf_op jit(solution)/shard_map/ppermute | solution.py:26
  12.6 8.4 %collective-permute-start.8 = (bf16[16,16,384]{2,1,0:T(8,128)(2,1)S(1)}, bf16[16,16,384]{2,1,0:T(8,128)(2,1)S(1)}, u32[]{:S(2)}, u32[]{:S(2)}) collective-permute-start(bf16[16,16,384]{2,1,0:T(8,128)(2,1)S(1)} %get-tuple-element.28.q2), channel_id=1, source_target_pairs={{0,2},{1,3},{2,0},{3,1},{4,6},{5,7},{6,4},{7,5},{8,10},{9,11},{10,... | collective-permute-start | bytes 589832 | tf_op jit(solution)/shard_map/ppermute | solution.py:26
  14.4 16.6 %collective-permute-start.7 = (bf16[16,64,256]{2,1,0:T(8,128)(2,1)}, bf16[16,64,256]{2,1,0:T(8,128)(2,1)S(1)}, u32[]{:S(2)}, u32[]{:S(2)}) collective-permute-start(bf16[16,64,256]{2,1,0:T(8,128)(2,1)} %points.3), channel_id=1, source_target_pairs={{0,2},{1,3},{2,0},{3,1},{4,6},{5,7},{6,4},{7,5},{8,10},{9,11},{10,... | collective-permute-start | bytes 1572872 | tf_op jit(solution)/shard_map/ppermute | solution.py:26
  20.5 15.4 %collective-permute-start.3 = (bf16[80,128]{1,0:T(8,128)(2,1)S(1)}, bf16[80,128]{1,0:T(8,128)(2,1)S(1)}, u32[]{:S(2)}, u32[]{:S(2)}) collective-permute-start(bf16[80,128]{1,0:T(8,128)(2,1)S(1)} %get-tuple-element.30.mine.refs_0_), channel_id=1, source_target_pairs={{0,4},{4,0},{8,12},{12,8},{16,20},{20,16},{24,28},{28,24},{1,5},{5... | collective-permute-start | bytes 61448 | tf_op jit(solution)/shard_map/ppermute | solution.py:26
  21.0 21.0 %collective-permute-start.11 = (bf16[16,16,384]{2,1,0:T(8,128)(2,1)S(1)}, bf16[16,16,384]{2,1,0:T(8,128)(2,1)S(1)}, u32[]{:S(2)}, u32[]{:S(2)}) collective-permute-start(bf16[16,16,384]{2,1,0:T(8,128)(2,1)S(1)} %collective-permute-done.8.q2), channel_id=1, source_target_pairs={{0,1},{1,0},{2,3},{3,2},{4,5},{5,4},{6,7},{7,6},{8,9},{9,8},{10,11... | collective-permute-start | bytes 589832 | tf_op jit(solution)/shard_map/ppermute | solution.py:26
  31.0 11.0 %collective-permute-start.10 = (bf16[16,64,256]{2,1,0:T(8,128)(2,1)S(1)}, bf16[16,64,256]{2,1,0:T(8,128)(2,1)S(1)}, u32[]{:S(2)}, u32[]{:S(2)}) collective-permute-start(bf16[16,64,256]{2,1,0:T(8,128)(2,1)S(1)} %collective-permute-done.7.points), channel_id=1, source_target_pairs={{0,1},{1,0},{2,3},{3,2},{4,5},{5,4},{6,7},{7,6},{8,9},{9,8},{10,11... | collective-permute-start | bytes 1572872 | tf_op jit(solution)/shard_map/ppermute | solution.py:26
  31.0 5.0 %copy-start.6 = (bf16[1,2,128,256]{3,2,1,0:T(8,128)(2,1)S(1)}, bf16[1,2,128,256]{3,2,1,0:T(8,128)(2,1)}, u32[]{:S(2)}) copy-start(bf16[1,2,128,256]{3,2,1,0:T(8,128)(2,1)} %refs_6_.1) | copy-start | bytes 393220
  31.0 5.0 %copy-start.11 = (s32[1,2,128]{2,1,0:T(2,128)S(1)}, s32[1,2,128]{2,1,0:T(2,128)}, u32[]{:S(2)}) copy-start(s32[1,2,128]{2,1,0:T(2,128)} %skel.5) | copy-start | bytes 3076
  36.2 3.8 %collective-permute-start.6 = (bf16[80,128]{1,0:T(8,128)(2,1)S(1)}, bf16[80,128]{1,0:T(8,128)(2,1)S(1)}, u32[]{:S(2)}, u32[]{:S(2)}) collective-permute-start(bf16[80,128]{1,0:T(8,128)(2,1)S(1)} %shard_map.131.after.mine.refs_2_), channel_id=1, source_target_pairs={{0,8},{4,12},{8,0},{12,4},{16,24},{20,28},{24,16},{28,20},{1,9},{5... | collective-permute-start | bytes 61448 | tf_op jit(solution)/shard_map/ppermute | solution.py:26
  40.2 6.8 %collective-permute-start.9 = (bf16[80,128]{1,0:T(8,128)(2,1)S(1)}, bf16[80,128]{1,0:T(8,128)(2,1)S(1)}, u32[]{:S(2)}, u32[]{:S(2)}) collective-permute-start(bf16[80,128]{1,0:T(8,128)(2,1)S(1)} %shard_map.133.after.refs_4_), channel_id=1, source_target_pairs={{0,16},{4,20},{8,24},{12,28},{16,0},{20,4},{24,8},{28,12},{1,17},{... | collective-permute-start | bytes 61448 | tf_op jit(solution)/shard_map/ppermute | solution.py:26
  42.0 5.0 %copy-start.1 = (bf16[16,128,256]{2,1,0:T(8,128)(2,1)S(1)}, bf16[16,128,256]{2,1,0:T(8,128)(2,1)}, u32[]{:S(2)}) copy-start(bf16[16,128,256]{2,1,0:T(8,128)(2,1)} %refs_9_.1) | copy-start | bytes 3145732
  42.0 5.0 %copy-start.3 = (bf16[1,128,2048]{2,1,0:T(8,128)(2,1)S(1)}, bf16[1,128,2048]{2,1,0:T(8,128)(2,1)}, u32[]{:S(2)}) copy-start(bf16[1,128,2048]{2,1,0:T(8,128)(2,1)} %refs_8_.1) | copy-start | bytes 1572868

commit v3 on v2

--- a/solution.py
+++ b/solution.py
@@ -12,11 +12,14 @@
 F32 = jnp.float32
 AUG = 16
 NEAR_STEP = 16
+OWN_STEP = 8
+CHUNKS = 4
 FAR_STEP = 32
 LIST_ROWS = 16
 VMEM = pl.BlockSpec(memory_space=pltpu.VMEM)
 SMEM = pl.BlockSpec(memory_space=pltpu.SMEM)
 ANY = pl.BlockSpec(memory_space=pl.ANY)
+HBM = pl.BlockSpec(memory_space=pltpu.HBM)
 VMEM_LIMIT = 24 << 20
 TOKEN = (8, 128)
 
@@ -76,24 +79,72 @@
 
 
 def prep_kernel(
-    points, bits, leaf_skel, leaf_basis, dev_skel, dev_basis, near, near_count, far, q1, q2
+    points_in, bits_in, skel_in, basis_in, dev_skel_in, dev_basis_in, near_in, near_count, far_in,
+    q1, q2, points, bits, leaf_skel, leaf_basis, dev_skel, dev_basis, near, far, sems,
 ):
     leaves, features, size = points.shape
     probes = bits.shape[1]
     skeleton = leaf_skel.shape[1]
-    node_weights = jnp.zeros((probes, skeleton), F32)
-    node_coords = jnp.zeros((features, skeleton), F32)
-    for leaf in range(leaves):
-        span = slice(leaf * skeleton, (leaf + 1) * skeleton)
-        signs = (2 * bits[leaf] - 1).astype(F32).astype(BF16)
-        q2[leaf, :, :size] = signs
-        weights = dot(signs, leaf_basis[leaf], 1, 1).astype(BF16)
-        q2[leaf, :, size:] = weights
-        node_weights += dot(weights, dev_basis[0, :, span], 1, 1)
-        coords = dot(points[leaf], one_hot(leaf_skel[leaf : leaf + 1, :], size), 1, 0).astype(BF16)
-        node_coords += dot(coords, one_hot(dev_skel[...], skeleton, leaf * skeleton), 1, 0)
-    q1[:features] = node_coords.astype(BF16)
-    q1[features : features + probes] = node_weights.astype(BF16)
+    small = [
+        pltpu.make_async_copy(source, target, sems.at[index])
+        for index, (source, target) in enumerate(
+            ((skel_in, leaf_skel), (dev_skel_in, dev_skel), (near_in, near), (far_in, far))
+        )
+    ]
+    chunk = leaves // CHUNKS
+    large = []
+    for index in range(CHUNKS):
+        rows = pl.ds(index * chunk, chunk)
+        columns = pl.ds(index * chunk * skeleton, chunk * skeleton)
+        base = 4 + 4 * index
+        large.append(
+            [
+                pltpu.make_async_copy(points_in.at[rows], points.at[rows], sems.at[base]),
+                pltpu.make_async_copy(bits_in.at[rows], bits.at[rows], sems.at[base + 1]),
+                pltpu.make_async_copy(basis_in.at[rows], leaf_basis.at[rows], sems.at[base + 2]),
+                pltpu.make_async_copy(
+                    dev_basis_in.at[0, :, columns], dev_basis.at[:, columns], sems.at[base + 3]
+                ),
+            ]
+        )
+    for copy in small + [copy for group in large for copy in group]:
+        copy.start()
+    for copy in small:
+        copy.wait()
+    names = jnp.concatenate(
+        [leaf_skel[...].astype(F32), jnp.broadcast_to(dev_skel[...].astype(F32), (8, skeleton))], 0
+    ).T
+    lane = lax.broadcasted_iota(jnp.int32, (skeleton, size), 1).astype(F32)
+    total = jnp.zeros((features + probes, size), F32)
+    for first in range(0, leaves, 2):
+        if first % chunk == 0:
+            for copy in large[first // chunk]:
+                copy.wait()
+        coords, weights = [], []
+        for leaf in (first, first + 1):
+            signs = (2 * bits[leaf] - 1).astype(F32).astype(BF16)
+            hot = jnp.where(lane == names[:, leaf : leaf + 1], 1.0, 0.0).astype(BF16)
+            both = dot(
+                jnp.concatenate([points[leaf], signs], 0),
+                jnp.concatenate([hot, leaf_basis[leaf]], 0),
+                1,
+                1,
+            ).astype(BF16)
+            coords.append(both[:features, :skeleton])
+            weights.append(both[features:, skeleton:])
+            q2[leaf, :, :size] = signs
+            q2[leaf, :, size:] = weights[-1]
+        spots = lane + float(first * skeleton)
+        hot = jnp.where(spots == names[:, leaves : leaves + 1], 1.0, 0.0).astype(BF16)
+        columns = slice(first * skeleton, (first + 2) * skeleton)
+        total += dot(
+            jnp.concatenate([jnp.concatenate(coords, 1), jnp.concatenate(weights, 1)], 0),
+            jnp.concatenate([hot, dev_basis[:, columns]], 0),
+            1,
+            1,
+        )
+    q1[:features] = total[:features, :skeleton].astype(BF16)
+    q1[features : features + probes] = total[features:, skeleton:].astype(BF16)
     lists = list_rows(near[0], 0, skeleton) + list_rows(far[0], 2, skeleton)
     row = lax.broadcasted_iota(jnp.int32, lists.shape, 0)
     lists = jnp.where(row == 4, near_count[0].astype(F32), lists)
@@ -109,15 +160,21 @@
         right = with_norms(points[leaf], False)
         both = dot(
             jnp.concatenate([left, right], 0), one_hot(leaf_skel[leaf : leaf + 1, :], size), 1, 0
-        )
+        ).astype(BF16)
         rhs[leaf] = right
         lhs_t[leaf] = left.T
-        lhs_c[leaf] = both[: features + AUG].T.astype(BF16)
-        rhs_c[leaf] = both[features + AUG :].astype(BF16)
+        lhs_c[leaf] = both[: features + AUG].T
+        rhs_c[leaf] = both[features + AUG :]
         sw[leaf] = q2[leaf]
-    for leaf in range(leaves):
-        block = tile(lhs_t[leaf], rhs[leaf], 1, 0)
-        near[leaf] = dot(q2[leaf, :, :size], block, 1, 1)
+
+    def step_of(step, carry):
+        for index in range(OWN_STEP):
+            leaf = step * OWN_STEP + index
+            block = tile(lhs_t[leaf], rhs[leaf], 1, 0)
+            near[leaf] = dot(q2[leaf, :, :size], block, 1, 1)
+        return carry
+
+    lax.fori_loop(0, leaves // OWN_STEP, step_of, 0)
     token[...] = jnp.zeros_like(token)
 
 
@@ -155,7 +212,7 @@
             owner = second >> shift
             inner = second & (leaves - 1)
             if rel is not None:
-                line = 0 if kind == 0 else 1 + (rel >> 1)
+                line = 0 if kind == 0 else max(rel, 1)
                 segments.append((line, inner, rel * leaves + first, used & (owner == me)))
                 continue
             apart = jnp.bitwise_xor(owner, me)
@@ -164,7 +221,8 @@
                 segments.append((0, first, slot, used))
             else:
                 segments.append((1, first, slot, used & (apart < 2)))
-                segments.append((2, first, slot, used & (apart >= 2)))
+                segments.append((2, first, slot, used & (apart == 2)))
+                segments.append((3, first, slot, used & (apart == 3)))
     masks = jnp.concatenate([jnp.where(part[3], 1.0, 0.0) for part in segments], 0)
     masks = jnp.concatenate([masks, jnp.zeros((-len(segments) % 16, skeleton), F32)], 0)
     before = lax.broadcasted_iota(jnp.int32, (skeleton, skeleton), 0) < lax.broadcasted_iota(
@@ -173,7 +231,7 @@
     prefix = dot(masks.astype(BF16), jnp.where(before, 1.0, 0.0).astype(BF16), 1, 0)
     totals = jnp.sum(masks, axis=1, keepdims=True)
     width = lists.shape[1]
-    for line in range(3):
+    for line in range(4):
         offset = jnp.zeros((1, 1), F32)
         result = jnp.zeros((8, width), F32)
         for index, part in enumerate(segments):
@@ -189,12 +247,12 @@
             result += dot(values, hot, 1, 1)
         lists[2 * line : 2 * line + 2] = result[:2].astype(jnp.int32)
         lists[8 + line : 9 + line] = jnp.broadcast_to(offset, (1, width)).astype(jnp.int32)
-    lists[6:8] = jnp.zeros((2, width), jnp.int32)
-    lists[11:] = jnp.zeros((5, width), jnp.int32)
+    lists[12:] = jnp.zeros((4, width), jnp.int32)
 
 
 def build(rel, points, q1, q2, rhs, rhs_c, sw):
-    leaves, _, size = points.shape
+    leaves = q2.shape[0]
+    size = points.shape[2]
     base = rel * leaves
     skels = q1[q1.shape[0] - leaves :].astype(F32).astype(jnp.int32)
     for leaf in range(leaves):
@@ -224,10 +282,10 @@
     skeleton = rhs_c.shape[2]
     count = lists[8 + line, 0]
 
-    def step_of(step, carry):
+    def some(start, many):
         results = []
-        for index in range(0, FAR_STEP, 2):
-            spots = [step * FAR_STEP + index + half for half in range(2)]
+        for index in range(0, many, 2):
+            spots = [start + index + half for half in range(2)]
             owns = [lists[2 * line, spot] for spot in spots]
             slots = [lists[2 * line + 1, spot] for spot in spots]
             blocks = [tile(lhs_c[own], rhs_c[slot], 1, 0) for own, slot in zip(owns, slots)]
@@ -241,27 +299,40 @@
                 results.append((owns[half], jnp.where(spots[half] < count, mine, 0.0)))
         for own, part in results:
             far[own] += part
-        return carry
-
-    lax.fori_loop(0, (count + FAR_STEP - 1) // FAR_STEP, step_of, 0)
+
+    stepped(count, FAR_STEP, some)
 
 
 def near_sums(size, lists, lhs_t, rhs, sw, near):
     count = lists[8, 0]
 
-    def step_of(step, carry):
+    def some(start, many):
         results = []
-        for index in range(NEAR_STEP):
-            spot = step * NEAR_STEP + index
+        for index in range(many):
+            spot = start + index
             own, slot = lists[0, spot], lists[1, spot]
             block = tile(lhs_t[own], rhs[slot], 1, 0)
             part = dot(sw[slot, :, :size], block, 1, 1)
             results.append((own, jnp.where(spot < count, part, 0.0)))
         for own, part in results:
             near[own] += part
+
+    stepped(count, NEAR_STEP, some)
+
+
+def stepped(count, many, some):
+    half = many // 2
+    whole = (count + half - 1) // many
+
+    def step_of(step, carry):
+        some(step * many, many)
         return carry
 
-    lax.fori_loop(0, (count + NEAR_STEP - 1) // NEAR_STEP, step_of, 0)
+    lax.fori_loop(0, whole, step_of, 0)
+
+    @pl.when(count > whole * many)
+    def _():
+        some(whole * many, half)
 
 
 def first_kernel(points, q1, q2, lists, lhs_c, _, __, ___, rhs, rhs_c, sw, far):
@@ -270,14 +341,12 @@
     far_sums(1, points.shape[2], lists, lhs_c, rhs_c, sw, far)
 
 
-def second_kernel(points, q1, q2, after, _, __, ___, rhs, rhs_c, sw, token):
-    build(2, points, q1, q2, rhs, rhs_c, sw)
-    token[...] = jnp.zeros_like(token)
-
-
-def third_kernel(points, q1, q2, lists, lhs_c, after, _, __, ___, ____, rhs, rhs_c, sw, far):
-    build(3, points, q1, q2, rhs, rhs_c, sw)
-    far_sums(2, points.shape[2], lists, lhs_c, rhs_c, sw, far)
+def other_kernel(
+    rel, points, q1, q2, lists, lhs_c, after, _, __, ___, ____,
+    rhs, rhs_c, sw, far,
+):
+    build(rel, points, q1, q2, rhs, rhs_c, sw)
+    far_sums(rel, rhs.shape[2], lists, lhs_c, rhs_c, sw, far)
 
 
 def last_kernel(features, levels, *refs):
@@ -324,6 +393,10 @@
             flops=int(micros * 1e9), bytes_accessed=int(micros * 1e6), transcendentals=0
         ),
     )(*args)
+
+
+def placed(*arrays):
+    return [pltpu.with_memory_space_constraint(array, pltpu.HBM) for array in arrays]
 
 
 def on_device(
@@ -363,17 +436,23 @@
     q1, q2 = call(
         prep_kernel,
         (shape((q1_rows, skeleton), BF16), shape((leaves, probes, size + skeleton), BF16)),
-        [VMEM] * 7 + [SMEM, VMEM],
+        [HBM] * 7 + [SMEM, HBM],
         4,
-        points,
-        probe_bits,
-        leaf_skel,
-        leaf_basis,
-        device_skel,
-        device_basis,
-        jnp.swapaxes(near_pairs, 1, 2),
+        *placed(points, probe_bits, leaf_skel, leaf_basis, device_skel, device_basis),
+        *placed(jnp.swapaxes(near_pairs, 1, 2)),
         near_count,
-        jnp.swapaxes(far_pairs, 1, 2),
+        *placed(jnp.swapaxes(far_pairs, 1, 2)),
+        scratch=[
+            pltpu.VMEM(points.shape, BF16),
+            pltpu.VMEM(probe_bits.shape, jnp.int32),
+            pltpu.VMEM(leaf_skel.shape, jnp.int32),
+            pltpu.VMEM(leaf_basis.shape, BF16),
+            pltpu.VMEM(device_skel.shape, jnp.int32),
+            pltpu.VMEM(device_basis.shape[1:], BF16),
+            pltpu.VMEM((1, 2, cap), jnp.int32),
+            pltpu.VMEM((1, 2, far_cap), jnp.int32),
+            pltpu.SemaphoreType.DMA((4 + 4 * CHUNKS,)),
+        ],
     )
     q1_one, q1_two, q1_three = (
         flipped(q1, "sub", bits) for bits in (1, 2, 3)
@@ -436,42 +515,6 @@
                 aliases=((5, 0), (6, 1), (7, 2)),
             )
             after = far
-        if height == 2:
-            points_three = flipped(points_two, "sub", 1)
-            q2_three = flipped(q2_two, "sub", 1)
-            rhs, rhs_c, sw, after = call(
-                second_kernel,
-                (rhs_shape, rhs_c_shape, sw_shape, token_shape),
-                [VMEM] * 3 + [ANY] * 4,
-                2,
-                points_two,
-                q1_two,
-                q2_two,
-                node,
-                rhs,
-                rhs_c,
-                sw,
-                aliases=((4, 0), (5, 1), (6, 2)),
-            )
-        if height == 3:
-            rhs, rhs_c, sw, far = call(
-                third_kernel,
-                (rhs_shape, rhs_c_shape, sw_shape, far_shape),
-                [VMEM] * 3 + [SMEM, VMEM] + [ANY] * 4 + [VMEM],
-                5,
-                points_three,
-                q1_three,
-                q2_three,
-                lists,
-                lhs_c,
-                node,
-                rhs,
-                rhs_c,
-                sw,
-                far,
-                aliases=((6, 0), (7, 1), (8, 2), (9, 3)),
-            )
-            after = far
         if height < levels:
             node = call(
                 functools.partial(level_kernel, features, height),
@@ -485,6 +528,27 @@
                 after,
                 scratch=[pltpu.VMEM((2, features + probes, skeleton), BF16)],
             )
+
+    points_three = flipped(points_two, "sub", 1)
+    q2_three = flipped(q2_two, "sub", 1)
+    for rel, sources in (
+        (2, (points_two, q1_two, q2_two)), (3, (points_three, q1_three, q2_three))
+    ):
+        rhs, rhs_c, sw, far = call(
+            functools.partial(other_kernel, rel),
+            (rhs_shape, rhs_c_shape, sw_shape, far_shape),
+            [VMEM] * 3 + [SMEM, VMEM] + [ANY] * 4 + [VMEM],
+            3,
+            *sources,
+            lists,
+            lhs_c,
+            node,
+            rhs,
+            rhs_c,
+            sw,
+            far,
+            aliases=((6, 0), (7, 1), (8, 2), (9, 3)),
+        )
 
     return call(
         functools.partial(last_kernel, features, levels),

time: 59.7 us -> 51.8 us (0.87)
  local copies, waits for them, and re-layouts: 5.95 us -> 0.04 us
  Pallas kernels: 32.4 us -> 30.5 us
  waiting for transfers between devices: 13 us -> 11.3 us
  starting transfers between devices: 7.18 us -> 8.62 us
    unnamed x28 -> x16, local copies, waits for them, and re-layouts: 5.95 us -> 0.04 us
    pallas_call x9, Pallas kernels: 32.4 us -> 30.5 us  [call(): pl.pallas_call(kernel, out_shape=out_shape, in_specs=in_specs, out_specs=...]
    ppermute x12, waiting for transfers between devices: 13 us -> 11.3 us  [flipped(): lax.ppermute(block, axis, [(low, low ^ bits) for low in range(count)])]
    ppermute x12, starting transfers between devices: 7.18 us -> 8.62 us  [flipped(): lax.ppermute(block, axis, [(low, low ^ bits) for low in range(count)])]
  transfers between devices with their start and end apart: 12 -> 12, of which waited for: 3 -> 2; matrix products, arithmetic and copies ran while one was open for 0% -> 0% of each run, Pallas kernels for 28% -> 28%
where the time goes in v3:
time: 51.8 us; the launch traced here: 51.4 us
  Pallas kernels  30.5 us (59%)
  waiting for transfers between devices  11.3 us (22%)
  starting transfers between devices  8.62 us (17%)
  between operations  0.84 us (2%)
    pallas_call x9, Pallas kernels, call(): pl.pallas_call(kernel, out_shape=out_shape, in_specs=in_specs, out_specs=...  30.5 us
    ppermute x12, waiting for transfers between devices, flipped(): lax.ppermute(block, axis, [(low, low ^ bits) for low in range(count)])  11.3 us
    ppermute x12, starting transfers between devices, flipped(): lax.ppermute(block, axis, [(low, low ^ bits) for low in range(count)])  8.62 us
  transfers between devices with their start and end apart: 12, of which 2 were waited for; matrix products, arithmetic and copies ran while one was open for 0% of the time, Pallas kernels for 28%

profile of v3, /device:TPU:6, one launch (start us, length us, event | category | flops | bytes accessed | tf_op | source)
XLA Modules:
  0.0 51.4 jit_solution(200452188006125201)
XLA Ops:
  0.7 0.0 copy-start.1
  0.7 0.0 copy-start.5
  0.7 3.6 %shard_map.127 = (bf16[112,128]{1,0:T(8,128)(2,1)S(1)}, bf16[16,16,384]{2,1,0:T(8,128)(2,1)S(1)}) custom-call(bf16[16,64,256]{2,1,0:T(8,128)(2,1)} %points.1, s32[16,16,256]{2,1,0:T(8,128)} %bits_in.1, s32[16,128]{1,0:T(8,128)} %leaf_skel.1, bf16[16,128,256]{2,1,0:T(8,128)(2,1)} %refs_9_.1, s32[1,128]{1,0:T(1,128)} %dev_skel_in.1, ...), custom_call_target="tpu_custom_call" | custom-call | flops 4000000000 | bytes 4000000 | tf_op jit(solution)/shard_map/pallas_call | solution.py:384
  4.3 0.1 collective-permute-start
  4.4 0.6 %collective-permute-start.1 = (bf16[112,128]{1,0:T(8,128)(2,1)S(1)}, bf16[112,128]{1,0:T(8,128)(2,1)S(1)}, u32[]{:S(2)}, u32[]{:S(2)}) collective-permute-start(bf16[112,128]{1,0:T(8,128)(2,1)S(1)} %get-tuple-element.27.mine), channel_id=1, source_target_pairs={{0,2},{1,3},{2,0},{3,1},{4,6},{5,7},{6,4},{7,5},{8,10},{9,11},{10,... | collective-permute-start | bytes 86024 | tf_op jit(solution)/shard_map/ppermute | solution.py:29
  5.0 1.2 %collective-permute-start.2 = (bf16[112,128]{1,0:T(8,128)(2,1)S(1)}, bf16[112,128]{1,0:T(8,128)(2,1)S(1)}, u32[]{:S(2)}, u32[]{:S(2)}) collective-permute-start(bf16[112,128]{1,0:T(8,128)(2,1)S(1)} %get-tuple-element.27.mine), channel_id=1, source_target_pairs={{0,3},{1,2},{2,1},{3,0},{4,7},{5,6},{6,5},{7,4},{8,11},{9,10},{10,... | collective-permute-start | bytes 86024 | tf_op jit(solution)/shard_map/ppermute | solution.py:29
  6.2 0.0 copy-done.1
  6.2 0.4 collective-permute-start.4
  6.6 0.5 %collective-permute-start.8 = (bf16[16,64,256]{2,1,0:T(8,128)(2,1)S(1)}, bf16[16,64,256]{2,1,0:T(8,128)(2,1)S(1)}, u32[]{:S(2)}, u32[]{:S(2)}) collective-permute-start(bf16[16,64,256]{2,1,0:T(8,128)(2,1)S(1)} %copy-done.1), channel_id=1, source_target_pairs={{0,2},{1,3},{2,0},{3,1},{4,6},{5,7},{6,4},{7,5},{8,10},{9,11},{10,... | collective-permute-start | bytes 1572872 | tf_op jit(solution)/shard_map/ppermute | solution.py:29
  7.1 0.0 collective-permute-done.one.q1
  7.1 0.0 copy-start.3
  7.1 0.0 collective-permute-start.5
  7.1 0.0 copy-done.5
  7.1 2.3 %shard_map.128 = (bf16[16,256,80]{2,1,0:T(8,128)(2,1)S(1)}, bf16[16,128,80]{2,1,0:T(8,128)(2,1)S(1)}, bf16[64,80,256]{2,1,0:T(8,128)(2,1)S(1)}, bf16[64,80,128]{...) custom-call(bf16[16,64,256]{2,1,0:T(8,128)(2,1)S(1)} %copy-done.1, ...), custom_call_target="tpu_custom_call" | custom-call | flops 5000000000 | bytes 5000000 | tf_op jit(solution)/shard_map/pallas_call | solution.py:384
  9.5 0.0 collective-permute-done.1.two.q1
  9.5 1.5 %collective-permute-start.10 = (bf16[16,16,384]{2,1,0:T(8,128)(2,1)S(1)}, bf16[16,16,384]{2,1,0:T(8,128)(2,1)S(1)}, u32[]{:S(2)}, u32[]{:S(2)}) collective-permute-start(bf16[16,16,384]{2,1,0:T(8,128)(2,1)S(1)} %get-tuple-element.28.q2), channel_id=1, source_target_pairs={{0,2},{1,3},{2,0},{3,1},{4,6},{5,7},{6,4},{7,5},{8,10},{9,11},{10,... | collective-permute-start | bytes 589832 | tf_op jit(solution)/shard_map/ppermute | solution.py:29
  11.0 0.0 collective-permute-done.2.three.q1
  11.0 0.0 copy-done.3
  11.0 0.0 copy-done.7
  11.0 0.8 %shard_map.129 = (bf16[80,128]{1,0:T(8,128)(2,1)S(1)}, s32[16,512]{1,0:T(8,128)S(1)}) custom-call(bf16[112,128]{1,0:T(8,128)(2,1)S(1)} %get-tuple-element.27.mine, bf16[112,128]{1,0:T(8,128)(2,1)S(1)} %collective-permute-done.one.q1, bf16[112,128]{1,0:T(8,128)(2,1)S(1)} %collective-permute-done.1.two.q1, ...), custom_call_target="tpu_custom_call" | custom-call | flops 2000000000 | bytes 2000000 | tf_op jit(solution)/shard_map/pallas_call | solution.py:384
  11.8 0.6 %collective-permute-start.3 = (bf16[80,128]{1,0:T(8,128)(2,1)S(1)}, bf16[80,128]{1,0:T(8,128)(2,1)S(1)}, u32[]{:S(2)}, u32[]{:S(2)}) collective-permute-start(bf16[80,128]{1,0:T(8,128)(2,1)S(1)} %get-tuple-element.30.mine.refs_0_), channel_id=1, source_target_pairs={{0,4},{4,0},{8,12},{12,8},{16,20},{20,16},{24,28},{28,24},{1,5},{5... | collective-permute-start | bytes 61448 | tf_op jit(solution)/shard_map/ppermute | solution.py:29
  12.3 9.1 %collective-permute-done.8.points = bf16[16,64,256]{2,1,0:T(8,128)(2,1)S(1)} collective-permute-done((bf16[16,64,256]{2,1,0:T(8,128)(2,1)S(1)}, bf16[16,64,256]{2,1,0:T(8,128)(2,1)S(1)}, u32[]{:S(2)}, u32[]{:S(2)}) %collective-permute-start.8) | collective-permute-done | bytes 524320 | tf_op jit(solution)/shard_map/ppermute | solution.py:29
  21.4 0.0 collective-permute-start.9
  21.4 0.0 collective-permute-done.5.q2
  21.4 0.0 collective-permute-done.4.points
  21.4 0.0 copy-start.4
  21.4 0.0 copy-start.6
  21.4 4.6 %shard_map.130 = (bf16[64,80,256]{2,1,0:T(8,128)(2,1)S(1)}, bf16[64,80,128]{2,1,0:T(8,128)(2,1)S(1)}, bf16[64,16,384]{2,1,0:T(8,128)(2,1)S(1)}, f32[16,16,128]{2,1,0:T(8,128)S(1)}) custom-call(bf16[16,64,256]{2,1,0:T(8,128)(2,1)S(1)} %collective-permute-done.4.points, ...), custom_call_target="tpu_custom_call", output_to_operand_aliasing={{0}: (5, {}), {1}: (6, {}), {2}: (7, {})} | custom-call | flops 5000000000 | bytes 5000000 | tf_op jit(solution)/shard_map/pallas_call | solution.py:384
  26.0 0.0 collective-permute-done.3.other.refs_1_
  26.1 0.0 copy-done.4
  26.1 0.0 copy-done.6
  26.1 0.2 shard_map.131.mine.refs_2_
  26.3 1.6 %collective-permute-start.6 = (bf16[80,128]{1,0:T(8,128)(2,1)S(1)}, bf16[80,128]{1,0:T(8,128)(2,1)S(1)}, u32[]{:S(2)}, u32[]{:S(2)}) collective-permute-start(bf16[80,128]{1,0:T(8,128)(2,1)S(1)} %shard_map.131.mine.refs_2_), channel_id=1, source_target_pairs={{0,8},{4,12},{8,0},{12,4},{16,24},{20,28},{24,16},{28,20},{1,9},{5... | collective-permute-start | bytes 61448 | tf_op jit(solution)/shard_map/ppermute | solution.py:29
  27.9 0.0 collective-permute-done.10.q2
  27.9 0.0 collective-permute-start.11
  27.9 2.2 %collective-permute-done.6.other.refs_3_ = bf16[80,128]{1,0:T(8,128)(2,1)S(1)} collective-permute-done((bf16[80,128]{1,0:T(8,128)(2,1)S(1)}, bf16[80,128]{1,0:T(8,128)(2,1)S(1)}, u32[]{:S(2)}, u32[]{:S(2)}) %collective-permute-start.6) | collective-permute-done | bytes 20512 | tf_op jit(solution)/shard_map/ppermute | solution.py:29
  30.1 0.2 shard_map.132.after.refs_4_
  30.3 2.1 %collective-permute-start.7 = (bf16[80,128]{1,0:T(8,128)(2,1)S(1)}, bf16[80,128]{1,0:T(8,128)(2,1)S(1)}, u32[]{:S(2)}, u32[]{:S(2)}) collective-permute-start(bf16[80,128]{1,0:T(8,128)(2,1)S(1)} %shard_map.132.after.refs_4_), channel_id=1, source_target_pairs={{0,16},{4,20},{8,24},{12,28},{16,0},{20,4},{24,8},{28,12},{1,17},{... | collective-permute-start | bytes 61448 | tf_op jit(solution)/shard_map/ppermute | solution.py:29
  32.4 3.2 %shard_map.133 = (bf16[64,80,256]{2,1,0:T(8,128)(2,1)S(1)}, bf16[64,80,128]{2,1,0:T(8,128)(2,1)S(1)}, bf16[64,16,384]{2,1,0:T(8,128)(2,1)S(1)}, f32[16,16,128]{2,1,0:T(8,128)S(1)}) custom-call(bf16[16,64,256]{2,1,0:T(8,128)(2,1)S(1)} %collective-permute-done.8.points, ...), custom_call_target="tpu_custom_call", output_to_operand_aliasing={{0}: (6, {}), {1}: (7, {}), {2}: (8, {}), {3}: (9, {})} | custom-call | flops 3000000000 | bytes 3000000 | tf_op jit(solution)/shard_map/pallas_call | solution.py:384
  35.6 0.0 collective-permute-done.11.q2
  35.6 0.0 collective-permute-done.9.points
  35.7 0.0 copy-start
  35.7 0.0 copy-start.2
  35.7 3.3 %shard_map.134 = (bf16[64,80,256]{2,1,0:T(8,128)(2,1)S(1)}, bf16[64,80,128]{2,1,0:T(8,128)(2,1)S(1)}, bf16[64,16,384]{2,1,0:T(8,128)(2,1)S(1)}, f32[16,16,128]{2,1,0:T(8,128)S(1)}) custom-call(bf16[16,64,256]{2,1,0:T(8,128)(2,1)S(1)} %collective-permute-done.9.points, ...), custom_call_target="tpu_custom_call", output_to_operand_aliasing={{0}: (6, {}), {1}: (7, {}), {2}: (8, {}), {3}: (9, {})} | custom-call | flops 3000000000 | bytes 3000000 | tf_op jit(solution)/shard_map/pallas_call | solution.py:384
  38.9 0.0 collective-permute-done.7.refs_5_
  39.0 0.0 copy-done
  39.0 0.0 copy-done.2
  39.0 12.4 %shard_map.135 = f32[16,16,256]{2,1,0:T(8,128)} custom-call(bf16[80,128]{1,0:T(8,128)(2,1)S(1)} %get-tuple-element.30.mine.refs_0_, bf16[80,128]{1,0:T(8,128)(2,1)S(1)} %collective-permute-done.3.other.refs_1_, bf16[80,128]{1,0:T(8,128)(2,1)S(1)} %shard_map.131.mine.refs_2_, bf16[80,128]{1,0:T(8,128)(2,1)S(1)} %collective-permute-done.6.other.refs_3_, ...), custom_call_target="tpu_custom_call" | custom-call | flops 10000000000 | bytes 10000000 | tf_op jit(solution)/shard_map/pallas_call | solution.py:384
  (1 shorter events, 0.0 us)
Async XLA Ops:
  0.7 5.6 %copy-start.1 = (bf16[16,64,256]{2,1,0:T(8,128)(2,1)S(1)}, bf16[16,64,256]{2,1,0:T(8,128)(2,1)}, u32[]{:S(2)}) copy-start(bf16[16,64,256]{2,1,0:T(8,128)(2,1)} %points.1) | copy-start | bytes 1572868
  0.7 6.5 %copy-start.5 = (s32[16,128]{1,0:T(8,128)S(1)}, s32[16,128]{1,0:T(8,128)}, u32[]{:S(2)}) copy-start(s32[16,128]{1,0:T(8,128)} %leaf_skel.1) | copy-start | bytes 24580
  4.3 2.8 %collective-permute-start = (bf16[112,128]{1,0:T(8,128)(2,1)S(1)}, bf16[112,128]{1,0:T(8,128)(2,1)S(1)}, u32[]{:S(2)}, u32[]{:S(2)}) collective-permute-start(bf16[112,128]{1,0:T(8,128)(2,1)S(1)} %get-tuple-element.27.mine), channel_id=1, source_target_pairs={{0,1},{1,0},{2,3},{3,2},{4,5},{5,4},{6,7},{7,6},{8,9},{9,8},{10,11... | collective-permute-start | bytes 86024 | tf_op jit(solution)/shard_map/ppermute | solution.py:29
  4.4 5.1 %collective-permute-start.1 = (bf16[112,128]{1,0:T(8,128)(2,1)S(1)}, bf16[112,128]{1,0:T(8,128)(2,1)S(1)}, u32[]{:S(2)}, u32[]{:S(2)}) collective-permute-start(bf16[112,128]{1,0:T(8,128)(2,1)S(1)} %get-tuple-element.27.mine), channel_id=1, source_target_pairs={{0,2},{1,3},{2,0},{3,1},{4,6},{5,7},{6,4},{7,5},{8,10},{9,11},{10,... | collective-permute-start | bytes 86024 | tf_op jit(solution)/shard_map/ppermute | solution.py:29
  5.0 6.0 %collective-permute-start.2 = (bf16[112,128]{1,0:T(8,128)(2,1)S(1)}, bf16[112,128]{1,0:T(8,128)(2,1)S(1)}, u32[]{:S(2)}, u32[]{:S(2)}) collective-permute-start(bf16[112,128]{1,0:T(8,128)(2,1)S(1)} %get-tuple-element.27.mine), channel_id=1, source_target_pairs={{0,3},{1,2},{2,1},{3,0},{4,7},{5,6},{6,5},{7,4},{8,11},{9,10},{10,... | collective-permute-start | bytes 86024 | tf_op jit(solution)/shard_map/ppermute | solution.py:29
  6.2 15.2 %collective-permute-start.4 = (bf16[16,64,256]{2,1,0:T(8,128)(2,1)S(1)}, bf16[16,64,256]{2,1,0:T(8,128)(2,1)S(1)}, u32[]{:S(2)}, u32[]{:S(2)}) collective-permute-start(bf16[16,64,256]{2,1,0:T(8,128)(2,1)S(1)} %copy-done.1), channel_id=1, source_target_pairs={{0,1},{1,0},{2,3},{3,2},{4,5},{5,4},{6,7},{7,6},{8,9},{9,8},{10,11... | collective-permute-start | bytes 1572872 | tf_op jit(solution)/shard_map/ppermute | solution.py:29
  6.6 14.8 %collective-permute-start.8 = (bf16[16,64,256]{2,1,0:T(8,128)(2,1)S(1)}, bf16[16,64,256]{2,1,0:T(8,128)(2,1)S(1)}, u32[]{:S(2)}, u32[]{:S(2)}) collective-permute-start(bf16[16,64,256]{2,1,0:T(8,128)(2,1)S(1)} %copy-done.1), channel_id=1, source_target_pairs={{0,2},{1,3},{2,0},{3,1},{4,6},{5,7},{6,4},{7,5},{8,10},{9,11},{10,... | collective-permute-start | bytes 1572872 | tf_op jit(solution)/shard_map/ppermute | solution.py:29
  7.1 3.9 %copy-start.3 = (bf16[1,128,512]{2,1,0:T(8,128)(2,1)S(1)}, bf16[1,128,512]{2,1,0:T(8,128)(2,1)}, u32[]{:S(2)}) copy-start(bf16[1,128,512]{2,1,0:T(8,128)(2,1)} %refs_7_.1) | copy-start | bytes 393220
  7.1 3.9 %copy-start.7 = (s32[1,128]{1,0:T(1,128)S(1)}, s32[1,128]{1,0:T(1,128)}, u32[]{:S(2)}) copy-start(s32[1,128]{1,0:T(1,128)} %skel.3) | copy-start | bytes 1540
  7.1 14.3 %collective-permute-start.5 = (bf16[16,16,384]{2,1,0:T(8,128)(2,1)S(1)}, bf16[16,16,384]{2,1,0:T(8,128)(2,1)S(1)}, u32[]{:S(2)}, u32[]{:S(2)}) collective-permute-start(bf16[16,16,384]{2,1,0:T(8,128)(2,1)S(1)} %get-tuple-element.28.q2), channel_id=1, source_target_pairs={{0,1},{1,0},{2,3},{3,2},{4,5},{5,4},{6,7},{7,6},{8,9},{9,8},{10,11... | collective-permute-start | bytes 589832 | tf_op jit(solution)/shard_map/ppermute | solution.py:29
  9.5 18.4 %collective-permute-start.10 = (bf16[16,16,384]{2,1,0:T(8,128)(2,1)S(1)}, bf16[16,16,384]{2,1,0:T(8,128)(2,1)S(1)}, u32[]{:S(2)}, u32[]{:S(2)}) collective-permute-start(bf16[16,16,384]{2,1,0:T(8,128)(2,1)S(1)} %get-tuple-element.28.q2), channel_id=1, source_target_pairs={{0,2},{1,3},{2,0},{3,1},{4,6},{5,7},{6,4},{7,5},{8,10},{9,11},{10,... | collective-permute-start | bytes 589832 | tf_op jit(solution)/shard_map/ppermute | solution.py:29
  11.8 14.3 %collective-permute-start.3 = (bf16[80,128]{1,0:T(8,128)(2,1)S(1)}, bf16[80,128]{1,0:T(8,128)(2,1)S(1)}, u32[]{:S(2)}, u32[]{:S(2)}) collective-permute-start(bf16[80,128]{1,0:T(8,128)(2,1)S(1)} %get-tuple-element.30.mine.refs_0_), channel_id=1, source_target_pairs={{0,4},{4,0},{8,12},{12,8},{16,20},{20,16},{24,28},{28,24},{1,5},{5... | collective-permute-start | bytes 61448 | tf_op jit(solution)/shard_map/ppermute | solution.py:29
  21.4 14.3 %collective-permute-start.9 = (bf16[16,64,256]{2,1,0:T(8,128)(2,1)S(1)}, bf16[16,64,256]{2,1,0:T(8,128)(2,1)S(1)}, u32[]{:S(2)}, u32[]{:S(2)}) collective-permute-start(bf16[16,64,256]{2,1,0:T(8,128)(2,1)S(1)} %collective-permute-done.8.points), channel_id=1, source_target_pairs={{0,1},{1,0},{2,3},{3,2},{4,5},{5,4},{6,7},{7,6},{8,9},{9,8},{10,11... | collective-permute-start | bytes 1572872 | tf_op jit(solution)/shard_map/ppermute | solution.py:29
  21.4 4.7 %copy-start.4 = (bf16[1,2,128,256]{3,2,1,0:T(8,128)(2,1)S(1)}, bf16[1,2,128,256]{3,2,1,0:T(8,128)(2,1)}, u32[]{:S(2)}) copy-start(bf16[1,2,128,256]{3,2,1,0:T(8,128)(2,1)} %refs_6_.1) | copy-start | bytes 393220
  21.4 4.7 %copy-start.6 = (s32[1,2,128]{2,1,0:T(2,128)S(1)}, s32[1,2,128]{2,1,0:T(2,128)}, u32[]{:S(2)}) copy-start(s32[1,2,128]{2,1,0:T(2,128)} %skel.5) | copy-start | bytes 3076
  26.3 3.8 %collective-permute-start.6 = (bf16[80,128]{1,0:T(8,128)(2,1)S(1)}, bf16[80,128]{1,0:T(8,128)(2,1)S(1)}, u32[]{:S(2)}, u32[]{:S(2)}) collective-permute-start(bf16[80,128]{1,0:T(8,128)(2,1)S(1)} %shard_map.131.mine.refs_2_), channel_id=1, source_target_pairs={{0,8},{4,12},{8,0},{12,4},{16,24},{20,28},{24,16},{28,20},{1,9},{5... | collective-permute-start | bytes 61448 | tf_op jit(solution)/shard_map/ppermute | solution.py:29
  27.9 7.7 %collective-permute-start.11 = (bf16[16,16,384]{2,1,0:T(8,128)(2,1)S(1)}, bf16[16,16,384]{2,1,0:T(8,128)(2,1)S(1)}, u32[]{:S(2)}, u32[]{:S(2)}) collective-permute-start(bf16[16,16,384]{2,1,0:T(8,128)(2,1)S(1)} %collective-permute-done.10.q2), channel_id=1, source_target_pairs={{0,1},{1,0},{2,3},{3,2},{4,5},{5,4},{6,7},{7,6},{8,9},{9,8},{10,11... | collective-permute-start | bytes 589832 | tf_op jit(solution)/shard_map/ppermute | solution.py:29
  30.3 8.7 %collective-permute-start.7 = (bf16[80,128]{1,0:T(8,128)(2,1)S(1)}, bf16[80,128]{1,0:T(8,128)(2,1)S(1)}, u32[]{:S(2)}, u32[]{:S(2)}) collective-permute-start(bf16[80,128]{1,0:T(8,128)(2,1)S(1)} %shard_map.132.after.refs_4_), channel_id=1, source_target_pairs={{0,16},{4,20},{8,24},{12,28},{16,0},{20,4},{24,8},{28,12},{1,17},{... | collective-permute-start | bytes 61448 | tf_op jit(solution)/shard_map/ppermute | solution.py:29
  35.7 3.3 %copy-start = (bf16[16,128,256]{2,1,0:T(8,128)(2,1)S(1)}, bf16[16,128,256]{2,1,0:T(8,128)(2,1)}, u32[]{:S(2)}) copy-start(bf16[16,128,256]{2,1,0:T(8,128)(2,1)} %refs_9_.1) | copy-start | bytes 3145732
  35.7 3.3 %copy-start.2 = (bf16[1,128,2048]{2,1,0:T(8,128)(2,1)S(1)}, bf16[1,128,2048]{2,1,0:T(8,128)(2,1)}, u32[]{:S(2)}) copy-start(bf16[1,128,2048]{2,1,0:T(8,128)(2,1)} %refs_8_.1) | copy-start | bytes 1572868

commit v4 on v3

--- a/solution.py
+++ b/solution.py
@@ -16,6 +16,8 @@
 CHUNKS = 4
 FAR_STEP = 32
 LIST_ROWS = 16
+LINES = 5
+PACK = 256
 VMEM = pl.BlockSpec(memory_space=pltpu.VMEM)
 SMEM = pl.BlockSpec(memory_space=pltpu.SMEM)
 ANY = pl.BlockSpec(memory_space=pl.ANY)
@@ -212,17 +214,18 @@
             owner = second >> shift
             inner = second & (leaves - 1)
             if rel is not None:
-                line = 0 if kind == 0 else max(rel, 1)
+                line = rel >> 1 if kind == 0 else 1 + max(rel, 1)
                 segments.append((line, inner, rel * leaves + first, used & (owner == me)))
                 continue
             apart = jnp.bitwise_xor(owner, me)
             slot = apart * leaves + inner
             if kind == 0:
-                segments.append((0, first, slot, used))
+                segments.append((0, first, slot, used & (apart < 2)))
+                segments.append((1, first, slot, used & (apart >= 2)))
             else:
-                segments.append((1, first, slot, used & (apart < 2)))
-                segments.append((2, first, slot, used & (apart == 2)))
-                segments.append((3, first, slot, used & (apart == 3)))
+                segments.append((2, first, slot, used & (apart < 2)))
+                segments.append((3, first, slot, used & (apart == 2)))
+                segments.append((4, first, slot, used & (apart == 3)))
     masks = jnp.concatenate([jnp.where(part[3], 1.0, 0.0) for part in segments], 0)
     masks = jnp.concatenate([masks, jnp.zeros((-len(segments) % 16, skeleton), F32)], 0)
     before = lax.broadcasted_iota(jnp.int32, (skeleton, skeleton), 0) < lax.broadcasted_iota(
@@ -231,7 +234,8 @@
     prefix = dot(masks.astype(BF16), jnp.where(before, 1.0, 0.0).astype(BF16), 1, 0)
     totals = jnp.sum(masks, axis=1, keepdims=True)
     width = lists.shape[1]
-    for line in range(4):
+    counts = jnp.zeros((1, skeleton), F32)
+    for line in range(LINES):
         offset = jnp.zeros((1, 1), F32)
         result = jnp.zeros((8, width), F32)
         for index, part in enumerate(segments):
@@ -245,9 +249,12 @@
                 [part[1].astype(F32), part[2].astype(F32), jnp.zeros((6, skeleton), F32)], 0
             ).astype(BF16)
             result += dot(values, hot, 1, 1)
-        lists[2 * line : 2 * line + 2] = result[:2].astype(jnp.int32)
-        lists[8 + line : 9 + line] = jnp.broadcast_to(offset, (1, width)).astype(jnp.int32)
-    lists[12:] = jnp.zeros((4, width), jnp.int32)
+        whole_result = result.astype(jnp.int32)
+        lists[line : line + 1] = whole_result[:1] + whole_result[1:2] * PACK
+        counts = jnp.where(lane == line, jnp.broadcast_to(offset, (1, skeleton)), counts)
+    lists[LINES : LINES + 1, :skeleton] = counts.astype(jnp.int32)
+    lists[LINES : LINES + 1, skeleton:] = jnp.zeros((1, width - skeleton), jnp.int32)
+    lists[LINES + 1 :] = jnp.zeros((8 - LINES - 1, width), jnp.int32)
 
 
 def build(rel, points, q1, q2, rhs, rhs_c, sw):
@@ -278,16 +285,20 @@
     node[features:] = weights.astype(BF16)
 
 
+def entry(lists, line, spot):
+    value = lists[line, spot]
+    return value & (PACK - 1), value // PACK
+
+
 def far_sums(line, size, lists, lhs_c, rhs_c, sw, far):
     skeleton = rhs_c.shape[2]
-    count = lists[8 + line, 0]
+    count = lists[LINES, line]
 
     def some(start, many):
         results = []
         for index in range(0, many, 2):
             spots = [start + index + half for half in range(2)]
-            owns = [lists[2 * line, spot] for spot in spots]
-            slots = [lists[2 * line + 1, spot] for spot in spots]
+            owns, slots = zip(*[entry(lists, line, spot) for spot in spots])
             blocks = [tile(lhs_c[own], rhs_c[slot], 1, 0) for own, slot in zip(owns, slots)]
             weights = jnp.concatenate([sw[slot, :, size:] for slot in slots], 0)
             part = dot(weights, jnp.concatenate(blocks, 0), 1, 1)
@@ -303,26 +314,29 @@
     stepped(count, FAR_STEP, some)
 
 
-def near_sums(size, lists, lhs_t, rhs, sw, near):
-    count = lists[8, 0]
-
+def near_parts(line, start, many, size, lists, lhs_t, rhs, sw):
+    count = lists[LINES, line]
+    results = []
+    for index in range(many):
+        spot = start + index
+        own, slot = entry(lists, line, spot)
+        block = tile(lhs_t[own], rhs[slot], 1, 0)
+        part = dot(sw[slot, :, :size], block, 1, 1)
+        results.append((own, jnp.where(spot < count, part, 0.0)))
+    return results
+
+
+def near_sums(line, size, lists, lhs_t, rhs, sw, near, done=0):
     def some(start, many):
-        results = []
-        for index in range(many):
-            spot = start + index
-            own, slot = lists[0, spot], lists[1, spot]
-            block = tile(lhs_t[own], rhs[slot], 1, 0)
-            part = dot(sw[slot, :, :size], block, 1, 1)
-            results.append((own, jnp.where(spot < count, part, 0.0)))
-        for own, part in results:
+        for own, part in near_parts(line, start + done, many, size, lists, lhs_t, rhs, sw):
             near[own] += part
 
-    stepped(count, NEAR_STEP, some)
+    stepped(lists[LINES, line] - done, NEAR_STEP, some)
 
 
 def stepped(count, many, some):
     half = many // 2
-    whole = (count + half - 1) // many
+    whole = jnp.maximum(count + half - 1, 0) // many
 
     def step_of(step, carry):
         some(step * many, many)
@@ -335,23 +349,39 @@
         some(whole * many, half)
 
 
-def first_kernel(points, q1, q2, lists, lhs_c, _, __, ___, rhs, rhs_c, sw, far):
+def first_kernel(points, q1, q2, lists_in, lhs_c, _, __, ___, rhs, rhs_c, sw, far, lists, sem):
+    copy = pltpu.make_async_copy(lists_in, lists, sem)
+    copy.start()
     build(1, points, q1, q2, rhs, rhs_c, sw)
     far[...] = jnp.zeros_like(far)
-    far_sums(1, points.shape[2], lists, lhs_c, rhs_c, sw, far)
+    copy.wait()
+    far_sums(2, points.shape[2], lists, lhs_c, rhs_c, sw, far)
 
 
 def other_kernel(
-    rel, points, q1, q2, lists, lhs_c, after, _, __, ___, ____,
-    rhs, rhs_c, sw, far,
+    rel, points, q1, q2, lists_in, lhs_c, after, _, __, ___, ____,
+    rhs, rhs_c, sw, far, lists, sem,
 ):
+    copy = pltpu.make_async_copy(lists_in, lists, sem)
+    copy.start()
     build(rel, points, q1, q2, rhs, rhs_c, sw)
-    far_sums(rel, rhs.shape[2], lists, lhs_c, rhs_c, sw, far)
+    copy.wait()
+    far_sums(rel + 1, rhs.shape[2], lists, lhs_c, rhs_c, sw, far)
+
+
+def mid_kernel(size, lists_in, lhs_t, rhs, sw, near_in, _, near, lists, sem):
+    copy = pltpu.make_async_copy(lists_in, lists, sem)
+    copy.start()
+    copy.wait()
+    near_sums(0, size, lists, lhs_t, rhs, sw, near)
 
 
 def last_kernel(features, levels, *refs):
     nodes, refs = refs[: 2 * levels], refs[2 * levels :]
-    upper_basis, subtree_basis, dev_basis, leaf_basis, lists, lhs_t, rhs, sw, far, near, out = refs
+    upper_basis, subtree_basis, dev_basis, leaf_basis, lists_in, lhs_t, *refs = refs
+    rhs, sw, far, near, out, lists, sem = refs
+    copy = pltpu.make_async_copy(lists_in, lists, sem)
+    copy.start()
     leaves, probes, size = out.shape
     skeleton = nodes[0].shape[1]
     me = lax.axis_index("sub")
@@ -371,21 +401,25 @@
     spot = pl.multiple_of(me * skeleton, skeleton)
     device = dot(potential.astype(BF16), subtree_basis[0, :, pl.ds(spot, skeleton)], 1, 0)
     spread = dot(device.astype(BF16), dev_basis[0], 1, 0).astype(BF16)
+    copy.wait()
+    early = near_parts(1, 0, NEAR_STEP // 2, size, lists, lhs_t, rhs, sw)
     for leaf in range(leaves):
         total = spread[:, leaf * skeleton : (leaf + 1) * skeleton].astype(F32) + far[leaf]
         high = total.astype(BF16)
         low = (total - high.astype(F32)).astype(BF16)
         part = dot(jnp.concatenate([high, low], 0), leaf_basis[leaf], 1, 0)
         out[leaf] = near[leaf] + part[:probes] + part[probes:]
-    near_sums(size, lists, lhs_t, rhs, sw, out)
-
-
-def call(kernel, out_shape, in_specs, micros, *args, scratch=(), aliases=()):
+    for own, part in early:
+        out[own] += part
+    near_sums(1, size, lists, lhs_t, rhs, sw, out, NEAR_STEP // 2)
+
+
+def call(kernel, out_shape, in_specs, micros, *args, scratch=(), aliases=(), out_specs=None):
     return pl.pallas_call(
         kernel,
         out_shape=out_shape,
         in_specs=in_specs,
-        out_specs=jax.tree.map(lambda _: VMEM, out_shape),
+        out_specs=out_specs or jax.tree.map(lambda _: VMEM, out_shape),
         scratch_shapes=scratch,
         input_output_aliases=dict(aliases),
         compiler_params=pltpu.CompilerParams(vmem_limit_bytes=VMEM_LIMIT),
@@ -421,7 +455,7 @@
     cap = near_pairs.shape[1]
     far_cap = far_pairs.shape[1]
     depth = features + AUG
-    width = max(-(-5 * cap // 128), -(-3 * far_cap // 128)) * 128
+    width = max(-(-3 * cap // 128), -(-3 * far_cap // 128)) * 128
     q1_rows = features + probes + LIST_ROWS + leaves
     slots = 4 * leaves
     shape = jax.ShapeDtypeStruct
@@ -432,6 +466,7 @@
     far_shape = shape((leaves, probes, skeleton), F32)
     node_shape = shape((features + probes, skeleton), BF16)
     token_shape = shape(TOKEN, F32)
+    line_scratch = [pltpu.SMEM((8, width), jnp.int32), pltpu.SemaphoreType.DMA]
 
     q1, q2 = call(
         prep_kernel,
@@ -481,7 +516,7 @@
     )
     node, lists = call(
         functools.partial(node_kernel, features, probes, cap, far_cap),
-        (node_shape, shape((16, width), jnp.int32)),
+        (node_shape, shape((8, width), jnp.int32)),
         [VMEM] * 6 + [ANY],
         2,
         q1,
@@ -502,7 +537,7 @@
             rhs, rhs_c, sw, far = call(
                 first_kernel,
                 (rhs_shape, rhs_c_shape, sw_shape, far_shape),
-                [VMEM] * 3 + [SMEM, VMEM] + [ANY] * 3,
+                [VMEM] * 3 + [ANY, VMEM] + [ANY] * 3,
                 5,
                 points_one,
                 q1_one,
@@ -513,6 +548,7 @@
                 rhs_c,
                 sw,
                 aliases=((5, 0), (6, 1), (7, 2)),
+                scratch=line_scratch,
             )
             after = far
         if height < levels:
@@ -529,6 +565,20 @@
                 scratch=[pltpu.VMEM((2, features + probes, skeleton), BF16)],
             )
 
+    near = call(
+        functools.partial(mid_kernel, size),
+        near_shape,
+        [ANY] + [VMEM] * 4 + [ANY],
+        5,
+        lists,
+        lhs_t,
+        rhs,
+        sw,
+        near,
+        node,
+        aliases=((4, 0),),
+        scratch=line_scratch,
+    )
     points_three = flipped(points_two, "sub", 1)
     q2_three = flipped(q2_two, "sub", 1)
     for rel, sources in (
@@ -537,7 +587,7 @@
         rhs, rhs_c, sw, far = call(
             functools.partial(other_kernel, rel),
             (rhs_shape, rhs_c_shape, sw_shape, far_shape),
-            [VMEM] * 3 + [SMEM, VMEM] + [ANY] * 4 + [VMEM],
+            [VMEM] * 3 + [ANY, VMEM] + [ANY] * 4 + [VMEM],
             3,
             *sources,
             lists,
@@ -548,12 +598,13 @@
             sw,
             far,
             aliases=((6, 0), (7, 1), (8, 2), (9, 3)),
+            scratch=line_scratch,
         )
 
     return call(
         functools.partial(last_kernel, features, levels),
         near_shape,
-        [VMEM] * (2 * levels + 4) + [SMEM] + [VMEM] * 5,
+        [VMEM] * (2 * levels + 4) + [ANY] + [VMEM] * 5,
         10,
         *nodes,
         upper_basis,
@@ -566,6 +617,7 @@
         sw,
         far,
         near,
+        scratch=line_scratch,
     )
 
 

time: 51.8 us -> 49.3 us (0.952)
  the two profiles are of different devices: /device:TPU:6 before, /device:TPU:7 now
where the time goes in v4:
time: 49.3 us; the launch traced here: 49.1 us
  Pallas kernels  29 us (59%)
  starting transfers between devices  10.7 us (22%)
  waiting for transfers between devices  8.36 us (17%)
  between operations  0.99 us (2%)
    pallas_call x10, Pallas kernels, call(): pl.pallas_call(kernel, out_shape=out_shape, in_specs=in_specs, out_specs=...  29 us
    ppermute x12, starting transfers between devices, flipped(): lax.ppermute(block, axis, [(low, low ^ bits) for low in range(count)])  10.7 us
    ppermute x12, waiting for transfers between devices, flipped(): lax.ppermute(block, axis, [(low, low ^ bits) for low in range(count)])  8.36 us
  transfers between devices with their start and end apart: 12, of which 1 were waited for; matrix products, arithmetic and copies ran while one was open for 0% of the time, Pallas kernels for 36%

profile of v4, /device:TPU:7, one launch (start us, length us, event | category | flops | bytes accessed | tf_op | source)
XLA Modules:
  0.0 49.1 jit_solution(14727445805778986127)
XLA Ops:
  0.7 0.0 copy-start.1
  0.7 0.0 copy-start.5
  0.7 3.6 %shard_map.127 = (bf16[112,128]{1,0:T(8,128)(2,1)S(1)}, bf16[16,16,384]{2,1,0:T(8,128)(2,1)S(1)}) custom-call(bf16[16,64,256]{2,1,0:T(8,128)(2,1)} %points.1, s32[16,16,256]{2,1,0:T(8,128)} %bits_in.1, s32[16,128]{1,0:T(8,128)} %leaf_skel.1, bf16[16,128,256]{2,1,0:T(8,128)(2,1)} %refs_9_.1, s32[1,128]{1,0:T(1,128)} %dev_skel_in.1, ...), custom_call_target="tpu_custom_call" | custom-call | flops 4000000000 | bytes 4000000 | tf_op jit(solution)/shard_map/pallas_call | solution.py:418
  4.3 0.7 %collective-permute-start = (bf16[112,128]{1,0:T(8,128)(2,1)S(1)}, bf16[112,128]{1,0:T(8,128)(2,1)S(1)}, u32[]{:S(2)}, u32[]{:S(2)}) collective-permute-start(bf16[112,128]{1,0:T(8,128)(2,1)S(1)} %get-tuple-element.27.mine), channel_id=1, source_target_pairs={{0,1},{1,0},{2,3},{3,2},{4,5},{5,4},{6,7},{7,6},{8,9},{9,8},{10,11... | collective-permute-start | bytes 86024 | tf_op jit(solution)/shard_map/ppermute | solution.py:31
  5.0 0.3 collective-permute-start.1
  5.3 1.5 %collective-permute-start.2 = (bf16[112,128]{1,0:T(8,128)(2,1)S(1)}, bf16[112,128]{1,0:T(8,128)(2,1)S(1)}, u32[]{:S(2)}, u32[]{:S(2)}) collective-permute-start(bf16[112,128]{1,0:T(8,128)(2,1)S(1)} %get-tuple-element.27.mine), channel_id=1, source_target_pairs={{0,3},{1,2},{2,1},{3,0},{4,7},{5,6},{6,5},{7,4},{8,11},{9,10},{10,... | collective-permute-start | bytes 86024 | tf_op jit(solution)/shard_map/ppermute | solution.py:31
  6.7 0.0 copy-done.1
  6.7 0.2 collective-permute-start.4
  6.9 0.0 copy-start.3
  6.9 0.4 collective-permute-start.5
  7.3 0.0 copy-done.5
  7.3 2.3 %shard_map.128 = (bf16[16,256,80]{2,1,0:T(8,128)(2,1)S(1)}, bf16[16,128,80]{2,1,0:T(8,128)(2,1)S(1)}, bf16[64,80,256]{2,1,0:T(8,128)(2,1)S(1)}, bf16[64,80,128]{...) custom-call(bf16[16,64,256]{2,1,0:T(8,128)(2,1)S(1)} %copy-done.1, ...), custom_call_target="tpu_custom_call" | custom-call | flops 5000000000 | bytes 5000000 | tf_op jit(solution)/shard_map/pallas_call | solution.py:418
  9.6 0.0 collective-permute-done.one.q1
  9.6 0.3 collective-permute-start.10
  9.9 0.0 collective-permute-done.1.two.q1
  9.9 1.2 %collective-permute-start.8 = (bf16[16,64,256]{2,1,0:T(8,128)(2,1)S(1)}, bf16[16,64,256]{2,1,0:T(8,128)(2,1)S(1)}, u32[]{:S(2)}, u32[]{:S(2)}) collective-permute-start(bf16[16,64,256]{2,1,0:T(8,128)(2,1)S(1)} %copy-done.1), channel_id=1, source_target_pairs={{0,2},{1,3},{2,0},{3,1},{4,6},{5,7},{6,4},{7,5},{8,10},{9,11},{10,... | collective-permute-start | bytes 1572872 | tf_op jit(solution)/shard_map/ppermute | solution.py:31
  11.1 0.0 collective-permute-done.2.three.q1
  11.1 0.0 copy-done.3
  11.1 0.0 copy-done.7
  11.1 0.8 %shard_map.129 = (bf16[80,128]{1,0:T(8,128)(2,1)S(1)}, s32[8,384]{1,0:T(8,128)S(1)}) custom-call(bf16[112,128]{1,0:T(8,128)(2,1)S(1)} %get-tuple-element.27.mine, bf16[112,128]{1,0:T(8,128)(2,1)S(1)} %collective-permute-done.one.q1, bf16[112,128]{1,0:T(8,128)(2,1)S(1)} %collective-permute-done.1.two.q1, ...), custom_call_target="tpu_custom_call" | custom-call | flops 2000000000 | bytes 2000000 | tf_op jit(solution)/shard_map/pallas_call | solution.py:418
  11.9 0.3 collective-permute-start.3
  12.1 0.0 collective-permute-done.5.q2
  12.1 0.0 collective-permute-done.4.points
  12.1 0.0 copy-start.6
  12.2 3.8 %shard_map.130 = (bf16[64,80,256]{2,1,0:T(8,128)(2,1)S(1)}, bf16[64,80,128]{2,1,0:T(8,128)(2,1)S(1)}, bf16[64,16,384]{2,1,0:T(8,128)(2,1)S(1)}, f32[16,16,128]{2,1,0:T(8,128)S(1)}) custom-call(bf16[16,64,256]{2,1,0:T(8,128)(2,1)S(1)} %collective-permute-done.4.points, ...), custom_call_target="tpu_custom_call", output_to_operand_aliasing={{0}: (5, {}), {1}: (6, {}), {2}: (7, {})} | custom-call | flops 5000000000 | bytes 5000000 | tf_op jit(solution)/shard_map/pallas_call | solution.py:418
  16.0 0.0 collective-permute-done.3.other.refs_1_
  16.0 0.0 copy-done.4
  16.0 0.0 copy-done.6
  16.0 0.2 shard_map.131.mine.refs_2_
  16.2 0.8 %collective-permute-start.6 = (bf16[80,128]{1,0:T(8,128)(2,1)S(1)}, bf16[80,128]{1,0:T(8,128)(2,1)S(1)}, u32[]{:S(2)}, u32[]{:S(2)}) collective-permute-start(bf16[80,128]{1,0:T(8,128)(2,1)S(1)} %shard_map.131.mine.refs_2_), channel_id=1, source_target_pairs={{0,8},{4,12},{8,0},{12,4},{16,24},{20,28},{24,16},{28,20},{1,9},{5... | collective-permute-start | bytes 61448 | tf_op jit(solution)/shard_map/ppermute | solution.py:31
  17.0 0.0 collective-permute-done.10.q2
  17.0 1.8 %collective-permute-start.11 = (bf16[16,16,384]{2,1,0:T(8,128)(2,1)S(1)}, bf16[16,16,384]{2,1,0:T(8,128)(2,1)S(1)}, u32[]{:S(2)}, u32[]{:S(2)}) collective-permute-start(bf16[16,16,384]{2,1,0:T(8,128)(2,1)S(1)} %collective-permute-done.10.q2), channel_id=1, source_target_pairs={{0,1},{1,0},{2,3},{3,2},{4,5},{5,4},{6,7},{7,6},{8,9},{9,8},{10,11... | collective-permute-start | bytes 589832 | tf_op jit(solution)/shard_map/ppermute | solution.py:31
  18.8 8.3 %collective-permute-done.8.points = bf16[16,64,256]{2,1,0:T(8,128)(2,1)S(1)} collective-permute-done((bf16[16,64,256]{2,1,0:T(8,128)(2,1)S(1)}, bf16[16,64,256]{2,1,0:T(8,128)(2,1)S(1)}, u32[]{:S(2)}, u32[]{:S(2)}) %collective-permute-start.8) | collective-permute-done | bytes 524320 | tf_op jit(solution)/shard_map/ppermute | solution.py:31
  27.2 1.0 %collective-permute-start.9 = (bf16[16,64,256]{2,1,0:T(8,128)(2,1)S(1)}, bf16[16,64,256]{2,1,0:T(8,128)(2,1)S(1)}, u32[]{:S(2)}, u32[]{:S(2)}) collective-permute-start(bf16[16,64,256]{2,1,0:T(8,128)(2,1)S(1)} %collective-permute-done.8.points), channel_id=1, source_target_pairs={{0,1},{1,0},{2,3},{3,2},{4,5},{5,4},{6,7},{7,6},{8,9},{9,8},{10,11... | collective-permute-start | bytes 1572872 | tf_op jit(solution)/shard_map/ppermute | solution.py:31
  28.2 0.0 collective-permute-done.6.other.refs_3_
  28.2 0.2 shard_map.132.after._.refs_4_
  28.3 2.4 %collective-permute-start.7 = (bf16[80,128]{1,0:T(8,128)(2,1)S(1)}, bf16[80,128]{1,0:T(8,128)(2,1)S(1)}, u32[]{:S(2)}, u32[]{:S(2)}) collective-permute-start(bf16[80,128]{1,0:T(8,128)(2,1)S(1)} %shard_map.132.after._.refs_4_), channel_id=1, source_target_pairs={{0,16},{4,20},{8,24},{12,28},{16,0},{20,4},{24,8},{28,12},{1,17},{... | collective-permute-start | bytes 61448 | tf_op jit(solution)/shard_map/ppermute | solution.py:31
  30.7 6.2 %shard_map.135.refs_15_ = f32[16,16,256]{2,1,0:T(8,128)S(1)} custom-call(s32[8,384]{1,0:T(8,128)S(1)} %get-tuple-element.31.lists_in.refs_10_, bf16[16,256,80]{2,1,0:T(8,128)(2,1)S(1)} %get-tuple-element.37.lhs_t.refs_11_, bf16[64,80,256]{2,1,0:T(8,128)(2,1)S(1)} %get-tuple-element.38._.rhs, ...), custom_call_target="tpu_custom_call", output_to_operand_aliasing={{}: (4, {})} | custom-call | flops 5000000000 | bytes 5000000 | tf_op jit(solution)/shard_map/pallas_call | solution.py:418
  36.9 2.2 %shard_map.133 = (bf16[64,80,256]{2,1,0:T(8,128)(2,1)S(1)}, bf16[64,80,128]{2,1,0:T(8,128)(2,1)S(1)}, bf16[64,16,384]{2,1,0:T(8,128)(2,1)S(1)}, f32[16,16,128]{2,1,0:T(8,128)S(1)}) custom-call(bf16[16,64,256]{2,1,0:T(8,128)(2,1)S(1)} %collective-permute-done.8.points, ...), custom_call_target="tpu_custom_call", output_to_operand_aliasing={{0}: (6, {}), {1}: (7, {}), {2}: (8, {}), {3}: (9, {})} | custom-call | flops 3000000000 | bytes 3000000 | tf_op jit(solution)/shard_map/pallas_call | solution.py:418
  39.1 0.0 collective-permute-done.11.q2
  39.1 0.0 collective-permute-done.9.points
  39.1 0.0 copy-start
  39.1 0.0 copy-start.2
  39.1 2.3 %shard_map.134 = (bf16[64,80,256]{2,1,0:T(8,128)(2,1)S(1)}, bf16[64,80,128]{2,1,0:T(8,128)(2,1)S(1)}, bf16[64,16,384]{2,1,0:T(8,128)(2,1)S(1)}, f32[16,16,128]{2,1,0:T(8,128)S(1)}) custom-call(bf16[16,64,256]{2,1,0:T(8,128)(2,1)S(1)} %collective-permute-done.9.points, ...), custom_call_target="tpu_custom_call", output_to_operand_aliasing={{0}: (6, {}), {1}: (7, {}), {2}: (8, {}), {3}: (9, {})} | custom-call | flops 3000000000 | bytes 3000000 | tf_op jit(solution)/shard_map/pallas_call | solution.py:418
  41.4 0.0 collective-permute-done.7.refs_5_
  41.4 0.0 copy-done
  41.4 0.0 copy-done.2
  41.4 7.5 %shard_map.136 = f32[16,16,256]{2,1,0:T(8,128)} custom-call(bf16[80,128]{1,0:T(8,128)(2,1)S(1)} %get-tuple-element.30.mine.refs_0_, bf16[80,128]{1,0:T(8,128)(2,1)S(1)} %collective-permute-done.3.other.refs_1_, bf16[80,128]{1,0:T(8,128)(2,1)S(1)} %shard_map.131.mine.refs_2_, bf16[80,128]{1,0:T(8,128)(2,1)S(1)} %collective-permute-done.6.other.refs_3_, ...), custom_call_target="tpu_custom_call" | custom-call | flops 10000000000 | bytes 10000000 | tf_op jit(solution)/shard_map/pallas_call | solution.py:418
  (2 shorter events, 0.0 us)
Async XLA Ops:
  0.7 6.1 %copy-start.1 = (bf16[16,64,256]{2,1,0:T(8,128)(2,1)S(1)}, bf16[16,64,256]{2,1,0:T(8,128)(2,1)}, u32[]{:S(2)}) copy-start(bf16[16,64,256]{2,1,0:T(8,128)(2,1)} %points.1) | copy-start | bytes 1572868
  0.7 6.6 %copy-start.5 = (s32[16,128]{1,0:T(8,128)S(1)}, s32[16,128]{1,0:T(8,128)}, u32[]{:S(2)}) copy-start(s32[16,128]{1,0:T(8,128)} %leaf_skel.1) | copy-start | bytes 24580
  4.3 5.3 %collective-permute-start = (bf16[112,128]{1,0:T(8,128)(2,1)S(1)}, bf16[112,128]{1,0:T(8,128)(2,1)S(1)}, u32[]{:S(2)}, u32[]{:S(2)}) collective-permute-start(bf16[112,128]{1,0:T(8,128)(2,1)S(1)} %get-tuple-element.27.mine), channel_id=1, source_target_pairs={{0,1},{1,0},{2,3},{3,2},{4,5},{5,4},{6,7},{7,6},{8,9},{9,8},{10,11... | collective-permute-start | bytes 86024 | tf_op jit(solution)/shard_map/ppermute | solution.py:31
  5.0 4.8 %collective-permute-start.1 = (bf16[112,128]{1,0:T(8,128)(2,1)S(1)}, bf16[112,128]{1,0:T(8,128)(2,1)S(1)}, u32[]{:S(2)}, u32[]{:S(2)}) collective-permute-start(bf16[112,128]{1,0:T(8,128)(2,1)S(1)} %get-tuple-element.27.mine), channel_id=1, source_target_pairs={{0,2},{1,3},{2,0},{3,1},{4,6},{5,7},{6,4},{7,5},{8,10},{9,11},{10,... | collective-permute-start | bytes 86024 | tf_op jit(solution)/shard_map/ppermute | solution.py:31
  5.3 5.8 %collective-permute-start.2 = (bf16[112,128]{1,0:T(8,128)(2,1)S(1)}, bf16[112,128]{1,0:T(8,128)(2,1)S(1)}, u32[]{:S(2)}, u32[]{:S(2)}) collective-permute-start(bf16[112,128]{1,0:T(8,128)(2,1)S(1)} %get-tuple-element.27.mine), channel_id=1, source_target_pairs={{0,3},{1,2},{2,1},{3,0},{4,7},{5,6},{6,5},{7,4},{8,11},{9,10},{10,... | collective-permute-start | bytes 86024 | tf_op jit(solution)/shard_map/ppermute | solution.py:31
  6.7 5.4 %collective-permute-start.4 = (bf16[16,64,256]{2,1,0:T(8,128)(2,1)S(1)}, bf16[16,64,256]{2,1,0:T(8,128)(2,1)S(1)}, u32[]{:S(2)}, u32[]{:S(2)}) collective-permute-start(bf16[16,64,256]{2,1,0:T(8,128)(2,1)S(1)} %copy-done.1), channel_id=1, source_target_pairs={{0,1},{1,0},{2,3},{3,2},{4,5},{5,4},{6,7},{7,6},{8,9},{9,8},{10,11... | collective-permute-start | bytes 1572872 | tf_op jit(solution)/shard_map/ppermute | solution.py:31
  6.9 4.2 %copy-start.3 = (bf16[1,128,512]{2,1,0:T(8,128)(2,1)S(1)}, bf16[1,128,512]{2,1,0:T(8,128)(2,1)}, u32[]{:S(2)}) copy-start(bf16[1,128,512]{2,1,0:T(8,128)(2,1)} %refs_7_.1) | copy-start | bytes 393220
  6.9 4.2 %copy-start.7 = (s32[1,128]{1,0:T(1,128)S(1)}, s32[1,128]{1,0:T(1,128)}, u32[]{:S(2)}) copy-start(s32[1,128]{1,0:T(1,128)} %skel.3) | copy-start | bytes 1540
  6.9 5.2 %collective-permute-start.5 = (bf16[16,16,384]{2,1,0:T(8,128)(2,1)S(1)}, bf16[16,16,384]{2,1,0:T(8,128)(2,1)S(1)}, u32[]{:S(2)}, u32[]{:S(2)}) collective-permute-start(bf16[16,16,384]{2,1,0:T(8,128)(2,1)S(1)} %get-tuple-element.28.q2), channel_id=1, source_target_pairs={{0,1},{1,0},{2,3},{3,2},{4,5},{5,4},{6,7},{7,6},{8,9},{9,8},{10,11... | collective-permute-start | bytes 589832 | tf_op jit(solution)/shard_map/ppermute | solution.py:31
  9.6 7.4 %collective-permute-start.10 = (bf16[16,16,384]{2,1,0:T(8,128)(2,1)S(1)}, bf16[16,16,384]{2,1,0:T(8,128)(2,1)S(1)}, u32[]{:S(2)}, u32[]{:S(2)}) collective-permute-start(bf16[16,16,384]{2,1,0:T(8,128)(2,1)S(1)} %get-tuple-element.28.q2), channel_id=1, source_target_pairs={{0,2},{1,3},{2,0},{3,1},{4,6},{5,7},{6,4},{7,5},{8,10},{9,11},{10,... | collective-permute-start | bytes 589832 | tf_op jit(solution)/shard_map/ppermute | solution.py:31
  9.9 17.3 %collective-permute-start.8 = (bf16[16,64,256]{2,1,0:T(8,128)(2,1)S(1)}, bf16[16,64,256]{2,1,0:T(8,128)(2,1)S(1)}, u32[]{:S(2)}, u32[]{:S(2)}) collective-permute-start(bf16[16,64,256]{2,1,0:T(8,128)(2,1)S(1)} %copy-done.1), channel_id=1, source_target_pairs={{0,2},{1,3},{2,0},{3,1},{4,6},{5,7},{6,4},{7,5},{8,10},{9,11},{10,... | collective-permute-start | bytes 1572872 | tf_op jit(solution)/shard_map/ppermute | solution.py:31
  11.9 4.1 %collective-permute-start.3 = (bf16[80,128]{1,0:T(8,128)(2,1)S(1)}, bf16[80,128]{1,0:T(8,128)(2,1)S(1)}, u32[]{:S(2)}, u32[]{:S(2)}) collective-permute-start(bf16[80,128]{1,0:T(8,128)(2,1)S(1)} %get-tuple-element.30.mine.refs_0_), channel_id=1, source_target_pairs={{0,4},{4,0},{8,12},{12,8},{16,20},{20,16},{24,28},{28,24},{1,5},{5... | collective-permute-start | bytes 61448 | tf_op jit(solution)/shard_map/ppermute | solution.py:31
  12.1 3.8 %copy-start.4 = (bf16[1,2,128,256]{3,2,1,0:T(8,128)(2,1)S(1)}, bf16[1,2,128,256]{3,2,1,0:T(8,128)(2,1)}, u32[]{:S(2)}) copy-start(bf16[1,2,128,256]{3,2,1,0:T(8,128)(2,1)} %refs_6_.1) | copy-start | bytes 393220
  12.1 3.9 %copy-start.6 = (s32[1,2,128]{2,1,0:T(2,128)S(1)}, s32[1,2,128]{2,1,0:T(2,128)}, u32[]{:S(2)}) copy-start(s32[1,2,128]{2,1,0:T(2,128)} %skel.5) | copy-start | bytes 3076
  16.2 12.0 %collective-permute-start.6 = (bf16[80,128]{1,0:T(8,128)(2,1)S(1)}, bf16[80,128]{1,0:T(8,128)(2,1)S(1)}, u32[]{:S(2)}, u32[]{:S(2)}) collective-permute-start(bf16[80,128]{1,0:T(8,128)(2,1)S(1)} %shard_map.131.mine.refs_2_), channel_id=1, source_target_pairs={{0,8},{4,12},{8,0},{12,4},{16,24},{20,28},{24,16},{28,20},{1,9},{5... | collective-permute-start | bytes 61448 | tf_op jit(solution)/shard_map/ppermute | solution.py:31
  17.0 22.1 %collective-permute-start.11 = (bf16[16,16,384]{2,1,0:T(8,128)(2,1)S(1)}, bf16[16,16,384]{2,1,0:T(8,128)(2,1)S(1)}, u32[]{:S(2)}, u32[]{:S(2)}) collective-permute-start(bf16[16,16,384]{2,1,0:T(8,128)(2,1)S(1)} %collective-permute-done.10.q2), channel_id=1, source_target_pairs={{0,1},{1,0},{2,3},{3,2},{4,5},{5,4},{6,7},{7,6},{8,9},{9,8},{10,11... | collective-permute-start | bytes 589832 | tf_op jit(solution)/shard_map/ppermute | solution.py:31
  27.2 11.9 %collective-permute-start.9 = (bf16[16,64,256]{2,1,0:T(8,128)(2,1)S(1)}, bf16[16,64,256]{2,1,0:T(8,128)(2,1)S(1)}, u32[]{:S(2)}, u32[]{:S(2)}) collective-permute-start(bf16[16,64,256]{2,1,0:T(8,128)(2,1)S(1)} %collective-permute-done.8.points), channel_id=1, source_target_pairs={{0,1},{1,0},{2,3},{3,2},{4,5},{5,4},{6,7},{7,6},{8,9},{9,8},{10,11... | collective-permute-start | bytes 1572872 | tf_op jit(solution)/shard_map/ppermute | solution.py:31
  28.3 13.1 %collective-permute-start.7 = (bf16[80,128]{1,0:T(8,128)(2,1)S(1)}, bf16[80,128]{1,0:T(8,128)(2,1)S(1)}, u32[]{:S(2)}, u32[]{:S(2)}) collective-permute-start(bf16[80,128]{1,0:T(8,128)(2,1)S(1)} %shard_map.132.after._.refs_4_), channel_id=1, source_target_pairs={{0,16},{4,20},{8,24},{12,28},{16,0},{20,4},{24,8},{28,12},{1,17},{... | collective-permute-start | bytes 61448 | tf_op jit(solution)/shard_map/ppermute | solution.py:31
  39.1 2.4 %copy-start = (bf16[16,128,256]{2,1,0:T(8,128)(2,1)S(1)}, bf16[16,128,256]{2,1,0:T(8,128)(2,1)}, u32[]{:S(2)}) copy-start(bf16[16,128,256]{2,1,0:T(8,128)(2,1)} %refs_9_.1) | copy-start | bytes 3145732
  39.1 2.4 %copy-start.2 = (bf16[1,128,2048]{2,1,0:T(8,128)(2,1)S(1)}, bf16[1,128,2048]{2,1,0:T(8,128)(2,1)}, u32[]{:S(2)}) copy-start(bf16[1,128,2048]{2,1,0:T(8,128)(2,1)} %refs_8_.1) | copy-start | bytes 1572868

commit v5 on v4

--- a/solution.py
+++ b/solution.py
@@ -68,6 +68,19 @@
 
 def tile(left, right, left_dim, right_dim):
     return jnp.exp(dot(left, right, left_dim, right_dim)).astype(BF16)
+
+
+def parts_of(pack, leaf, leaves, features, probes):
+    size = pack.shape[1]
+    skeleton = size // 2
+    signs = leaves * features + leaf * probes
+    weights = leaves * (features + probes) + (leaf // 2) * probes
+    side = (leaf % 2) * skeleton
+    return (
+        pack.at[leaf * features : (leaf + 1) * features],
+        pack.at[signs : signs + probes],
+        pack.at[weights : weights + probes, side : side + skeleton],
+    )
 
 
 def list_rows(pairs, row, width):
@@ -113,6 +126,12 @@
         copy.start()
     for copy in small:
         copy.wait()
+    lists = list_rows(near[0], 0, skeleton) + list_rows(far[0], 2, skeleton)
+    row = lax.broadcasted_iota(jnp.int32, lists.shape, 0)
+    lists = jnp.where(row == 4, near_count[0].astype(F32), lists)
+    base = features + probes
+    q1[base : base + LIST_ROWS] = jnp.concatenate([lists, jnp.zeros_like(lists)], 0).astype(BF16)
+    q1[base + LIST_ROWS :] = leaf_skel[...].astype(F32).astype(BF16)
     names = jnp.concatenate(
         [leaf_skel[...].astype(F32), jnp.broadcast_to(dev_skel[...].astype(F32), (8, skeleton))], 0
     ).T
@@ -134,8 +153,10 @@
             ).astype(BF16)
             coords.append(both[:features, :skeleton])
             weights.append(both[features:, skeleton:])
-            q2[leaf, :, :size] = signs
-            q2[leaf, :, size:] = weights[-1]
+            pack_points, pack_signs, pack_weights = parts_of(q2, leaf, leaves, features, probes)
+            pack_points[...] = points[leaf]
+            pack_signs[...] = signs
+            pack_weights[...] = weights[-1]
         spots = lane + float(first * skeleton)
         hot = jnp.where(spots == names[:, leaves : leaves + 1], 1.0, 0.0).astype(BF16)
         columns = slice(first * skeleton, (first + 2) * skeleton)
@@ -147,19 +168,14 @@
         )
     q1[:features] = total[:features, :skeleton].astype(BF16)
     q1[features : features + probes] = total[features:, skeleton:].astype(BF16)
-    lists = list_rows(near[0], 0, skeleton) + list_rows(far[0], 2, skeleton)
-    row = lax.broadcasted_iota(jnp.int32, lists.shape, 0)
-    lists = jnp.where(row == 4, near_count[0].astype(F32), lists)
-    base = features + probes
-    q1[base : base + LIST_ROWS] = jnp.concatenate([lists, jnp.zeros_like(lists)], 0).astype(BF16)
-    q1[base + LIST_ROWS :] = leaf_skel[...].astype(F32).astype(BF16)
-
-
-def own_kernel(points, leaf_skel, q2, lhs_t, lhs_c, rhs, rhs_c, sw, near, token):
-    leaves, features, size = points.shape
+
+
+def own_kernel(features, leaf_skel, q2, lhs_t, lhs_c, rhs, rhs_c, sw, near, token):
+    leaves, probes, size = near.shape
     for leaf in range(leaves):
-        left = with_norms(points[leaf], True)
-        right = with_norms(points[leaf], False)
+        points, signs, weights = parts_of(q2, leaf, leaves, features, probes)
+        left = with_norms(points[...], True)
+        right = with_norms(points[...], False)
         both = dot(
             jnp.concatenate([left, right], 0), one_hot(leaf_skel[leaf : leaf + 1, :], size), 1, 0
         ).astype(BF16)
@@ -167,13 +183,14 @@
         lhs_t[leaf] = left.T
         lhs_c[leaf] = both[: features + AUG].T
         rhs_c[leaf] = both[features + AUG :]
-        sw[leaf] = q2[leaf]
+        sw[leaf, :, :size] = signs[...]
+        sw[leaf, :, size:] = weights[...]
 
     def step_of(step, carry):
         for index in range(OWN_STEP):
             leaf = step * OWN_STEP + index
             block = tile(lhs_t[leaf], rhs[leaf], 1, 0)
-            near[leaf] = dot(q2[leaf, :, :size], block, 1, 1)
+            near[leaf] = dot(sw[leaf, :, :size], block, 1, 1)
         return carry
 
     lax.fori_loop(0, leaves // OWN_STEP, step_of, 0)
@@ -257,16 +274,18 @@
     lists[LINES + 1 :] = jnp.zeros((8 - LINES - 1, width), jnp.int32)
 
 
-def build(rel, points, q1, q2, rhs, rhs_c, sw):
-    leaves = q2.shape[0]
-    size = points.shape[2]
+def build(rel, features, q1, q2, rhs, rhs_c, sw):
+    probes, size = sw.shape[1], rhs.shape[2]
+    leaves = rhs.shape[0] // 4
     base = rel * leaves
     skels = q1[q1.shape[0] - leaves :].astype(F32).astype(jnp.int32)
     for leaf in range(leaves):
-        right = with_norms(points[leaf], False)
+        points, signs, weights = parts_of(q2, leaf, leaves, features, probes)
+        right = with_norms(points[...], False)
         rhs[base + leaf] = right
         rhs_c[base + leaf] = dot(right, one_hot(skels[leaf : leaf + 1], size), 1, 0).astype(BF16)
-        sw[base + leaf] = q2[leaf]
+        sw[base + leaf, :, :size] = signs[...]
+        sw[base + leaf, :, size:] = weights[...]
 
 
 def level_kernel(features, height, mine, other, basis, skel, after, node, pair):
@@ -290,14 +309,14 @@
     return value & (PACK - 1), value // PACK
 
 
-def far_sums(line, size, lists, lhs_c, rhs_c, sw, far):
+def far_sums(line, size, lists, lhs_c, rhs_c, sw, far, begin=0, head=False):
     skeleton = rhs_c.shape[2]
     count = lists[LINES, line]
 
     def some(start, many):
         results = []
         for index in range(0, many, 2):
-            spots = [start + index + half for half in range(2)]
+            spots = [begin + start + index + half for half in range(2)]
             owns, slots = zip(*[entry(lists, line, spot) for spot in spots])
             blocks = [tile(lhs_c[own], rhs_c[slot], 1, 0) for own, slot in zip(owns, slots)]
             weights = jnp.concatenate([sw[slot, :, size:] for slot in slots], 0)
@@ -311,7 +330,10 @@
         for own, part in results:
             far[own] += part
 
-    stepped(count, FAR_STEP, some)
+    if head:
+        some(0, FAR_STEP)
+    else:
+        stepped(count - begin, FAR_STEP, some)
 
 
 def near_parts(line, start, many, size, lists, lhs_t, rhs, sw):
@@ -349,24 +371,33 @@
         some(whole * many, half)
 
 
-def first_kernel(points, q1, q2, lists_in, lhs_c, _, __, ___, rhs, rhs_c, sw, far, lists, sem):
+def first_kernel(
+    features, q1, q2, lists_in, lhs_c, _, __, ___, rhs, rhs_c, sw, far, lists, sem
+):
     copy = pltpu.make_async_copy(lists_in, lists, sem)
     copy.start()
-    build(1, points, q1, q2, rhs, rhs_c, sw)
+    build(1, features, q1, q2, rhs, rhs_c, sw)
     far[...] = jnp.zeros_like(far)
     copy.wait()
-    far_sums(2, points.shape[2], lists, lhs_c, rhs_c, sw, far)
+    far_sums(2, rhs.shape[2], lists, lhs_c, rhs_c, sw, far, head=True)
 
 
 def other_kernel(
-    rel, points, q1, q2, lists_in, lhs_c, after, _, __, ___, ____,
+    rel, features, q1, q2, lists_in, lhs_c, after, _, __, ___, ____,
     rhs, rhs_c, sw, far, lists, sem,
 ):
     copy = pltpu.make_async_copy(lists_in, lists, sem)
     copy.start()
-    build(rel, points, q1, q2, rhs, rhs_c, sw)
+    build(rel, features, q1, q2, rhs, rhs_c, sw)
     copy.wait()
     far_sums(rel + 1, rhs.shape[2], lists, lhs_c, rhs_c, sw, far)
+
+
+def rest_kernel(size, lists_in, lhs_c, rhs_c, sw, far_in, _, far, lists, sem):
+    copy = pltpu.make_async_copy(lists_in, lists, sem)
+    copy.start()
+    copy.wait()
+    far_sums(2, size, lists, lhs_c, rhs_c, sw, far, begin=FAR_STEP)
 
 
 def mid_kernel(size, lists_in, lhs_t, rhs, sw, near_in, _, near, lists, sem):
@@ -458,6 +489,7 @@
     width = max(-(-3 * cap // 128), -(-3 * far_cap // 128)) * 128
     q1_rows = features + probes + LIST_ROWS + leaves
     slots = 4 * leaves
+    pack_rows = leaves * (features + probes) + leaves // 2 * probes
     shape = jax.ShapeDtypeStruct
     rhs_shape = shape((slots, depth, size), BF16)
     rhs_c_shape = shape((slots, depth, skeleton), BF16)
@@ -470,7 +502,7 @@
 
     q1, q2 = call(
         prep_kernel,
-        (shape((q1_rows, skeleton), BF16), shape((leaves, probes, size + skeleton), BF16)),
+        (shape((q1_rows, skeleton), BF16), shape((pack_rows, size), BF16)),
         [HBM] * 7 + [SMEM, HBM],
         4,
         *placed(points, probe_bits, leaf_skel, leaf_basis, device_skel, device_basis),
@@ -493,12 +525,10 @@
         flipped(q1, "sub", bits) for bits in (1, 2, 3)
     )
     q2_two = flipped(q2, "sub", 2)
-    points_two = flipped(points, "sub", 2)
     q2_one = flipped(q2, "sub", 1)
-    points_one = flipped(points, "sub", 1)
 
     lhs_t, lhs_c, rhs, rhs_c, sw, near, token = call(
-        own_kernel,
+        functools.partial(own_kernel, features),
         (
             shape((leaves, size, depth), BF16),
             shape((leaves, skeleton, depth), BF16),
@@ -508,9 +538,8 @@
             near_shape,
             token_shape,
         ),
-        [VMEM] * 3,
+        [VMEM] * 2,
         5,
-        points,
         leaf_skel,
         q2,
     )
@@ -535,11 +564,10 @@
         nodes += [node, other]
         if height == 1:
             rhs, rhs_c, sw, far = call(
-                first_kernel,
+                functools.partial(first_kernel, features),
                 (rhs_shape, rhs_c_shape, sw_shape, far_shape),
-                [VMEM] * 3 + [ANY, VMEM] + [ANY] * 3,
+                [VMEM] * 2 + [ANY, VMEM] + [ANY] * 3,
                 5,
-                points_one,
                 q1_one,
                 q2_one,
                 lists,
@@ -547,7 +575,23 @@
                 rhs,
                 rhs_c,
                 sw,
-                aliases=((5, 0), (6, 1), (7, 2)),
+                aliases=((4, 0), (5, 1), (6, 2)),
+                scratch=line_scratch,
+            )
+            after = far
+        if height == 2:
+            far = call(
+                functools.partial(rest_kernel, size),
+                far_shape,
+                [ANY] + [VMEM] * 4 + [ANY],
+                3,
+                lists,
+                lhs_c,
+                rhs_c,
+                sw,
+                far,
+                node,
+                aliases=((4, 0),),
                 scratch=line_scratch,
             )
             after = far
@@ -579,15 +623,12 @@
         aliases=((4, 0),),
         scratch=line_scratch,
     )
-    points_three = flipped(points_two, "sub", 1)
     q2_three = flipped(q2_two, "sub", 1)
-    for rel, sources in (
-        (2, (points_two, q1_two, q2_two)), (3, (points_three, q1_three, q2_three))
-    ):
+    for rel, sources in ((2, (q1_two, q2_two)), (3, (q1_three, q2_three))):
         rhs, rhs_c, sw, far = call(
-            functools.partial(other_kernel, rel),
+            functools.partial(other_kernel, rel, features),
             (rhs_shape, rhs_c_shape, sw_shape, far_shape),
-            [VMEM] * 3 + [ANY, VMEM] + [ANY] * 4 + [VMEM],
+            [VMEM] * 2 + [ANY, VMEM] + [ANY] * 4 + [VMEM],
             3,
             *sources,
             lists,
@@ -597,7 +638,7 @@
             rhs_c,
             sw,
             far,
-            aliases=((6, 0), (7, 1), (8, 2), (9, 3)),
+            aliases=((5, 0), (6, 1), (7, 2), (8, 3)),
             scratch=line_scratch,
         )
 

time: 49.3 us -> 46.8 us (0.949)
  starting transfers between devices: 10.7 us -> 7.58 us
  Pallas kernels: 29 us -> 29.7 us
    ppermute x12 -> x9, starting transfers between devices: 10.7 us -> 7.58 us  [flipped(): lax.ppermute(block, axis, [(low, low ^ bits) for low in range(count)])]
    pallas_call x10 -> x11, Pallas kernels: 29 us -> 29.7 us  [call(): pl.pallas_call(kernel, out_shape=out_shape, in_specs=in_specs, out_specs=...]
    ppermute x12 -> x9, waiting for transfers between devices: 8.36 us -> 8.29 us  [flipped(): lax.ppermute(block, axis, [(low, low ^ bits) for low in range(count)])]
  transfers between devices with their start and end apart: 12 -> 9, of which waited for: 1 -> 2; matrix products, arithmetic and copies ran while one was open for 0% -> 0% of each run, Pallas kernels for 36% -> 40%
where the time goes in v5:
time: 46.8 us; the launch traced here: 46.6 us
  Pallas kernels  29.7 us (63%)
  waiting for transfers between devices  8.29 us (18%)
  starting transfers between devices  7.58 us (16%)
  between operations  1 us (2%)
    pallas_call x11, Pallas kernels, call(): pl.pallas_call(kernel, out_shape=out_shape, in_specs=in_specs, out_specs=...  29.7 us
    ppermute x9, waiting for transfers between devices, flipped(): lax.ppermute(block, axis, [(low, low ^ bits) for low in range(count)])  8.29 us
    ppermute x9, starting transfers between devices, flipped(): lax.ppermute(block, axis, [(low, low ^ bits) for low in range(count)])  7.58 us
  transfers between devices with their start and end apart: 9, of which 2 were waited for; matrix products, arithmetic and copies ran while one was open for 0% of the time, Pallas kernels for 40%

profile of v5, /device:TPU:7, one launch (start us, length us, event | category | flops | bytes accessed | tf_op | source)
XLA Modules:
  0.0 46.6 jit_solution(10679240127648624287)
XLA Ops:
  0.7 0.0 copy-start.4
  0.7 3.6 %shard_map.127 = (bf16[112,128]{1,0:T(8,128)(2,1)S(1)}, bf16[1408,256]{1,0:T(8,128)(2,1)S(1)}) custom-call(bf16[16,64,256]{2,1,0:T(8,128)(2,1)} %points_in.1, s32[16,16,256]{2,1,0:T(8,128)} %bits_in.1, s32[16,128]{1,0:T(8,128)} %leaf_skel.1, bf16[16,128,256]{2,1,0:T(8,128)(2,1)} %refs_9_.1, s32[1,128]{1,0:T(1,128)} %dev_skel_in.1, ...), custom_call_target="tpu_custom_call" | custom-call | flops 4000000000 | bytes 4000000 | tf_op jit(solution)/shard_map/pallas_call | solution.py:449
  4.2 0.7 %collective-permute-start.4 = (bf16[1408,256]{1,0:T(8,128)(2,1)S(1)}, bf16[1408,256]{1,0:T(8,128)(2,1)S(1)}, u32[]{:S(2)}, u32[]{:S(2)}) collective-permute-start(bf16[1408,256]{1,0:T(8,128)(2,1)S(1)} %get-tuple-element.28.q2), channel_id=1, source_target_pairs={{0,1},{1,0},{2,3},{3,2},{4,5},{5,4},{6,7},{7,6},{8,9},{9,8},{10,11... | collective-permute-start | bytes 2162696 | tf_op jit(solution)/shard_map/ppermute | solution.py:31
  5.0 0.0 copy-start.2
  5.0 0.0 copy-start.6
  5.0 0.1 collective-permute-start
  5.1 0.3 collective-permute-start.1
  5.3 1.8 %collective-permute-start.2 = (bf16[112,128]{1,0:T(8,128)(2,1)S(1)}, bf16[112,128]{1,0:T(8,128)(2,1)S(1)}, u32[]{:S(2)}, u32[]{:S(2)}) collective-permute-start(bf16[112,128]{1,0:T(8,128)(2,1)S(1)} %get-tuple-element.27.mine), channel_id=1, source_target_pairs={{0,3},{1,2},{2,1},{3,0},{4,7},{5,6},{6,5},{7,4},{8,11},{9,10},{10,... | collective-permute-start | bytes 86024 | tf_op jit(solution)/shard_map/ppermute | solution.py:31
  7.1 0.3 collective-permute-start.7
  7.4 0.0 copy-done.4
  7.4 2.3 %shard_map.128 = (bf16[16,256,80]{2,1,0:T(8,128)(2,1)S(1)}, bf16[16,128,80]{2,1,0:T(8,128)(2,1)S(1)}, bf16[64,80,256]{2,1,0:T(8,128)(2,1)S(1)}, bf16[64,80,128]{...) custom-call(s32[16,128]{1,0:T(8,128)S(1)} %copy-done.4, ...), custom_call_target="tpu_custom_call" | custom-call | flops 5000000000 | bytes 5000000 | tf_op jit(solution)/shard_map/pallas_call | solution.py:449
  9.7 0.0 collective-permute-done.one.q1
  9.7 0.0 collective-permute-done.1.two.q1
  9.7 0.0 collective-permute-done.2.three.q1
  9.7 0.0 copy-done.2
  9.7 0.0 copy-done.6
  9.8 0.8 %shard_map.129 = (bf16[80,128]{1,0:T(8,128)(2,1)S(1)}, s32[8,384]{1,0:T(8,128)S(1)}) custom-call(bf16[112,128]{1,0:T(8,128)(2,1)S(1)} %get-tuple-element.27.mine, bf16[112,128]{1,0:T(8,128)(2,1)S(1)} %collective-permute-done.one.q1, bf16[112,128]{1,0:T(8,128)(2,1)S(1)} %collective-permute-done.1.two.q1, ...), custom_call_target="tpu_custom_call" | custom-call | flops 2000000000 | bytes 2000000 | tf_op jit(solution)/shard_map/pallas_call | solution.py:449
  10.5 0.0 collective-permute-start.3
  10.6 0.0 collective-permute-done.4.q2
  10.6 0.0 copy-start.3
  10.6 0.0 copy-start.5
  10.6 1.6 %shard_map.130 = (bf16[64,80,256]{2,1,0:T(8,128)(2,1)S(1)}, bf16[64,80,128]{2,1,0:T(8,128)(2,1)S(1)}, bf16[64,16,384]{2,1,0:T(8,128)(2,1)S(1)}, f32[16,16,128]{2,1,0:T(8,128)S(1)}) custom-call(bf16[112,128]{1,0:T(8,128)(2,1)S(1)} %collective-permute-done.one.q1, ...), custom_call_target="tpu_custom_call", output_to_operand_aliasing={{0}: (4, {}), {1}: (5, {}), {2}: (6, {})} | custom-call | flops 5000000000 | bytes 5000000 | tf_op jit(solution)/shard_map/pallas_call | solution.py:449
  12.2 1.3 %collective-permute-done.3.other.refs_1_ = bf16[80,128]{1,0:T(8,128)(2,1)S(1)} collective-permute-done((bf16[80,128]{1,0:T(8,128)(2,1)S(1)}, bf16[80,128]{1,0:T(8,128)(2,1)S(1)}, u32[]{:S(2)}, u32[]{:S(2)}) %collective-permute-start.3) | collective-permute-done | bytes 20512 | tf_op jit(solution)/shard_map/ppermute | solution.py:31
  13.5 0.0 copy-done.3
  13.5 0.0 copy-done.5
  13.5 0.2 shard_map.131._.mine.refs_2_
  13.7 1.4 %collective-permute-start.5 = (bf16[80,128]{1,0:T(8,128)(2,1)S(1)}, bf16[80,128]{1,0:T(8,128)(2,1)S(1)}, u32[]{:S(2)}, u32[]{:S(2)}) collective-permute-start(bf16[80,128]{1,0:T(8,128)(2,1)S(1)} %shard_map.131._.mine.refs_2_), channel_id=1, source_target_pairs={{0,8},{4,12},{8,0},{12,4},{16,24},{20,28},{24,16},{28,20},{1,9},{5... | collective-permute-start | bytes 61448 | tf_op jit(solution)/shard_map/ppermute | solution.py:31
  15.0 3.0 %shard_map.132.after.____ = f32[16,16,128]{2,1,0:T(8,128)S(1)} custom-call(s32[8,384]{1,0:T(8,128)S(1)} %get-tuple-element.31.lists_in.refs_10_, bf16[16,128,80]{2,1,0:T(8,128)(2,1)S(1)} %get-tuple-element.32.lhs_c, bf16[64,80,128]{2,1,0:T(8,128)(2,1)S(1)} %get-tuple-element.37.rhs_c.__, ...), custom_call_target="tpu_custom_call", output_to_operand_aliasing={{}: (4, {})} | custom-call | flops 3000000000 | bytes 3000000 | tf_op jit(solution)/shard_map/pallas_call | solution.py:449
  18.0 7.0 %collective-permute-done.7.q2 = bf16[1408,256]{1,0:T(8,128)(2,1)S(1)} collective-permute-done((bf16[1408,256]{1,0:T(8,128)(2,1)S(1)}, bf16[1408,256]{1,0:T(8,128)(2,1)S(1)}, u32[]{:S(2)}, u32[]{:S(2)}) %collective-permute-start.7) | collective-permute-done | bytes 720928 | tf_op jit(solution)/shard_map/ppermute | solution.py:31
  25.0 0.7 %collective-permute-start.8 = (bf16[1408,256]{1,0:T(8,128)(2,1)S(1)}, bf16[1408,256]{1,0:T(8,128)(2,1)S(1)}, u32[]{:S(2)}, u32[]{:S(2)}) collective-permute-start(bf16[1408,256]{1,0:T(8,128)(2,1)S(1)} %collective-permute-done.7.q2), channel_id=1, source_target_pairs={{0,1},{1,0},{2,3},{3,2},{4,5},{5,4},{6,7},{7,6},{8,9},{9,8},{10,11... | collective-permute-start | bytes 2162696 | tf_op jit(solution)/shard_map/ppermute | solution.py:31
  25.7 0.0 collective-permute-done.5.other.refs_3_
  25.7 0.2 shard_map.133.after._.refs_4_
  25.8 2.4 %collective-permute-start.6 = (bf16[80,128]{1,0:T(8,128)(2,1)S(1)}, bf16[80,128]{1,0:T(8,128)(2,1)S(1)}, u32[]{:S(2)}, u32[]{:S(2)}) collective-permute-start(bf16[80,128]{1,0:T(8,128)(2,1)S(1)} %shard_map.133.after._.refs_4_), channel_id=1, source_target_pairs={{0,16},{4,20},{8,24},{12,28},{16,0},{20,4},{24,8},{28,12},{1,17},{... | collective-permute-start | bytes 61448 | tf_op jit(solution)/shard_map/ppermute | solution.py:31
  28.2 6.2 %shard_map.136.refs_15_ = f32[16,16,256]{2,1,0:T(8,128)S(1)} custom-call(s32[8,384]{1,0:T(8,128)S(1)} %get-tuple-element.31.lists_in.refs_10_, bf16[16,256,80]{2,1,0:T(8,128)(2,1)S(1)} %get-tuple-element.39.lhs_t.refs_11_, bf16[64,80,256]{2,1,0:T(8,128)(2,1)S(1)} %get-tuple-element.40._.rhs, ...), custom_call_target="tpu_custom_call", output_to_operand_aliasing={{}: (4, {})} | custom-call | flops 5000000000 | bytes 5000000 | tf_op jit(solution)/shard_map/pallas_call | solution.py:449
  34.4 2.2 %shard_map.134 = (bf16[64,80,256]{2,1,0:T(8,128)(2,1)S(1)}, bf16[64,80,128]{2,1,0:T(8,128)(2,1)S(1)}, bf16[64,16,384]{2,1,0:T(8,128)(2,1)S(1)}, f32[16,16,128]{2,1,0:T(8,128)S(1)}) custom-call(bf16[112,128]{1,0:T(8,128)(2,1)S(1)} %collective-permute-done.1.two.q1, ...), custom_call_target="tpu_custom_call", output_to_operand_aliasing={{0}: (5, {}), {1}: (6, {}), {2}: (7, {}), {3}: (8, {})} | custom-call | flops 3000000000 | bytes 3000000 | tf_op jit(solution)/shard_map/pallas_call | solution.py:449
  36.5 0.0 collective-permute-done.8.q2
  36.6 0.0 copy-start
  36.6 0.0 copy-start.1
  36.6 2.3 %shard_map.135 = (bf16[64,80,256]{2,1,0:T(8,128)(2,1)S(1)}, bf16[64,80,128]{2,1,0:T(8,128)(2,1)S(1)}, bf16[64,16,384]{2,1,0:T(8,128)(2,1)S(1)}, f32[16,16,128]{2,1,0:T(8,128)S(1)}) custom-call(bf16[112,128]{1,0:T(8,128)(2,1)S(1)} %collective-permute-done.2.three.q1, ...), custom_call_target="tpu_custom_call", output_to_operand_aliasing={{0}: (5, {}), {1}: (6, {}), {2}: (7, {}), {3}: (8, {})} | custom-call | flops 3000000000 | bytes 3000000 | tf_op jit(solution)/shard_map/pallas_call | solution.py:449
  38.9 0.0 collective-permute-done.6.refs_5_
  38.9 0.0 copy-done
  38.9 0.0 copy-done.1
  38.9 7.5 %shard_map.137 = f32[16,16,256]{2,1,0:T(8,128)} custom-call(bf16[80,128]{1,0:T(8,128)(2,1)S(1)} %get-tuple-element.30.mine.refs_0_, bf16[80,128]{1,0:T(8,128)(2,1)S(1)} %collective-permute-done.3.other.refs_1_, bf16[80,128]{1,0:T(8,128)(2,1)S(1)} %shard_map.131._.mine.refs_2_, bf16[80,128]{1,0:T(8,128)(2,1)S(1)} %collective-permute-done.5.other.refs_3_, ...), custom_call_target="tpu_custom_call" | custom-call | flops 10000000000 | bytes 10000000 | tf_op jit(solution)/shard_map/pallas_call | solution.py:449
Async XLA Ops:
  0.7 6.7 %copy-start.4 = (s32[16,128]{1,0:T(8,128)S(1)}, s32[16,128]{1,0:T(8,128)}, u32[]{:S(2)}) copy-start(s32[16,128]{1,0:T(8,128)} %leaf_skel.1) | copy-start | bytes 24580
  4.2 6.4 %collective-permute-start.4 = (bf16[1408,256]{1,0:T(8,128)(2,1)S(1)}, bf16[1408,256]{1,0:T(8,128)(2,1)S(1)}, u32[]{:S(2)}, u32[]{:S(2)}) collective-permute-start(bf16[1408,256]{1,0:T(8,128)(2,1)S(1)} %get-tuple-element.28.q2), channel_id=1, source_target_pairs={{0,1},{1,0},{2,3},{3,2},{4,5},{5,4},{6,7},{7,6},{8,9},{9,8},{10,11... | collective-permute-start | bytes 2162696 | tf_op jit(solution)/shard_map/ppermute | solution.py:31
  5.0 4.8 %copy-start.2 = (bf16[1,128,512]{2,1,0:T(8,128)(2,1)S(1)}, bf16[1,128,512]{2,1,0:T(8,128)(2,1)}, u32[]{:S(2)}) copy-start(bf16[1,128,512]{2,1,0:T(8,128)(2,1)} %refs_7_.1) | copy-start | bytes 393220
  5.0 4.8 %copy-start.6 = (s32[1,128]{1,0:T(1,128)S(1)}, s32[1,128]{1,0:T(1,128)}, u32[]{:S(2)}) copy-start(s32[1,128]{1,0:T(1,128)} %skel.3) | copy-start | bytes 1540
  5.0 4.7 %collective-permute-start = (bf16[112,128]{1,0:T(8,128)(2,1)S(1)}, bf16[112,128]{1,0:T(8,128)(2,1)S(1)}, u32[]{:S(2)}, u32[]{:S(2)}) collective-permute-start(bf16[112,128]{1,0:T(8,128)(2,1)S(1)} %get-tuple-element.27.mine), channel_id=1, source_target_pairs={{0,1},{1,0},{2,3},{3,2},{4,5},{5,4},{6,7},{7,6},{8,9},{9,8},{10,11... | collective-permute-start | bytes 86024 | tf_op jit(solution)/shard_map/ppermute | solution.py:31
  5.1 4.6 %collective-permute-start.1 = (bf16[112,128]{1,0:T(8,128)(2,1)S(1)}, bf16[112,128]{1,0:T(8,128)(2,1)S(1)}, u32[]{:S(2)}, u32[]{:S(2)}) collective-permute-start(bf16[112,128]{1,0:T(8,128)(2,1)S(1)} %get-tuple-element.27.mine), channel_id=1, source_target_pairs={{0,2},{1,3},{2,0},{3,1},{4,6},{5,7},{6,4},{7,5},{8,10},{9,11},{10,... | collective-permute-start | bytes 86024 | tf_op jit(solution)/shard_map/ppermute | solution.py:31
  5.3 4.4 %collective-permute-start.2 = (bf16[112,128]{1,0:T(8,128)(2,1)S(1)}, bf16[112,128]{1,0:T(8,128)(2,1)S(1)}, u32[]{:S(2)}, u32[]{:S(2)}) collective-permute-start(bf16[112,128]{1,0:T(8,128)(2,1)S(1)} %get-tuple-element.27.mine), channel_id=1, source_target_pairs={{0,3},{1,2},{2,1},{3,0},{4,7},{5,6},{6,5},{7,4},{8,11},{9,10},{10,... | collective-permute-start | bytes 86024 | tf_op jit(solution)/shard_map/ppermute | solution.py:31
  7.1 17.9 %collective-permute-start.7 = (bf16[1408,256]{1,0:T(8,128)(2,1)S(1)}, bf16[1408,256]{1,0:T(8,128)(2,1)S(1)}, u32[]{:S(2)}, u32[]{:S(2)}) collective-permute-start(bf16[1408,256]{1,0:T(8,128)(2,1)S(1)} %get-tuple-element.28.q2), channel_id=1, source_target_pairs={{0,2},{1,3},{2,0},{3,1},{4,6},{5,7},{6,4},{7,5},{8,10},{9,11},{10,... | collective-permute-start | bytes 2162696 | tf_op jit(solution)/shard_map/ppermute | solution.py:31
  10.5 3.0 %collective-permute-start.3 = (bf16[80,128]{1,0:T(8,128)(2,1)S(1)}, bf16[80,128]{1,0:T(8,128)(2,1)S(1)}, u32[]{:S(2)}, u32[]{:S(2)}) collective-permute-start(bf16[80,128]{1,0:T(8,128)(2,1)S(1)} %get-tuple-element.30.mine.refs_0_), channel_id=1, source_target_pairs={{0,4},{4,0},{8,12},{12,8},{16,20},{20,16},{24,28},{28,24},{1,5},{5... | collective-permute-start | bytes 61448 | tf_op jit(solution)/shard_map/ppermute | solution.py:31
  10.6 2.9 %copy-start.3 = (bf16[1,2,128,256]{3,2,1,0:T(8,128)(2,1)S(1)}, bf16[1,2,128,256]{3,2,1,0:T(8,128)(2,1)}, u32[]{:S(2)}) copy-start(bf16[1,2,128,256]{3,2,1,0:T(8,128)(2,1)} %refs_6_.1) | copy-start | bytes 393220
  10.6 2.9 %copy-start.5 = (s32[1,2,128]{2,1,0:T(2,128)S(1)}, s32[1,2,128]{2,1,0:T(2,128)}, u32[]{:S(2)}) copy-start(s32[1,2,128]{2,1,0:T(2,128)} %skel.5) | copy-start | bytes 3076
  13.7 12.0 %collective-permute-start.5 = (bf16[80,128]{1,0:T(8,128)(2,1)S(1)}, bf16[80,128]{1,0:T(8,128)(2,1)S(1)}, u32[]{:S(2)}, u32[]{:S(2)}) collective-permute-start(bf16[80,128]{1,0:T(8,128)(2,1)S(1)} %shard_map.131._.mine.refs_2_), channel_id=1, source_target_pairs={{0,8},{4,12},{8,0},{12,4},{16,24},{20,28},{24,16},{28,20},{1,9},{5... | collective-permute-start | bytes 61448 | tf_op jit(solution)/shard_map/ppermute | solution.py:31
  25.0 11.6 %collective-permute-start.8 = (bf16[1408,256]{1,0:T(8,128)(2,1)S(1)}, bf16[1408,256]{1,0:T(8,128)(2,1)S(1)}, u32[]{:S(2)}, u32[]{:S(2)}) collective-permute-start(bf16[1408,256]{1,0:T(8,128)(2,1)S(1)} %collective-permute-done.7.q2), channel_id=1, source_target_pairs={{0,1},{1,0},{2,3},{3,2},{4,5},{5,4},{6,7},{7,6},{8,9},{9,8},{10,11... | collective-permute-start | bytes 2162696 | tf_op jit(solution)/shard_map/ppermute | solution.py:31
  25.8 13.1 %collective-permute-start.6 = (bf16[80,128]{1,0:T(8,128)(2,1)S(1)}, bf16[80,128]{1,0:T(8,128)(2,1)S(1)}, u32[]{:S(2)}, u32[]{:S(2)}) collective-permute-start(bf16[80,128]{1,0:T(8,128)(2,1)S(1)} %shard_map.133.after._.refs_4_), channel_id=1, source_target_pairs={{0,16},{4,20},{8,24},{12,28},{16,0},{20,4},{24,8},{28,12},{1,17},{... | collective-permute-start | bytes 61448 | tf_op jit(solution)/shard_map/ppermute | solution.py:31
  36.6 2.3 %copy-start = (bf16[16,128,256]{2,1,0:T(8,128)(2,1)S(1)}, bf16[16,128,256]{2,1,0:T(8,128)(2,1)}, u32[]{:S(2)}) copy-start(bf16[16,128,256]{2,1,0:T(8,128)(2,1)} %refs_9_.1) | copy-start | bytes 3145732
  36.6 2.3 %copy-start.1 = (bf16[1,128,2048]{2,1,0:T(8,128)(2,1)S(1)}, bf16[1,128,2048]{2,1,0:T(8,128)(2,1)}, u32[]{:S(2)}) copy-start(bf16[1,128,2048]{2,1,0:T(8,128)(2,1)} %refs_8_.1) | copy-start | bytes 1572868

commit v6 on v5

--- a/solution.py
+++ b/solution.py
@@ -12,8 +12,9 @@
 F32 = jnp.float32
 AUG = 16
 NEAR_STEP = 16
+MID_MOST = 3 * NEAR_STEP
 OWN_STEP = 8
-CHUNKS = 4
+CHUNKS = 2
 FAR_STEP = 32
 LIST_ROWS = 16
 LINES = 5
@@ -348,12 +349,15 @@
     return results
 
 
-def near_sums(line, size, lists, lhs_t, rhs, sw, near, done=0):
+def near_sums(line, size, lists, lhs_t, rhs, sw, near, done=0, most=None):
     def some(start, many):
         for own, part in near_parts(line, start + done, many, size, lists, lhs_t, rhs, sw):
             near[own] += part
 
-    stepped(lists[LINES, line] - done, NEAR_STEP, some)
+    count = lists[LINES, line]
+    if most is not None:
+        count = jnp.minimum(count, most)
+    stepped(count - done, NEAR_STEP, some)
 
 
 def stepped(count, many, some):
@@ -404,7 +408,7 @@
     copy = pltpu.make_async_copy(lists_in, lists, sem)
     copy.start()
     copy.wait()
-    near_sums(0, size, lists, lhs_t, rhs, sw, near)
+    near_sums(0, size, lists, lhs_t, rhs, sw, near, most=MID_MOST)
 
 
 def last_kernel(features, levels, *refs):
@@ -443,6 +447,7 @@
     for own, part in early:
         out[own] += part
     near_sums(1, size, lists, lhs_t, rhs, sw, out, NEAR_STEP // 2)
+    near_sums(0, size, lists, lhs_t, rhs, sw, out, MID_MOST)
 
 
 def call(kernel, out_shape, in_specs, micros, *args, scratch=(), aliases=(), out_specs=None):

time: 46.8 us -> 46.3 us (0.989)
  the two profiles are of different devices: /device:TPU:7 before, /device:TPU:11 now
where the time goes in v6:
time: 46.3 us; the launch traced here: 46.2 us
  Pallas kernels  29.3 us (63%)
  waiting for transfers between devices  8.29 us (18%)
  starting transfers between devices  7.61 us (16%)
  between operations  0.97 us (2%)
    pallas_call x11, Pallas kernels, call(): pl.pallas_call(kernel, out_shape=out_shape, in_specs=in_specs, out_specs=...  29.3 us
    ppermute x9, waiting for transfers between devices, flipped(): lax.ppermute(block, axis, [(low, low ^ bits) for low in range(count)])  8.29 us
    ppermute x9, starting transfers between devices, flipped(): lax.ppermute(block, axis, [(low, low ^ bits) for low in range(count)])  7.61 us
  transfers between devices with their start and end apart: 9, of which 2 were waited for; matrix products, arithmetic and copies ran while one was open for 0% of the time, Pallas kernels for 37%

profile of v6, /device:TPU:11, one launch (start us, length us, event | category | flops | bytes accessed | tf_op | source)
XLA Modules:
  0.0 46.2 jit_solution(14105850907237391024)
XLA Ops:
  0.7 0.0 copy-start.4
  0.7 3.1 %shard_map.127 = (bf16[112,128]{1,0:T(8,128)(2,1)S(1)}, bf16[1408,256]{1,0:T(8,128)(2,1)S(1)}) custom-call(bf16[16,64,256]{2,1,0:T(8,128)(2,1)} %points_in.1, s32[16,16,256]{2,1,0:T(8,128)} %bits_in.1, s32[16,128]{1,0:T(8,128)} %leaf_skel.1, bf16[16,128,256]{2,1,0:T(8,128)(2,1)} %refs_9_.1, s32[1,128]{1,0:T(1,128)} %dev_skel_in.1, ...), custom_call_target="tpu_custom_call" | custom-call | flops 4000000000 | bytes 4000000 | tf_op jit(solution)/shard_map/pallas_call | solution.py:454
  3.8 0.7 %collective-permute-start.4 = (bf16[1408,256]{1,0:T(8,128)(2,1)S(1)}, bf16[1408,256]{1,0:T(8,128)(2,1)S(1)}, u32[]{:S(2)}, u32[]{:S(2)}) collective-permute-start(bf16[1408,256]{1,0:T(8,128)(2,1)S(1)} %get-tuple-element.28.q2), channel_id=1, source_target_pairs={{0,1},{1,0},{2,3},{3,2},{4,5},{5,4},{6,7},{7,6},{8,9},{9,8},{10,11... | collective-permute-start | bytes 2162696 | tf_op jit(solution)/shard_map/ppermute | solution.py:32
  4.5 0.0 copy-start.2
  4.5 0.0 copy-start.6
  4.5 0.1 collective-permute-start
  4.6 0.3 collective-permute-start.1
  4.9 1.8 %collective-permute-start.2 = (bf16[112,128]{1,0:T(8,128)(2,1)S(1)}, bf16[112,128]{1,0:T(8,128)(2,1)S(1)}, u32[]{:S(2)}, u32[]{:S(2)}) collective-permute-start(bf16[112,128]{1,0:T(8,128)(2,1)S(1)} %get-tuple-element.27.mine), channel_id=1, source_target_pairs={{0,3},{1,2},{2,1},{3,0},{4,7},{5,6},{6,5},{7,4},{8,11},{9,10},{10,... | collective-permute-start | bytes 86024 | tf_op jit(solution)/shard_map/ppermute | solution.py:32
  6.7 0.3 collective-permute-start.7
  6.9 0.0 copy-done.4
  6.9 2.3 %shard_map.128 = (bf16[16,256,80]{2,1,0:T(8,128)(2,1)S(1)}, bf16[16,128,80]{2,1,0:T(8,128)(2,1)S(1)}, bf16[64,80,256]{2,1,0:T(8,128)(2,1)S(1)}, bf16[64,80,128]{...) custom-call(s32[16,128]{1,0:T(8,128)S(1)} %copy-done.4, ...), custom_call_target="tpu_custom_call" | custom-call | flops 5000000000 | bytes 5000000 | tf_op jit(solution)/shard_map/pallas_call | solution.py:454
  9.3 0.0 collective-permute-done.one.q1
  9.3 0.0 collective-permute-done.1.two.q1
  9.3 0.0 collective-permute-done.2.three.q1
  9.3 0.0 copy-done.2
  9.3 0.0 copy-done.6
  9.3 0.8 %shard_map.129 = (bf16[80,128]{1,0:T(8,128)(2,1)S(1)}, s32[8,384]{1,0:T(8,128)S(1)}) custom-call(bf16[112,128]{1,0:T(8,128)(2,1)S(1)} %get-tuple-element.27.mine, bf16[112,128]{1,0:T(8,128)(2,1)S(1)} %collective-permute-done.one.q1, bf16[112,128]{1,0:T(8,128)(2,1)S(1)} %collective-permute-done.1.two.q1, ...), custom_call_target="tpu_custom_call" | custom-call | flops 2000000000 | bytes 2000000 | tf_op jit(solution)/shard_map/pallas_call | solution.py:454
  10.1 1.3 %collective-permute-start.3 = (bf16[80,128]{1,0:T(8,128)(2,1)S(1)}, bf16[80,128]{1,0:T(8,128)(2,1)S(1)}, u32[]{:S(2)}, u32[]{:S(2)}) collective-permute-start(bf16[80,128]{1,0:T(8,128)(2,1)S(1)} %get-tuple-element.30.mine.refs_0_), channel_id=1, source_target_pairs={{0,4},{4,0},{8,12},{12,8},{16,20},{20,16},{24,28},{28,24},{1,5},{5... | collective-permute-start | bytes 61448 | tf_op jit(solution)/shard_map/ppermute | solution.py:32
  11.4 0.0 collective-permute-done.4.q2
  11.4 0.0 copy-start.3
  11.4 0.0 copy-start.5
  11.4 1.6 %shard_map.130 = (bf16[64,80,256]{2,1,0:T(8,128)(2,1)S(1)}, bf16[64,80,128]{2,1,0:T(8,128)(2,1)S(1)}, bf16[64,16,384]{2,1,0:T(8,128)(2,1)S(1)}, f32[16,16,128]{2,1,0:T(8,128)S(1)}) custom-call(bf16[112,128]{1,0:T(8,128)(2,1)S(1)} %collective-permute-done.one.q1, ...), custom_call_target="tpu_custom_call", output_to_operand_aliasing={{0}: (4, {}), {1}: (5, {}), {2}: (6, {})} | custom-call | flops 5000000000 | bytes 5000000 | tf_op jit(solution)/shard_map/pallas_call | solution.py:454
  13.0 0.1 collective-permute-done.3.other.refs_1_
  13.1 0.0 copy-done.3
  13.1 0.0 copy-done.5
  13.1 0.2 shard_map.131._.mine.refs_2_
  13.2 0.2 collective-permute-start.5
  13.4 3.0 %shard_map.132.after.____ = f32[16,16,128]{2,1,0:T(8,128)S(1)} custom-call(s32[8,384]{1,0:T(8,128)S(1)} %get-tuple-element.31.lists_in.refs_10_, bf16[16,128,80]{2,1,0:T(8,128)(2,1)S(1)} %get-tuple-element.32.lhs_c, bf16[64,80,128]{2,1,0:T(8,128)(2,1)S(1)} %get-tuple-element.37.rhs_c.__, ...), custom_call_target="tpu_custom_call", output_to_operand_aliasing={{}: (4, {})} | custom-call | flops 3000000000 | bytes 3000000 | tf_op jit(solution)/shard_map/pallas_call | solution.py:454
  16.4 8.2 %collective-permute-done.7.q2 = bf16[1408,256]{1,0:T(8,128)(2,1)S(1)} collective-permute-done((bf16[1408,256]{1,0:T(8,128)(2,1)S(1)}, bf16[1408,256]{1,0:T(8,128)(2,1)S(1)}, u32[]{:S(2)}, u32[]{:S(2)}) %collective-permute-start.7) | collective-permute-done | bytes 720928 | tf_op jit(solution)/shard_map/ppermute | solution.py:32
  24.5 0.7 %collective-permute-start.8 = (bf16[1408,256]{1,0:T(8,128)(2,1)S(1)}, bf16[1408,256]{1,0:T(8,128)(2,1)S(1)}, u32[]{:S(2)}, u32[]{:S(2)}) collective-permute-start(bf16[1408,256]{1,0:T(8,128)(2,1)S(1)} %collective-permute-done.7.q2), channel_id=1, source_target_pairs={{0,1},{1,0},{2,3},{3,2},{4,5},{5,4},{6,7},{7,6},{8,9},{9,8},{10,11... | collective-permute-start | bytes 2162696 | tf_op jit(solution)/shard_map/ppermute | solution.py:32
  25.2 0.0 collective-permute-done.5.other.refs_3_
  25.2 0.2 shard_map.133.after._.refs_4_
  25.4 2.4 %collective-permute-start.6 = (bf16[80,128]{1,0:T(8,128)(2,1)S(1)}, bf16[80,128]{1,0:T(8,128)(2,1)S(1)}, u32[]{:S(2)}, u32[]{:S(2)}) collective-permute-start(bf16[80,128]{1,0:T(8,128)(2,1)S(1)} %shard_map.133.after._.refs_4_), channel_id=1, source_target_pairs={{0,16},{4,20},{8,24},{12,28},{16,0},{20,4},{24,8},{28,12},{1,17},{... | collective-permute-start | bytes 61448 | tf_op jit(solution)/shard_map/ppermute | solution.py:32
  27.8 4.8 %shard_map.136.refs_15_ = f32[16,16,256]{2,1,0:T(8,128)S(1)} custom-call(s32[8,384]{1,0:T(8,128)S(1)} %get-tuple-element.31.lists_in.refs_10_, bf16[16,256,80]{2,1,0:T(8,128)(2,1)S(1)} %get-tuple-element.39.lhs_t.refs_11_, bf16[64,80,256]{2,1,0:T(8,128)(2,1)S(1)} %get-tuple-element.40._.rhs, ...), custom_call_target="tpu_custom_call", output_to_operand_aliasing={{}: (4, {})} | custom-call | flops 5000000000 | bytes 5000000 | tf_op jit(solution)/shard_map/pallas_call | solution.py:454
  32.6 2.1 %shard_map.134 = (bf16[64,80,256]{2,1,0:T(8,128)(2,1)S(1)}, bf16[64,80,128]{2,1,0:T(8,128)(2,1)S(1)}, bf16[64,16,384]{2,1,0:T(8,128)(2,1)S(1)}, f32[16,16,128]{2,1,0:T(8,128)S(1)}) custom-call(bf16[112,128]{1,0:T(8,128)(2,1)S(1)} %collective-permute-done.1.two.q1, ...), custom_call_target="tpu_custom_call", output_to_operand_aliasing={{0}: (5, {}), {1}: (6, {}), {2}: (7, {}), {3}: (8, {})} | custom-call | flops 3000000000 | bytes 3000000 | tf_op jit(solution)/shard_map/pallas_call | solution.py:454
  34.7 0.0 collective-permute-done.8.q2
  34.8 0.0 copy-start
  34.8 0.0 copy-start.1
  34.8 2.3 %shard_map.135 = (bf16[64,80,256]{2,1,0:T(8,128)(2,1)S(1)}, bf16[64,80,128]{2,1,0:T(8,128)(2,1)S(1)}, bf16[64,16,384]{2,1,0:T(8,128)(2,1)S(1)}, f32[16,16,128]{2,1,0:T(8,128)S(1)}) custom-call(bf16[112,128]{1,0:T(8,128)(2,1)S(1)} %collective-permute-done.2.three.q1, ...), custom_call_target="tpu_custom_call", output_to_operand_aliasing={{0}: (5, {}), {1}: (6, {}), {2}: (7, {}), {3}: (8, {})} | custom-call | flops 3000000000 | bytes 3000000 | tf_op jit(solution)/shard_map/pallas_call | solution.py:454
  37.1 0.0 collective-permute-done.6.refs_5_
  37.1 0.0 copy-done
  37.1 0.0 copy-done.1
  37.1 8.9 %shard_map.137 = f32[16,16,256]{2,1,0:T(8,128)} custom-call(bf16[80,128]{1,0:T(8,128)(2,1)S(1)} %get-tuple-element.30.mine.refs_0_, bf16[80,128]{1,0:T(8,128)(2,1)S(1)} %collective-permute-done.3.other.refs_1_, bf16[80,128]{1,0:T(8,128)(2,1)S(1)} %shard_map.131._.mine.refs_2_, bf16[80,128]{1,0:T(8,128)(2,1)S(1)} %collective-permute-done.5.other.refs_3_, ...), custom_call_target="tpu_custom_call" | custom-call | flops 10000000000 | bytes 10000000 | tf_op jit(solution)/shard_map/pallas_call | solution.py:454
Async XLA Ops:
  0.7 6.3 %copy-start.4 = (s32[16,128]{1,0:T(8,128)S(1)}, s32[16,128]{1,0:T(8,128)}, u32[]{:S(2)}) copy-start(s32[16,128]{1,0:T(8,128)} %leaf_skel.1) | copy-start | bytes 24580
  3.8 7.6 %collective-permute-start.4 = (bf16[1408,256]{1,0:T(8,128)(2,1)S(1)}, bf16[1408,256]{1,0:T(8,128)(2,1)S(1)}, u32[]{:S(2)}, u32[]{:S(2)}) collective-permute-start(bf16[1408,256]{1,0:T(8,128)(2,1)S(1)} %get-tuple-element.28.q2), channel_id=1, source_target_pairs={{0,1},{1,0},{2,3},{3,2},{4,5},{5,4},{6,7},{7,6},{8,9},{9,8},{10,11... | collective-permute-start | bytes 2162696 | tf_op jit(solution)/shard_map/ppermute | solution.py:32
  4.5 4.8 %copy-start.2 = (bf16[1,128,512]{2,1,0:T(8,128)(2,1)S(1)}, bf16[1,128,512]{2,1,0:T(8,128)(2,1)}, u32[]{:S(2)}) copy-start(bf16[1,128,512]{2,1,0:T(8,128)(2,1)} %refs_7_.1) | copy-start | bytes 393220
  4.5 4.8 %copy-start.6 = (s32[1,128]{1,0:T(1,128)S(1)}, s32[1,128]{1,0:T(1,128)}, u32[]{:S(2)}) copy-start(s32[1,128]{1,0:T(1,128)} %skel.3) | copy-start | bytes 1540
  4.5 4.7 %collective-permute-start = (bf16[112,128]{1,0:T(8,128)(2,1)S(1)}, bf16[112,128]{1,0:T(8,128)(2,1)S(1)}, u32[]{:S(2)}, u32[]{:S(2)}) collective-permute-start(bf16[112,128]{1,0:T(8,128)(2,1)S(1)} %get-tuple-element.27.mine), channel_id=1, source_target_pairs={{0,1},{1,0},{2,3},{3,2},{4,5},{5,4},{6,7},{7,6},{8,9},{9,8},{10,11... | collective-permute-start | bytes 86024 | tf_op jit(solution)/shard_map/ppermute | solution.py:32
  4.6 4.6 %collective-permute-start.1 = (bf16[112,128]{1,0:T(8,128)(2,1)S(1)}, bf16[112,128]{1,0:T(8,128)(2,1)S(1)}, u32[]{:S(2)}, u32[]{:S(2)}) collective-permute-start(bf16[112,128]{1,0:T(8,128)(2,1)S(1)} %get-tuple-element.27.mine), channel_id=1, source_target_pairs={{0,2},{1,3},{2,0},{3,1},{4,6},{5,7},{6,4},{7,5},{8,10},{9,11},{10,... | collective-permute-start | bytes 86024 | tf_op jit(solution)/shard_map/ppermute | solution.py:32
  4.9 4.4 %collective-permute-start.2 = (bf16[112,128]{1,0:T(8,128)(2,1)S(1)}, bf16[112,128]{1,0:T(8,128)(2,1)S(1)}, u32[]{:S(2)}, u32[]{:S(2)}) collective-permute-start(bf16[112,128]{1,0:T(8,128)(2,1)S(1)} %get-tuple-element.27.mine), channel_id=1, source_target_pairs={{0,3},{1,2},{2,1},{3,0},{4,7},{5,6},{6,5},{7,4},{8,11},{9,10},{10,... | collective-permute-start | bytes 86024 | tf_op jit(solution)/shard_map/ppermute | solution.py:32
  6.7 17.9 %collective-permute-start.7 = (bf16[1408,256]{1,0:T(8,128)(2,1)S(1)}, bf16[1408,256]{1,0:T(8,128)(2,1)S(1)}, u32[]{:S(2)}, u32[]{:S(2)}) collective-permute-start(bf16[1408,256]{1,0:T(8,128)(2,1)S(1)} %get-tuple-element.28.q2), channel_id=1, source_target_pairs={{0,2},{1,3},{2,0},{3,1},{4,6},{5,7},{6,4},{7,5},{8,10},{9,11},{10,... | collective-permute-start | bytes 2162696 | tf_op jit(solution)/shard_map/ppermute | solution.py:32
  10.1 3.0 %collective-permute-start.3 = (bf16[80,128]{1,0:T(8,128)(2,1)S(1)}, bf16[80,128]{1,0:T(8,128)(2,1)S(1)}, u32[]{:S(2)}, u32[]{:S(2)}) collective-permute-start(bf16[80,128]{1,0:T(8,128)(2,1)S(1)} %get-tuple-element.30.mine.refs_0_), channel_id=1, source_target_pairs={{0,4},{4,0},{8,12},{12,8},{16,20},{20,16},{24,28},{28,24},{1,5},{5... | collective-permute-start | bytes 61448 | tf_op jit(solution)/shard_map/ppermute | solution.py:32
  11.4 1.7 %copy-start.3 = (bf16[1,2,128,256]{3,2,1,0:T(8,128)(2,1)S(1)}, bf16[1,2,128,256]{3,2,1,0:T(8,128)(2,1)}, u32[]{:S(2)}) copy-start(bf16[1,2,128,256]{3,2,1,0:T(8,128)(2,1)} %refs_6_.1) | copy-start | bytes 393220
  11.4 1.7 %copy-start.5 = (s32[1,2,128]{2,1,0:T(2,128)S(1)}, s32[1,2,128]{2,1,0:T(2,128)}, u32[]{:S(2)}) copy-start(s32[1,2,128]{2,1,0:T(2,128)} %skel.5) | copy-start | bytes 3076
  13.2 12.0 %collective-permute-start.5 = (bf16[80,128]{1,0:T(8,128)(2,1)S(1)}, bf16[80,128]{1,0:T(8,128)(2,1)S(1)}, u32[]{:S(2)}, u32[]{:S(2)}) collective-permute-start(bf16[80,128]{1,0:T(8,128)(2,1)S(1)} %shard_map.131._.mine.refs_2_), channel_id=1, source_target_pairs={{0,8},{4,12},{8,0},{12,4},{16,24},{20,28},{24,16},{28,20},{1,9},{5... | collective-permute-start | bytes 61448 | tf_op jit(solution)/shard_map/ppermute | solution.py:32
  24.5 10.2 %collective-permute-start.8 = (bf16[1408,256]{1,0:T(8,128)(2,1)S(1)}, bf16[1408,256]{1,0:T(8,128)(2,1)S(1)}, u32[]{:S(2)}, u32[]{:S(2)}) collective-permute-start(bf16[1408,256]{1,0:T(8,128)(2,1)S(1)} %collective-permute-done.7.q2), channel_id=1, source_target_pairs={{0,1},{1,0},{2,3},{3,2},{4,5},{5,4},{6,7},{7,6},{8,9},{9,8},{10,11... | collective-permute-start | bytes 2162696 | tf_op jit(solution)/shard_map/ppermute | solution.py:32
  25.4 11.7 %collective-permute-start.6 = (bf16[80,128]{1,0:T(8,128)(2,1)S(1)}, bf16[80,128]{1,0:T(8,128)(2,1)S(1)}, u32[]{:S(2)}, u32[]{:S(2)}) collective-permute-start(bf16[80,128]{1,0:T(8,128)(2,1)S(1)} %shard_map.133.after._.refs_4_), channel_id=1, source_target_pairs={{0,16},{4,20},{8,24},{12,28},{16,0},{20,4},{24,8},{28,12},{1,17},{... | collective-permute-start | bytes 61448 | tf_op jit(solution)/shard_map/ppermute | solution.py:32
  34.8 2.3 %copy-start = (bf16[16,128,256]{2,1,0:T(8,128)(2,1)S(1)}, bf16[16,128,256]{2,1,0:T(8,128)(2,1)}, u32[]{:S(2)}) copy-start(bf16[16,128,256]{2,1,0:T(8,128)(2,1)} %refs_9_.1) | copy-start | bytes 3145732
  34.8 2.3 %copy-start.1 = (bf16[1,128,2048]{2,1,0:T(8,128)(2,1)S(1)}, bf16[1,128,2048]{2,1,0:T(8,128)(2,1)}, u32[]{:S(2)}) copy-start(bf16[1,128,2048]{2,1,0:T(8,128)(2,1)} %refs_8_.1) | copy-start | bytes 1572868
